TPU v7x, 32 devices: a whole 2x2x4 slice. The times are simulated.
32 devices in a mesh: fsdp: 32 (over z, y, x, core).
Axes of the slice: x: 2, y: 2, z: 4, core: 2. Of those that a mesh axis runs over, the one named last changes fastest.
Arguments:
- hidden_in: bfloat16 [4096, 960], P('fsdp'), may hold values from -6 to 6
- positions: int32 [4096], P('fsdp'), may hold values from 0 to 511, as said below
- norm1_gain: float32 [960], replicated, may hold values from 0.5 to 1.5
- q_weight: bfloat16 [921600], P('fsdp'), may hold values from -0.19364917 to 0.19364917
- k_weight: bfloat16 [307200], P('fsdp'), may hold values from -0.19364917 to 0.19364917
- v_weight: bfloat16 [307200], P('fsdp'), may hold values from -0.1875 to 0.1875
- o_weight: bfloat16 [921600], P('fsdp'), may hold values from -2 to 2
- norm2_gain: float32 [960], replicated, may hold values from 0.5 to 1.5
- gate_weight: bfloat16 [2457600], P('fsdp'), may hold values from -0.1875 to 0.1875
- up_weight: bfloat16 [2457600], P('fsdp'), may hold values from -0.1875 to 0.1875
- down_weight: bfloat16 [2457600], P('fsdp'), may hold values from -0.25 to 0.25
- cotangent: bfloat16 [4096, 960], P('fsdp'), may hold values from -6 to 6
Outputs:
- block_out: bfloat16 [4096, 960], P('fsdp')
- grad_in: bfloat16 [4096, 960], P('fsdp')
- grad_norm1_gain: float32 [960], replicated
- grad_q_weight: float32 [921600], P('fsdp')
- grad_k_weight: float32 [307200], P('fsdp')
- grad_v_weight: float32 [307200], P('fsdp')
- grad_o_weight: float32 [921600], P('fsdp')
- grad_norm2_gain: float32 [960], replicated
- grad_gate_weight: float32 [2457600], P('fsdp')
- grad_up_weight: float32 [2457600], P('fsdp')
- grad_down_weight: float32 [2457600], P('fsdp')
Inputs may be any that keep to these rules, and one draw needn't show every extreme that they name: positions[0] is 0, and each later token's position is 0 (a new sequence starts) or one more than the previous token's. Sequences are 256 to 512 tokens long, one of them exactly 512; the last one may be cut by the end of the pack.
All inputs are finite; a program needn't handle non-finite values.
Results may differ from a plain program's by a relative error of at most 0.015.
The roundings to bfloat16 on the way count: a program that leaves them out, or rounds other values in their place, can miss the bound.
Values may be sent and summed in bfloat16 or wider, within the bound.
No kernel may reach another device: no remote copies, remote signals or barrier semaphores. Data moves between devices by JAX's collectives and lax.ppermute only.
A program may use at most 192 MiB of HBM per device.

v0:
```python
import math

import jax
import jax.numpy as jnp
from jax import lax
from jax.sharding import PartitionSpec as P

KV_HEADS = 5
HEAD_DIM = 64
MAXLEN = 512


EPS = 1e-05
NEG_FILL = -1e30


def passed_along(block, axis, distance):
    devices = range(lax.axis_size(axis))
    route = [(i - distance, i) for i in devices if i - distance in devices]
    return lax.ppermute(block, axis, route)


def rotary_tables(positions):
    half_width = HEAD_DIM // 2
    frequency = jnp.exp(
        jnp.arange(half_width, dtype=jnp.float32) * (-2.0 * math.log(10000.0) / HEAD_DIM)
    )
    angles = positions.astype(jnp.float32)[:, None] * frequency[None, :]
    return (jnp.cos(angles), jnp.sin(angles))


def rotate(matrix, cosine, sine_table):
    row_count = matrix.shape[0]
    half_width = HEAD_DIM // 2
    shaped = matrix.reshape(row_count, -1, HEAD_DIM)
    first_half = shaped[:, :, :half_width]
    second_half = shaped[:, :, half_width:]
    cosine_rows = cosine[:, None, :]
    sine_rows = sine_table[:, None, :]
    turned = jnp.concatenate(
        [
            first_half * cosine_rows - second_half * sine_rows,
            second_half * cosine_rows + first_half * sine_rows,
        ],
        axis=2,
    )
    return turned.reshape(row_count, -1)


def norm_scale(matrix):
    return lax.rsqrt(jnp.mean(matrix * matrix, axis=1, keepdims=True) + EPS)


def norm_backward(matrix, scale_rows, gain, grad_normed):
    unit_rows = matrix * scale_rows
    weighted = grad_normed * gain[None, :]
    grad_gain = jnp.sum(grad_normed * unit_rows, axis=0)
    grad_rows = scale_rows * (
        weighted - unit_rows * jnp.mean(weighted * unit_rows, axis=1, keepdims=True)
    )
    return (grad_rows, grad_gain)


def outer_sum(left_side, right_side):
    return lax.dot_general(
        left_side, right_side, (((0,), (0,)), ((), ())), preferred_element_type=jnp.float32
    )


def back_product(left_side, weight):
    return lax.dot_general(
        left_side, weight, (((1,), (1,)), ((), ())), preferred_element_type=jnp.float32
    )


def forward_product(left_side, weight):
    return jnp.dot(left_side, weight, preferred_element_type=jnp.float32)


def shape_weights(flat_parts, model_width):
    return (
        flat_parts[0].reshape(model_width, -1),
        flat_parts[1].reshape(model_width, -1),
        flat_parts[2].reshape(model_width, -1),
        flat_parts[3].reshape(-1, model_width),
        flat_parts[4].reshape(model_width, -1),
        flat_parts[5].reshape(model_width, -1),
        flat_parts[6].reshape(-1, model_width),
    )


def score_block(query_block, key_block, position_block, prefix):
    row_count = query_block.shape[0]
    key_count = key_block.shape[0]
    grouped = query_block.reshape(row_count, KV_HEADS, -1, HEAD_DIM)
    key_heads = key_block.reshape(key_count, KV_HEADS, HEAD_DIM)
    scores = jnp.einsum(
        "qkgd,skd->kgqs", grouped, key_heads, preferred_element_type=jnp.float32
    ) * HEAD_DIM ** (-0.5)
    key_offset = jnp.arange(key_count, dtype=jnp.int32) - prefix
    row_index = jnp.arange(row_count, dtype=jnp.int32)
    allowed = (key_offset[None, :] <= row_index[:, None]) & (
        key_offset[None, :] >= row_index[:, None] - position_block[:, None]
    )
    return jnp.where(allowed[None, None], scores, NEG_FILL)


def attend(query_block, key_block, value_block, position_block, prefix):
    row_count = query_block.shape[0]
    key_count = key_block.shape[0]
    scores = score_block(query_block, key_block, position_block, prefix)
    row_max = jnp.max(scores, axis=3, keepdims=True)
    log_total = row_max + jnp.log(jnp.sum(jnp.exp(scores - row_max), axis=3, keepdims=True))
    prob_low = jnp.exp(scores - log_total).astype(jnp.bfloat16)
    value_heads = value_block.reshape(key_count, KV_HEADS, HEAD_DIM)
    mixed_out = jnp.einsum(
        "kgqs,skd->qkgd", prob_low, value_heads, preferred_element_type=jnp.float32
    )
    return (mixed_out.reshape(row_count, -1).astype(jnp.bfloat16), log_total)


def attend_back(
    query_block,
    key_block,
    value_block,
    position_block,
    prefix,
    log_total,
    attended_block,
    grad_block,
):
    row_count = query_block.shape[0]
    key_count = key_block.shape[0]
    scores = score_block(query_block, key_block, position_block, prefix)
    prob_full = jnp.exp(scores - log_total)
    prob_low = prob_full.astype(jnp.bfloat16)
    grouped = query_block.reshape(row_count, KV_HEADS, -1, HEAD_DIM)
    grad_grouped = grad_block.reshape(row_count, KV_HEADS, -1, HEAD_DIM)
    out_grouped = attended_block.reshape(row_count, KV_HEADS, -1, HEAD_DIM)
    key_heads = key_block.reshape(key_count, KV_HEADS, HEAD_DIM)
    value_heads = value_block.reshape(key_count, KV_HEADS, HEAD_DIM)
    grad_prob = jnp.einsum(
        "qkgd,skd->kgqs", grad_grouped, value_heads, preferred_element_type=jnp.float32
    )
    delta_sum = jnp.einsum(
        "qkgd,qkgd->kgq", grad_grouped, out_grouped, preferred_element_type=jnp.float32
    )[..., None]
    grad_score = (prob_full * (grad_prob - delta_sum) * HEAD_DIM ** (-0.5)).astype(jnp.bfloat16)
    grad_query = jnp.einsum(
        "kgqs,skd->qkgd", grad_score, key_heads, preferred_element_type=jnp.float32
    ).reshape(row_count, -1)
    grad_key = jnp.einsum(
        "kgqs,qkgd->skd", grad_score, grouped, preferred_element_type=jnp.float32
    ).reshape(key_count, -1)
    grad_value = jnp.einsum(
        "kgqs,qkgd->skd", prob_low, grad_grouped, preferred_element_type=jnp.float32
    ).reshape(key_count, -1)
    return (grad_query, grad_key, grad_value)


def local(
    hidden_in,
    positions,
    norm1_gain,
    q_weight,
    k_weight,
    v_weight,
    o_weight,
    norm2_gain,
    gate_weight,
    up_weight,
    down_weight,
    cotangent,
):
    tok_rows = hidden_in.shape[0]
    model_width = hidden_in.shape[1]
    device_count = lax.axis_size("fsdp")
    window_span = (MAXLEN + tok_rows - 2) // tok_rows
    prefix = window_span * tok_rows
    gathered = (
        lax.all_gather(q_weight, "fsdp", axis=0, tiled=True),
        lax.all_gather(k_weight, "fsdp", axis=0, tiled=True),
        lax.all_gather(v_weight, "fsdp", axis=0, tiled=True),
        lax.all_gather(o_weight, "fsdp", axis=0, tiled=True),
        lax.all_gather(gate_weight, "fsdp", axis=0, tiled=True),
        lax.all_gather(up_weight, "fsdp", axis=0, tiled=True),
        lax.all_gather(down_weight, "fsdp", axis=0, tiled=True),
    )
    weight_query, weight_key, weight_value, weight_out, weight_gate, weight_up, weight_down = (
        shape_weights(gathered, model_width)
    )
    input_rows = hidden_in.astype(jnp.float32)
    scale_one = norm_scale(input_rows)
    normed_one = (input_rows * scale_one * norm1_gain[None, :]).astype(jnp.bfloat16)
    cosine, sine_table = rotary_tables(positions)
    query_low = rotate(forward_product(normed_one, weight_query), cosine, sine_table).astype(
        jnp.bfloat16
    )
    key_low = rotate(forward_product(normed_one, weight_key), cosine, sine_table).astype(
        jnp.bfloat16
    )
    value_low = forward_product(normed_one, weight_value).astype(jnp.bfloat16)
    key_pieces = [key_low]
    value_pieces = [value_low]
    for distance in range(1, window_span + 1):
        arrived = passed_along((key_low, value_low), "fsdp", distance)
        key_pieces.insert(0, arrived[0])
        value_pieces.insert(0, arrived[1])
    key_window = jnp.concatenate(key_pieces, axis=0)
    value_window = jnp.concatenate(value_pieces, axis=0)
    attended_low, log_total = attend(query_low, key_window, value_window, positions, prefix)
    mid_rows = input_rows + forward_product(attended_low, weight_out)
    scale_two = norm_scale(mid_rows)
    normed_two = (mid_rows * scale_two * norm2_gain[None, :]).astype(jnp.bfloat16)
    gate_pre = forward_product(normed_two, weight_gate)
    up_pre = forward_product(normed_two, weight_up)
    sigmoid_gate = jax.nn.sigmoid(gate_pre)
    silu_gate = gate_pre * sigmoid_gate
    hidden_low = (silu_gate * up_pre).astype(jnp.bfloat16)
    block_out = (mid_rows + forward_product(hidden_low, weight_down)).astype(jnp.bfloat16)
    grad_down = outer_sum(hidden_low, cotangent)
    grad_hidden = back_product(cotangent, weight_down)
    grad_gate_low = (
        grad_hidden * up_pre * sigmoid_gate * (1.0 + gate_pre * (1.0 - sigmoid_gate))
    ).astype(jnp.bfloat16)
    grad_up_low = (grad_hidden * silu_gate).astype(jnp.bfloat16)
    grad_gate = outer_sum(normed_two, grad_gate_low)
    grad_up = outer_sum(normed_two, grad_up_low)
    grad_normed_two = back_product(grad_gate_low, weight_gate) + back_product(
        grad_up_low, weight_up
    )
    grad_mid_norm, grad_gain_two = norm_backward(mid_rows, scale_two, norm2_gain, grad_normed_two)
    grad_mid = cotangent.astype(jnp.float32) + grad_mid_norm
    grad_mid_low = grad_mid.astype(jnp.bfloat16)
    grad_out = outer_sum(attended_low, grad_mid_low)
    grad_attended_low = back_product(grad_mid_low, weight_out).astype(jnp.bfloat16)
    grad_query, grad_key_window, grad_value_window = attend_back(
        query_low,
        key_window,
        value_window,
        positions,
        prefix,
        log_total,
        attended_low,
        grad_attended_low,
    )
    own_key = grad_key_window[prefix:]
    own_value = grad_value_window[prefix:]
    for distance in range(1, window_span + 1):
        start_row = prefix - distance * tok_rows
        returned = passed_along(
            (
                grad_key_window[start_row : start_row + tok_rows],
                grad_value_window[start_row : start_row + tok_rows],
            ),
            "fsdp",
            -distance,
        )
        own_key = own_key + returned[0]
        own_value = own_value + returned[1]
    grad_query_in = rotate(grad_query, cosine, -sine_table).astype(jnp.bfloat16)
    grad_key_in = rotate(own_key, cosine, -sine_table).astype(jnp.bfloat16)
    grad_value_in = own_value.astype(jnp.bfloat16)
    grad_query_weight = outer_sum(normed_one, grad_query_in)
    grad_key_weight = outer_sum(normed_one, grad_key_in)
    grad_value_weight = outer_sum(normed_one, grad_value_in)
    grad_normed_one = (
        back_product(grad_query_in, weight_query)
        + back_product(grad_key_in, weight_key)
        + back_product(grad_value_in, weight_value)
    )
    grad_in_norm, grad_gain_one = norm_backward(input_rows, scale_one, norm1_gain, grad_normed_one)
    grad_in = (grad_mid + grad_in_norm).astype(jnp.bfloat16)
    shards = (
        lax.psum_scatter(
            grad_query_weight.reshape(device_count, -1), "fsdp", scatter_dimension=0, tiled=True
        ),
        lax.psum_scatter(
            grad_key_weight.reshape(device_count, -1), "fsdp", scatter_dimension=0, tiled=True
        ),
        lax.psum_scatter(
            grad_value_weight.reshape(device_count, -1), "fsdp", scatter_dimension=0, tiled=True
        ),
        lax.psum_scatter(
            grad_out.reshape(device_count, -1), "fsdp", scatter_dimension=0, tiled=True
        ),
        lax.psum_scatter(
            grad_gate.reshape(device_count, -1), "fsdp", scatter_dimension=0, tiled=True
        ),
        lax.psum_scatter(
            grad_up.reshape(device_count, -1), "fsdp", scatter_dimension=0, tiled=True
        ),
        lax.psum_scatter(
            grad_down.reshape(device_count, -1), "fsdp", scatter_dimension=0, tiled=True
        ),
    )
    gain_totals = lax.psum((grad_gain_one, grad_gain_two), "fsdp")
    return (
        block_out,
        grad_in,
        gain_totals[0],
        shards[0].reshape(-1),
        shards[1].reshape(-1),
        shards[2].reshape(-1),
        shards[3].reshape(-1),
        gain_totals[1],
        shards[4].reshape(-1),
        shards[5].reshape(-1),
        shards[6].reshape(-1),
    )


def solution(mesh):
    placed = (
        P("fsdp", None),
        P("fsdp"),
        P(),
        P("fsdp"),
        P("fsdp"),
        P("fsdp"),
        P("fsdp"),
        P(),
        P("fsdp"),
        P("fsdp"),
        P("fsdp"),
        P("fsdp", None),
    )
    return jax.shard_map(
        local,
        mesh=mesh,
        in_specs=placed,
        out_specs=(
            P("fsdp", None),
            P("fsdp", None),
            P(),
            P("fsdp"),
            P("fsdp"),
            P("fsdp"),
            P("fsdp"),
            P(),
            P("fsdp"),
            P("fsdp"),
            P("fsdp"),
        ),
        check_vma=False,
    )
```

profile of v0, /device:TPU:0, one launch (start us, length us, event | category | flops | bytes accessed | tf_op | source)
XLA Modules:
  0.0 1062.8 jit_solution(17326669944928612935)
XLA Ops:
  13.2 47.7 %all-gather = bf16[32,1,9600]{2,1,0:T(2,128)(2,1)S(1)} all-gather(bf16[1,1,9600]{2,1,0:T(2,128)(2,1)S(1)} %reshape.331), channel_id=1, replica_groups=mesh['fsdp'=32] {'fsdp'}, dimensions={0}, use_global_device_ids=true | all-gather | bytes 633600 | tf_op jit(solution)/shard_map/all_gather | solution.py:183
  60.9 3.7 reduce.1
  72.5 40.9 %all-gather.1 = bf16[32,1,9600]{2,1,0:T(2,128)(2,1)S(1)} all-gather(bf16[1,1,9600]{2,1,0:T(2,128)(2,1)S(1)} %reshape.333), channel_id=1, replica_groups=mesh['fsdp'=32] {'fsdp'}, dimensions={0}, use_global_device_ids=true | all-gather | bytes 633600 | tf_op jit(solution)/shard_map/all_gather | solution.py:182
  113.5 3.7 reduce.2
  120.4 3.7 collective-permute-start.5
  125.6 2.8 collective-permute-start.7
  130.7 40.8 %reduce.3 = bf16[32,28800]{1,0:T(8,128)(2,1)} reduce(bf16[32,1,28800]{2,1,0:T(2,128)(2,1)} %all-gather.16.cloned.1.call-done, bf16[]{:T(256)} %constant.45), dimensions={1}, to_apply=%all-gather.2.reduce_sub_computation | reduce | bytes 3686402 | tf_op jit(solution)/shard_map/all_gather | solution.py:181
  171.5 3.1 reshape.310
  177.2 40.8 %reduce.4 = bf16[32,28800]{1,0:T(8,128)(2,1)} reduce(bf16[32,1,28800]{2,1,0:T(2,128)(2,1)} %all-gather.18.cloned.1.call-done, bf16[]{:T(256)} %constant.45), dimensions={1}, to_apply=%all-gather.3.reduce_sub_computation | reduce | bytes 3686402 | tf_op jit(solution)/shard_map/all_gather | solution.py:184
  218.0 4.3 reshape.311
  229.9 10.1 reshape.312
  240.0 36.6 %all-gather.12.cloned.1.call-done = bf16[2457600]{0:T(1024)(128)(2,1)} async-done(((bf16[76800]{0:T(1024)(128)(2,1)}), bf16[2457600]{0:T(1024)(128)(2,1)}) %all-gather.12.cloned.1.call-update) | async-done | bytes 4915216 | tf_op jit(solution)/shard_map/all_gather | solution.py:186
  276.7 10.0 reshape.313
  286.7 4.5 fusion.53
  293.1 48.9 %all-gather.14.cloned.1.call-done = bf16[2457600]{0:T(1024)(128)(2,1)} async-done(((bf16[76800]{0:T(1024)(128)(2,1)}), bf16[2457600]{0:T(1024)(128)(2,1)}) %all-gather.14.cloned.1.call-update) | async-done | bytes 4915216 | tf_op jit(solution)/shard_map/all_gather | solution.py:187
  342.1 9.7 reshape.314
  351.8 5.5 multiply_convert_fusion
  358.9 4.2 multiply_reduce_fusion
  371.4 5.1 fusion.57
  376.6 5.2 fusion.58
  390.2 5.4 fusion.59
  399.1 5.1 reshape.317
  404.2 5.1 reshape.323
  409.2 10.3 reshape.325
  419.6 10.3 reshape.327
  429.9 10.6 %reshape.329 = f32[32,76800]{1,0:T(8,128)} reshape(f32[2560,960]{1,0:T(8,128)} %fusion.59) | data formatting | bytes 19660800 | tf_op jit(solution)/shard_map/reshape | solution.py:294
  447.5 3.2 reshape.319
  455.2 3.1 reshape.321
  458.3 5.2 fusion.6
  466.0 52.9 %all-reduce.7 = (f32[960]{0:T(1024)}, f32[960]{0:T(1024)}) all-reduce(f32[960]{0:T(1024)S(1)} %get-tuple-element.13, f32[960]{0:T(1024)S(1)} %get-tuple-element.11), channel_id=1, replica_groups=mesh['fsdp'=32] {'fsdp'}, use_global_device_ids=true, to_apply=%region_7.8 | all-reduce | flops 1920 | bytes 15360 | tf_op jit(solution)/shard_map/psum | solution.py:297
  519.9 524.9 %all-reduce.11.cloned.1.call-done = (f32[32,28800]{1,0:T(8,128)}, f32[32,9600]{1,0:T(8,128)}, f32[32,9600]{1,0:T(8,128)}, f32[32,28800]{1,0:T(8,128)}, f32[32,76...) async-done(((f32[32,28800]{1,0:T(8,128)}, f32[32,9600]{1,0:T(8,128)}, f32[32,9600]{1,0:T(8,128)}, f32[32,28800]{1,0:T(8,128)}, f32[32,76800]{1,0:T(8,128)}, ...) | async-done | bytes 39321616
  1052.0 3.7 constant_dynamic-slice_fusion
  (180 shorter events, 76.1 us)
Async XLA Ops:
  7.2 58.2 %copy-start.1 = (bf16[128,960]{0,1:T(8,128)(2,1)S(1)}, bf16[128,960]{0,1:T(8,128)(2,1)}, u32[]{:S(2)}) copy-start(bf16[128,960]{0,1:T(8,128)(2,1)} %param.12) | copy-start | bytes 737284
  7.2 58.3 %copy-start.20 = (f32[960]{0:T(1024)S(1)}, f32[960]{0:T(1024)}, u32[]{:S(2)}) copy-start(f32[960]{0:T(1024)} %param.14) | copy-start | bytes 11524
  7.2 65.3 %copy-start.22 = (bf16[9600]{0:T(1024)(128)(2,1)S(1)}, bf16[9600]{0:T(1024)(128)(2,1)}, u32[]{:S(2)}) copy-start(bf16[9600]{0:T(1024)(128)(2,1)} %param.16) | copy-start | bytes 57604
  7.2 123.5 %all-gather.16.cloned.1.call-start = ((), (), s32[]{:S(2)}) async-start(), calls=%async_computation.3 | async-start | bytes 3801600 | tf_op jit(solution)/shard_map/all_gather | solution.py:181
  8.9 168.3 %all-gather.18.cloned.1.call-start = ((), (), s32[]{:S(2)}) async-start(), calls=%async_computation.4 | async-start | bytes 3801600 | tf_op jit(solution)/shard_map/all_gather | solution.py:184
  10.5 219.4 %all-gather.10.cloned.1.call-start = ((), (), s32[]{:S(2)}) async-start(), calls=%async_computation | async-start | bytes 5068800 | tf_op jit(solution)/shard_map/all_gather | solution.py:185
  11.2 265.5 %all-gather.12.cloned.1.call-start = ((), (), s32[]{:S(2)}) async-start(), calls=%async_computation.1 | async-start | bytes 5068800 | tf_op jit(solution)/shard_map/all_gather | solution.py:186
  11.8 330.3 %all-gather.14.cloned.1.call-start = ((), (), s32[]{:S(2)}) async-start(), calls=%async_computation.2 | async-start | bytes 5068800 | tf_op jit(solution)/shard_map/all_gather | solution.py:187
  12.4 1032.4 %all-reduce.11.cloned.1.call-start = ((), (), s32[]{:S(2)}) async-start(), calls=%async_computation.5 | async-start | bytes 78643200
  60.9 57.4 %copy-start.27 = (s32[128]{0:T(128)S(1)}, s32[128]{0:T(128)}, u32[]{:S(2)}) copy-start(s32[128]{0:T(128)} %param.13) | copy-start | bytes 1540
  66.1 54.3 %collective-permute-start = (bf16[128,320]{0,1:T(8,128)(2,1)S(1)}, bf16[128,320]{0,1:T(8,128)(2,1)S(1)}, u32[]{:S(2)}, u32[]{:S(2)}) collective-permute-start(bf16[128,320]{0,1:T(8,128)(2,1)S(1)} %convolution_convert_fusion.2), channel_id=1, source_target_pairs={{0,4},{1,5},{2,6},{3,7},{4,8},{5,9},{6,10},{7,11},{8,12},{9,13},{1... | collective-permute-start | bytes 245768 | tf_op jit(solution)/shard_map/ppermute | solution.py:20
  67.4 56.7 %collective-permute-start.1 = (bf16[128,320]{0,1:T(8,128)(2,1)S(1)}, bf16[128,320]{0,1:T(8,128)(2,1)S(1)}, u32[]{:S(2)}, u32[]{:S(2)}) collective-permute-start(bf16[128,320]{0,1:T(8,128)(2,1)S(1)} %convolution_convert_fusion.2), channel_id=1, source_target_pairs={{0,3},{1,4},{2,5},{3,6},{4,7},{5,8},{6,9},{7,10},{8,11},{9,12},{10... | collective-permute-start | bytes 245768 | tf_op jit(solution)/shard_map/ppermute | solution.py:20
  68.7 56.8 %collective-permute-start.2 = (bf16[128,320]{0,1:T(8,128)(2,1)S(1)}, bf16[128,320]{0,1:T(8,128)(2,1)S(1)}, u32[]{:S(2)}, u32[]{:S(2)}) collective-permute-start(bf16[128,320]{0,1:T(8,128)(2,1)S(1)} %convolution_convert_fusion.2), channel_id=1, source_target_pairs={{0,2},{1,3},{2,4},{3,5},{4,6},{5,7},{6,8},{7,9},{8,10},{9,11},{10,... | collective-permute-start | bytes 245768 | tf_op jit(solution)/shard_map/ppermute | solution.py:20
  71.2 57.2 %collective-permute-start.3 = (bf16[128,320]{0,1:T(8,128)(2,1)S(1)}, bf16[128,320]{0,1:T(8,128)(2,1)S(1)}, u32[]{:S(2)}, u32[]{:S(2)}) collective-permute-start(bf16[128,320]{0,1:T(8,128)(2,1)S(1)} %convolution_convert_fusion.2), channel_id=1, source_target_pairs={{0,1},{1,2},{2,3},{3,4},{4,5},{5,6},{6,7},{7,8},{8,9},{9,10},{10,1... | collective-permute-start | bytes 245768 | tf_op jit(solution)/shard_map/ppermute | solution.py:20
  117.9 12.7 %copy-start.5 = (bf16[960,320]{1,0:T(8,128)(2,1)}, bf16[960,320]{1,0:T(8,128)(2,1)S(1)}, u32[]{:S(2)}) copy-start(bf16[960,320]{1,0:T(8,128)(2,1)S(1)} %reshape.308) | copy-start | bytes 1843204
  118.9 9.6 collective-permute-start.4
  120.4 8.1 collective-permute-start.5
  124.2 6.4 collective-permute-start.6
  125.6 5.0 collective-permute-start.7
  128.5 98.3 %copy-start.23 = (bf16[640,320]{0,1:T(8,128)(2,1)}, bf16[640,320]{0,1:T(8,128)(2,1)S(1)}, u32[]{:S(2)}) copy-start(bf16[640,320]{0,1:T(8,128)(2,1)S(1)} %constant_dynamic-update-slice_fusion) | copy-start | bytes 1228804
  130.7 94.1 %copy-start.17 = (bf16[640,320]{0,1:T(8,128)(2,1)}, bf16[640,320]{0,1:T(8,128)(2,1)S(1)}, u32[]{:S(2)}) copy-start(bf16[640,320]{0,1:T(8,128)(2,1)S(1)} %constant_dynamic-update-slice_fusion.5) | copy-start | bytes 1228804
  229.9 61.3 %copy-start.7 = (bf16[128,960]{0,1:T(8,128)(2,1)}, bf16[128,960]{0,1:T(8,128)(2,1)S(1)}, u32[]{:S(2)}) copy-start(bf16[128,960]{0,1:T(8,128)(2,1)S(1)} %multiply_convert_fusion.3) | copy-start | bytes 737284
  342.1 15.3 %slice-start = ((s8[4915200]{0:T(1024)(128)(4,1)}), s8[720896]{0:T(1024)(128)(4,1)S(1)}, s32[]{:S(2)}) async-start(s8[4915200]{0:T(1024)(128)(4,1)} %bitcast.139), calls=%async_computation.6 | async-start | bytes 1441792
  357.4 32.9 %copy-start.9 = (bf16[128,2560]{1,0:T(8,128)(2,1)}, bf16[128,2560]{1,0:T(8,128)(2,1)S(1)}, u32[]{:S(2)}) copy-start(bf16[128,2560]{1,0:T(8,128)(2,1)S(1)} %get-tuple-element.26) | copy-start | bytes 1966084
  382.6 57.9 %collective-permute-start.11 = (f32[128,320]{0,1:T(8,128)}, f32[128,320]{0,1:T(8,128)}, u32[]{:S(2)}, u32[]{:S(2)}) collective-permute-start(f32[128,320]{0,1:T(8,128)} %bitcast.38), channel_id=1, source_target_pairs={{4,0},{5,1},{6,2},{7,3},{8,4},{9,5},{10,6},{11,7},{12,8},{13,9},{1... | collective-permute-start | bytes 491528 | tf_op jit(solution)/shard_map/ppermute | solution.py:20
  383.9 57.9 %collective-permute-start.10 = (f32[128,320]{0,1:T(8,128)}, f32[128,320]{0,1:T(8,128)}, u32[]{:S(2)}, u32[]{:S(2)}) collective-permute-start(f32[128,320]{0,1:T(8,128)} %bitcast.37), channel_id=1, source_target_pairs={{3,0},{4,1},{5,2},{6,3},{7,4},{8,5},{9,6},{10,7},{11,8},{12,9},{13... | collective-permute-start | bytes 491528 | tf_op jit(solution)/shard_map/ppermute | solution.py:20
  385.2 57.9 %collective-permute-start.9 = (f32[128,320]{0,1:T(8,128)}, f32[128,320]{0,1:T(8,128)}, u32[]{:S(2)}, u32[]{:S(2)}) collective-permute-start(f32[128,320]{0,1:T(8,128)} %bitcast.36), channel_id=1, source_target_pairs={{2,0},{3,1},{4,2},{5,3},{6,4},{7,5},{8,6},{9,7},{10,8},{11,9},{12,... | collective-permute-start | bytes 491528 | tf_op jit(solution)/shard_map/ppermute | solution.py:20
  386.5 58.2 %collective-permute-start.8 = (f32[128,320]{0,1:T(8,128)}, f32[128,320]{0,1:T(8,128)}, u32[]{:S(2)}, u32[]{:S(2)}) collective-permute-start(f32[128,320]{0,1:T(8,128)} %bitcast.35), channel_id=1, source_target_pairs={{1,0},{2,1},{3,2},{4,3},{5,4},{6,5},{7,6},{8,7},{9,8},{10,9},{11,1... | collective-permute-start | bytes 491528 | tf_op jit(solution)/shard_map/ppermute | solution.py:20
  388.7 61.9 %collective-permute-start.15 = (f32[128,320]{0,1:T(8,128)}, f32[128,320]{0,1:T(8,128)}, u32[]{:S(2)}, u32[]{:S(2)}) collective-permute-start(f32[128,320]{0,1:T(8,128)} %bitcast.49), channel_id=1, source_target_pairs={{4,0},{5,1},{6,2},{7,3},{8,4},{9,5},{10,6},{11,7},{12,8},{13,9},{1... | collective-permute-start | bytes 491528 | tf_op jit(solution)/shard_map/ppermute | solution.py:20
  440.5 10.1 collective-permute-start.14
  441.8 10.5 collective-permute-start.13
  443.1 9.2 collective-permute-start.12
  (22 other events, 86.1 us)
Sparse Core Ops, SparseCore 0:
  11.4 66.7 all-gather.15
  81.6 63.7 all-gather.17
  148.3 62.9 all-gather.9
  214.1 62.5 all-gather.11
  279.5 62.5 all-gather.13
  458.4 586.2 all-reduce.10
where the time goes:
time: 1070 us; the launch traced here: 1060 us
  waiting for transfers between devices  616 us (58%)
  blocking collectives  142 us (13%)
  local copies, waits for them, and re-layouts  108 us (10%)
  other arithmetic  94.6 us (9%)
  matrix products  61.1 us (6%)
  starting transfers between devices  26.5 us (2%)
  between operations  15.4 us (1%)
    unnamed x7, waiting for transfers between devices  527 us
    psum x1, blocking collectives, local(): gain_totals = lax.psum((grad_gain_one, grad_gain_two), 'fsdp')  52.9 us
    all_gather x1, waiting for transfers between devices, local(): lax.all_gather(down_weight, 'fsdp', axis=0, tiled=True)  48.9 us
    all_gather x1, blocking collectives, local(): lax.all_gather(v_weight, 'fsdp', axis=0, tiled=True)  47.7 us
    all_gather x1, blocking collectives, local(): lax.all_gather(k_weight, 'fsdp', axis=0, tiled=True)  40.9 us
    all_gather x1, other arithmetic, local(): lax.all_gather(o_weight, 'fsdp', axis=0, tiled=True)  40.8 us
    all_gather x1, other arithmetic, local(): lax.all_gather(q_weight, 'fsdp', axis=0, tiled=True)  40.8 us
    all_gather x1, waiting for transfers between devices, local(): lax.all_gather(up_weight, 'fsdp', axis=0, tiled=True)  36.6 us
  transfers between devices with their start and end apart: 22, of which 5 were waited for; matrix products, arithmetic and copies ran while one was open for 19% of the time, Pallas kernels for 0%

commit v1 on v0

--- a/solution.py
+++ b/solution.py
@@ -12,12 +12,34 @@
 
 EPS = 1e-05
 NEG_FILL = -1e30
-
-
-def passed_along(block, axis, distance):
-    devices = range(lax.axis_size(axis))
+AXIS = "fsdp"
+TEAM_BITS = (1, 2)
+TEAM = 1 << len(TEAM_BITS)
+LOW_BITS = 3
+ROW_TILE = 16
+LINK = jnp.bfloat16
+
+
+def swap(block, mask):
+    size = lax.axis_size(AXIS)
+    return lax.ppermute(block, AXIS, [(i, i ^ mask) for i in range(size)])
+
+
+def passed_along(block, distance):
+    devices = range(lax.axis_size(AXIS))
     route = [(i - distance, i) for i in devices if i - distance in devices]
-    return lax.ppermute(block, axis, route)
+    return lax.ppermute(block, AXIS, route)
+
+
+def pick(stack, index, axis=0):
+    return lax.dynamic_index_in_dim(stack, index, axis, keepdims=False)
+
+
+def team_masks():
+    masks = []
+    for member in range(TEAM):
+        masks.append(sum(((member >> j) & 1) << bit for j, bit in enumerate(TEAM_BITS)))
+    return masks
 
 
 def rotary_tables(positions):
@@ -75,18 +97,6 @@
 
 def forward_product(left_side, weight):
     return jnp.dot(left_side, weight, preferred_element_type=jnp.float32)
-
-
-def shape_weights(flat_parts, model_width):
-    return (
-        flat_parts[0].reshape(model_width, -1),
-        flat_parts[1].reshape(model_width, -1),
-        flat_parts[2].reshape(model_width, -1),
-        flat_parts[3].reshape(-1, model_width),
-        flat_parts[4].reshape(model_width, -1),
-        flat_parts[5].reshape(model_width, -1),
-        flat_parts[6].reshape(-1, model_width),
-    )
 
 
 def score_block(query_block, key_block, position_block, prefix):
@@ -158,6 +168,130 @@
     return (grad_query, grad_key, grad_value)
 
 
+class RowPlan:
+    def __init__(self, row_total):
+        size = lax.axis_size(AXIS)
+        self.unit = size // math.gcd(size, row_total)
+        self.rows = self.unit * row_total // size
+        self.pitch = -(-self.rows // ROW_TILE) * ROW_TILE
+        self.row_total = row_total
+        unit_bits = self.unit.bit_length() - 1
+        self.low = list(range(unit_bits))
+        free = [b for b in range(unit_bits, size.bit_length() - 1)]
+        self.outer = [b for b in free if b >= LOW_BITS]
+        self.team = [b for b in free if b in TEAM_BITS]
+        self.last = [b for b in free if b < LOW_BITS and b not in TEAM_BITS]
+        team_set = [0]
+        for bit in self.team:
+            team_set += [m | (1 << bit) for m in team_set]
+        self.team_set = team_set
+        offsets = [0]
+        for bit in self.outer:
+            offsets += [m ^ (1 << bit) for m in offsets]
+        offsets = [m ^ t for t in team_set for m in offsets]
+        for bit in self.last:
+            offsets += [m ^ (1 << bit) for m in offsets]
+        self.offsets = [m // self.unit for m in offsets]
+
+    def selector(self, place):
+        slots = jnp.arange(len(self.offsets) * self.pitch, dtype=jnp.int32)
+        block = slots // self.pitch
+        within = slots % self.pitch
+        start = jnp.repeat(jnp.array(self.offsets, jnp.int32), self.pitch)
+        row = ((place // self.unit) ^ start) * self.rows + within
+        row = jnp.where(within < self.rows, row, -1)
+        del block
+        return (jnp.arange(self.row_total, dtype=jnp.int32)[:, None] == row[None, :]).astype(
+            jnp.bfloat16
+        )
+
+    def local(self, flats, place):
+        parts = []
+        for flat in flats:
+            for bit in self.low:
+                other = swap(flat, 1 << bit)
+                high = (place >> bit) & 1
+                flat = jnp.concatenate(
+                    [jnp.where(high == 1, other, flat), jnp.where(high == 1, flat, other)]
+                )
+            parts.append(flat.reshape(self.rows, -1))
+        block = jnp.concatenate(parts, axis=1) if len(parts) > 1 else parts[0]
+        return jnp.pad(block, ((0, self.pitch - self.rows), (0, 0)))
+
+    def gather(self, flats, place):
+        stack = self.local(flats, place)
+        for bit in self.outer:
+            stack = jnp.concatenate([stack, swap(stack, 1 << bit)])
+        stack = jnp.concatenate([stack] + [swap(stack, m) for m in self.team_set[1:]])
+        for bit in self.last:
+            stack = jnp.concatenate([stack, swap(stack, 1 << bit)])
+        return stack
+
+    def scatter(self, stack, widths, place):
+        for bit in reversed(self.last):
+            half = stack.shape[0] // 2
+            stack = stack[:half] + swap(stack[half:].astype(LINK), 1 << bit).astype(jnp.float32)
+        members = stack.reshape(len(self.team_set), -1, stack.shape[1])
+        total = members[0]
+        for position, mask in enumerate(self.team_set):
+            if mask:
+                total = total + swap(members[position].astype(LINK), mask).astype(jnp.float32)
+        stack = total
+        for bit in reversed(self.outer):
+            half = stack.shape[0] // 2
+            stack = stack[:half] + swap(stack[half:].astype(LINK), 1 << bit).astype(jnp.float32)
+        stack = stack[: self.rows]
+        flats = []
+        start = 0
+        for width in widths:
+            flat = stack[:, start : start + width].reshape(-1)
+            start += width
+            for bit in reversed(self.low):
+                high = (place >> bit) & 1
+                halves = flat.reshape(2, -1)
+                flat = pick(halves, high) + swap(
+                    pick(halves, 1 - high).astype(LINK), 1 << bit
+                ).astype(jnp.float32)
+            flats.append(flat)
+        return flats
+
+
+def team_gather(block):
+    return jnp.concatenate([block] + [swap(block, mask) for mask in team_masks()[1:]])
+
+
+def team_scatter(stack, tok_rows):
+    total = stack[:tok_rows]
+    for member, mask in enumerate(team_masks()):
+        if mask:
+            part = stack[member * tok_rows : (member + 1) * tok_rows]
+            total = total + swap(part.astype(LINK), mask).astype(jnp.float32)
+    return total
+
+
+def outer_gather(stack):
+    size = lax.axis_size(AXIS)
+    stack = stack[None]
+    for bit in range(LOW_BITS, size.bit_length() - 1):
+        stack = jnp.concatenate([stack, swap(stack, 1 << bit)])
+    return jnp.stack([stack, swap(stack, 1)])
+
+
+def outer_scatter(stack, place):
+    size = lax.axis_size(AXIS)
+    core = place & 1
+    total = pick(stack, core, 1) + swap(pick(stack, 1 - core, 1).astype(LINK), 1).astype(
+        jnp.float32
+    )
+    for bit in reversed(range(LOW_BITS, size.bit_length() - 1)):
+        high = (place >> bit) & 1
+        halves = total.reshape((2, -1) + total.shape[1:])
+        total = pick(halves, high) + swap(pick(halves, 1 - high).astype(LINK), 1 << bit).astype(
+            jnp.float32
+        )
+    return total[0]
+
+
 def local(
     hidden_in,
     positions,
@@ -174,66 +308,133 @@
 ):
     tok_rows = hidden_in.shape[0]
     model_width = hidden_in.shape[1]
-    device_count = lax.axis_size("fsdp")
+    device_count = lax.axis_size(AXIS)
+    place = lax.axis_index(AXIS)
+    member = (place >> TEAM_BITS[0]) & (TEAM - 1)
+    outer_index = place >> LOW_BITS
+    outer_count = device_count >> LOW_BITS
     window_span = (MAXLEN + tok_rows - 2) // tok_rows
     prefix = window_span * tok_rows
-    gathered = (
-        lax.all_gather(q_weight, "fsdp", axis=0, tiled=True),
-        lax.all_gather(k_weight, "fsdp", axis=0, tiled=True),
-        lax.all_gather(v_weight, "fsdp", axis=0, tiled=True),
-        lax.all_gather(o_weight, "fsdp", axis=0, tiled=True),
-        lax.all_gather(gate_weight, "fsdp", axis=0, tiled=True),
-        lax.all_gather(up_weight, "fsdp", axis=0, tiled=True),
-        lax.all_gather(down_weight, "fsdp", axis=0, tiled=True),
-    )
-    weight_query, weight_key, weight_value, weight_out, weight_gate, weight_up, weight_down = (
-        shape_weights(gathered, model_width)
-    )
+    q_width = q_weight.shape[0] * device_count // model_width
+    k_width = k_weight.shape[0] * device_count // model_width
+    ff_width = gate_weight.shape[0] * device_count // model_width
+    team_width = ff_width // TEAM
+    column_run = 2 * ff_width // device_count
+    masks = team_masks()
+
+    in_plan = RowPlan(model_width)
+    out_plan = RowPlan(q_width)
+    weight_in = in_plan.gather((q_weight, k_weight, v_weight), place)
+    select_in = in_plan.selector(place)
+    weight_out = out_plan.gather((o_weight,), place)
+    select_out = out_plan.selector(place)
+
+    shard_size = gate_weight.shape[0]
+    piece_size = shard_size // TEAM
+    piece_shape = (
+        (piece_size // team_width, team_width) if piece_size % team_width == 0 else (piece_size,)
+    )
+
+    def column_runs(flat):
+        return flat.reshape(-1, TEAM, column_run)
+
+    runs = jnp.stack([column_runs(gate_weight), column_runs(up_weight)])
+    arrived = jnp.stack(
+        [
+            swap(pick(runs, member ^ r, 2), masks[r]) if r else pick(runs, member, 2)
+            for r in range(TEAM)
+        ]
+    )
+    ordered = jnp.stack([pick(arrived, member ^ t) for t in range(TEAM)], axis=1)
+    pair_rel = outer_gather(ordered.reshape((2, TEAM) + piece_shape))
+    down_rel = outer_gather(down_weight.reshape(-1, model_width))
+    core = place & 1
+
+    def in_order(rel, core_axis):
+        blocks = []
+        for j in range(outer_count):
+            pieces = [pick(pick(rel, core ^ c), outer_index ^ j) for c in range(2)]
+            blocks.append(jnp.stack(pieces, axis=core_axis))
+        return jnp.stack(blocks)
+
+    pair = in_order(pair_rel, 2)
+    weight_gate = pair[:, 0].reshape(model_width, team_width)
+    weight_up = pair[:, 1].reshape(model_width, team_width)
+    weight_down = in_order(down_rel, 0).reshape(team_width, model_width)
+    cotangent_all = team_gather(cotangent)
+
     input_rows = hidden_in.astype(jnp.float32)
     scale_one = norm_scale(input_rows)
     normed_one = (input_rows * scale_one * norm1_gain[None, :]).astype(jnp.bfloat16)
+    placed_one = forward_product(normed_one, select_in).astype(jnp.bfloat16)
     cosine, sine_table = rotary_tables(positions)
-    query_low = rotate(forward_product(normed_one, weight_query), cosine, sine_table).astype(
-        jnp.bfloat16
-    )
-    key_low = rotate(forward_product(normed_one, weight_key), cosine, sine_table).astype(
-        jnp.bfloat16
-    )
-    value_low = forward_product(normed_one, weight_value).astype(jnp.bfloat16)
-    key_pieces = [key_low]
-    value_pieces = [value_low]
-    for distance in range(1, window_span + 1):
-        arrived = passed_along((key_low, value_low), "fsdp", distance)
-        key_pieces.insert(0, arrived[0])
-        value_pieces.insert(0, arrived[1])
-    key_window = jnp.concatenate(key_pieces, axis=0)
-    value_window = jnp.concatenate(value_pieces, axis=0)
+    projected = forward_product(placed_one, weight_in)
+    rotated = rotate(projected[:, : q_width + k_width], cosine, sine_table).astype(jnp.bfloat16)
+    query_low = rotated[:, :q_width]
+    key_value = jnp.concatenate(
+        [rotated[:, q_width:], projected[:, q_width + k_width :].astype(jnp.bfloat16)], axis=1
+    )
+    pieces = [passed_along(key_value, distance) for distance in range(window_span, 0, -1)]
+    window = jnp.concatenate(pieces + [key_value], axis=0)
+    key_window = window[:, :k_width]
+    value_window = window[:, k_width:]
     attended_low, log_total = attend(query_low, key_window, value_window, positions, prefix)
-    mid_rows = input_rows + forward_product(attended_low, weight_out)
+    placed_attended = forward_product(attended_low, select_out).astype(jnp.bfloat16)
+    mid_rows = input_rows + forward_product(placed_attended, weight_out)
     scale_two = norm_scale(mid_rows)
     normed_two = (mid_rows * scale_two * norm2_gain[None, :]).astype(jnp.bfloat16)
-    gate_pre = forward_product(normed_two, weight_gate)
-    up_pre = forward_product(normed_two, weight_up)
+
+    normed_all = team_gather(normed_two)
+    gate_pre = forward_product(normed_all, weight_gate)
+    up_pre = forward_product(normed_all, weight_up)
     sigmoid_gate = jax.nn.sigmoid(gate_pre)
     silu_gate = gate_pre * sigmoid_gate
     hidden_low = (silu_gate * up_pre).astype(jnp.bfloat16)
-    block_out = (mid_rows + forward_product(hidden_low, weight_down)).astype(jnp.bfloat16)
-    grad_down = outer_sum(hidden_low, cotangent)
-    grad_hidden = back_product(cotangent, weight_down)
+    grad_hidden = back_product(cotangent_all, weight_down)
     grad_gate_low = (
         grad_hidden * up_pre * sigmoid_gate * (1.0 + gate_pre * (1.0 - sigmoid_gate))
     ).astype(jnp.bfloat16)
     grad_up_low = (grad_hidden * silu_gate).astype(jnp.bfloat16)
-    grad_gate = outer_sum(normed_two, grad_gate_low)
-    grad_up = outer_sum(normed_two, grad_up_low)
-    grad_normed_two = back_product(grad_gate_low, weight_gate) + back_product(
-        grad_up_low, weight_up
-    )
+    grad_normed_two = team_scatter(
+        back_product(grad_gate_low, weight_gate) + back_product(grad_up_low, weight_up), tok_rows
+    )
+    block_out = (
+        mid_rows + team_scatter(forward_product(hidden_low, weight_down), tok_rows)
+    ).astype(jnp.bfloat16)
+
+    grad_down = outer_scatter(
+        outer_sum(hidden_low, cotangent_all).reshape(outer_count, 2, -1, model_width), place
+    ).reshape(-1)
+    pair_shape = (outer_count, TEAM, 2) + piece_shape
+    grad_pair = outer_scatter(
+        jnp.stack(
+            [
+                jnp.moveaxis(outer_sum(normed_all, grad_low).reshape(pair_shape), 2, 1)
+                for grad_low in (grad_gate_low, grad_up_low)
+            ],
+            axis=2,
+        ),
+        place,
+    )
+    returned = jnp.stack(
+        [
+            swap(pick(grad_pair, member ^ r, 1).astype(LINK), masks[r]).astype(jnp.float32)
+            if r
+            else pick(grad_pair, member, 1)
+            for r in range(TEAM)
+        ]
+    ).reshape(TEAM, 2, -1, column_run)
+    ordered_back = jnp.stack([pick(returned, member ^ t) for t in range(TEAM)], axis=2)
+    grad_gate = ordered_back[0].reshape(-1)
+    grad_up = ordered_back[1].reshape(-1)
+
     grad_mid_norm, grad_gain_two = norm_backward(mid_rows, scale_two, norm2_gain, grad_normed_two)
     grad_mid = cotangent.astype(jnp.float32) + grad_mid_norm
     grad_mid_low = grad_mid.astype(jnp.bfloat16)
-    grad_out = outer_sum(attended_low, grad_mid_low)
-    grad_attended_low = back_product(grad_mid_low, weight_out).astype(jnp.bfloat16)
+    (grad_out,) = out_plan.scatter(outer_sum(placed_attended, grad_mid_low), (model_width,), place)
+    grad_attended_low = back_product(
+        back_product(grad_mid_low, weight_out).astype(jnp.bfloat16), select_out
+    ).astype(jnp.bfloat16)
     grad_query, grad_key_window, grad_value_window = attend_back(
         query_low,
         key_window,
@@ -244,69 +445,45 @@
         attended_low,
         grad_attended_low,
     )
-    own_key = grad_key_window[prefix:]
-    own_value = grad_value_window[prefix:]
+    grad_window = jnp.concatenate([grad_key_window, grad_value_window], axis=1)
+    own_pair = grad_window[prefix:]
     for distance in range(1, window_span + 1):
         start_row = prefix - distance * tok_rows
-        returned = passed_along(
-            (
-                grad_key_window[start_row : start_row + tok_rows],
-                grad_value_window[start_row : start_row + tok_rows],
-            ),
-            "fsdp",
-            -distance,
-        )
-        own_key = own_key + returned[0]
-        own_value = own_value + returned[1]
-    grad_query_in = rotate(grad_query, cosine, -sine_table).astype(jnp.bfloat16)
-    grad_key_in = rotate(own_key, cosine, -sine_table).astype(jnp.bfloat16)
-    grad_value_in = own_value.astype(jnp.bfloat16)
-    grad_query_weight = outer_sum(normed_one, grad_query_in)
-    grad_key_weight = outer_sum(normed_one, grad_key_in)
-    grad_value_weight = outer_sum(normed_one, grad_value_in)
-    grad_normed_one = (
-        back_product(grad_query_in, weight_query)
-        + back_product(grad_key_in, weight_key)
-        + back_product(grad_value_in, weight_value)
+        part = grad_window[start_row : start_row + tok_rows].astype(LINK)
+        own_pair = own_pair + passed_along(part, -distance).astype(jnp.float32)
+    turned_back = rotate(
+        jnp.concatenate([grad_query, own_pair[:, :k_width]], axis=1), cosine, -sine_table
+    )
+    grad_projected = jnp.concatenate([turned_back, own_pair[:, k_width:]], axis=1).astype(
+        jnp.bfloat16
+    )
+    grad_query_weight, grad_key_weight, grad_value_weight = in_plan.scatter(
+        outer_sum(placed_one, grad_projected), (q_width, k_width, k_width), place
+    )
+    grad_normed_one = lax.dot_general(
+        back_product(grad_projected, weight_in),
+        select_in.astype(jnp.float32),
+        (((1,), (1,)), ((), ())),
+        precision=lax.Precision.HIGHEST,
+        preferred_element_type=jnp.float32,
     )
     grad_in_norm, grad_gain_one = norm_backward(input_rows, scale_one, norm1_gain, grad_normed_one)
     grad_in = (grad_mid + grad_in_norm).astype(jnp.bfloat16)
-    shards = (
-        lax.psum_scatter(
-            grad_query_weight.reshape(device_count, -1), "fsdp", scatter_dimension=0, tiled=True
-        ),
-        lax.psum_scatter(
-            grad_key_weight.reshape(device_count, -1), "fsdp", scatter_dimension=0, tiled=True
-        ),
-        lax.psum_scatter(
-            grad_value_weight.reshape(device_count, -1), "fsdp", scatter_dimension=0, tiled=True
-        ),
-        lax.psum_scatter(
-            grad_out.reshape(device_count, -1), "fsdp", scatter_dimension=0, tiled=True
-        ),
-        lax.psum_scatter(
-            grad_gate.reshape(device_count, -1), "fsdp", scatter_dimension=0, tiled=True
-        ),
-        lax.psum_scatter(
-            grad_up.reshape(device_count, -1), "fsdp", scatter_dimension=0, tiled=True
-        ),
-        lax.psum_scatter(
-            grad_down.reshape(device_count, -1), "fsdp", scatter_dimension=0, tiled=True
-        ),
-    )
-    gain_totals = lax.psum((grad_gain_one, grad_gain_two), "fsdp")
+    gains = jnp.stack([grad_gain_one, grad_gain_two])
+    for bit in range(device_count.bit_length() - 1):
+        gains = gains + swap(gains, 1 << bit)
     return (
         block_out,
         grad_in,
-        gain_totals[0],
-        shards[0].reshape(-1),
-        shards[1].reshape(-1),
-        shards[2].reshape(-1),
-        shards[3].reshape(-1),
-        gain_totals[1],
-        shards[4].reshape(-1),
-        shards[5].reshape(-1),
-        shards[6].reshape(-1),
+        gains[0],
+        grad_query_weight,
+        grad_key_weight,
+        grad_value_weight,
+        grad_out,
+        gains[1],
+        grad_gate,
+        grad_up,
+        grad_down,
     )
 
 

time: 1070 us -> 452 us (0.42)
  waiting for transfers between devices: 616 us -> 137 us
  blocking collectives: 142 us -> 0 us
  starting transfers between devices: 26.5 us -> 84.5 us
  other arithmetic: 94.6 us -> 45.6 us
  local copies, waits for them, and re-layouts: 108 us -> 127 us
  matrix products: 61.1 us -> 47 us
  between operations: 15.4 us -> 2.66 us
    unnamed x7 -> x0, waiting for transfers between devices: 527 us -> none
    ppermute x16 -> x67, waiting for transfers between devices: 3.74 us -> 137 us  [the longest x59 129 us: swap(): return lax.ppermute(block, AXIS, [(i, i ^ mask) for i in range(size)])]
    all_gather x4 -> x0, other arithmetic: 89 us -> none  [the longest x1 40.8 us: local(): lax.all_gather(o_weight, 'fsdp', axis=0, tiled=True)]
    all_gather x2 -> x0, blocking collectives: 88.6 us -> none  [the longest x1 47.7 us: local(): lax.all_gather(v_weight, 'fsdp', axis=0, tiled=True)]
    all_gather x5 -> x0, waiting for transfers between devices: 85.6 us -> none  [the longest x1 48.9 us: local(): lax.all_gather(down_weight, 'fsdp', axis=0, tiled=True)]
    reshape x16 -> x10, local copies, waits for them, and re-layouts: 91.2 us -> 12.9 us  [the longest x2 6.37 us: local(): outer_sum(normed_all, grad_low).reshape(pair_shape)]
    ppermute x16 -> x67, starting transfers between devices: 26.3 us -> 84.5 us  [the longest x59 66.9 us: swap(): return lax.ppermute(block, AXIS, [(i, i ^ mask) for i in range(size)])]
    psum x1 -> x0, blocking collectives: 52.9 us -> none  [local(): gain_totals = lax.psum((grad_gain_one, grad_gain_two), 'fsdp')]
  transfers between devices with their start and end apart: 22 -> 67, of which waited for: 5 -> 22; matrix products, arithmetic and copies ran while one was open for 19% -> 39% of each run, Pallas kernels for 0% -> 0%
where the time goes in v1:
time: 452 us; the launch traced here: 443 us
  waiting for transfers between devices  137 us (30%)
  local copies, waits for them, and re-layouts  127 us (28%)
  starting transfers between devices  84.5 us (19%)
  matrix products  47 us (10%)
  other arithmetic  45.6 us (10%)
    ppermute x59, waiting for transfers between devices, swap(): return lax.ppermute(block, AXIS, [(i, i ^ mask) for i in range(size)])  129 us
    ppermute x59, starting transfers between devices, swap(): return lax.ppermute(block, AXIS, [(i, i ^ mask) for i in range(size)])  66.9 us
    unnamed x158, local copies, waits for them, and re-layouts  24.3 us
    ppermute x8, starting transfers between devices, passed_along(): return lax.ppermute(block, AXIS, route)  17.6 us
    ppermute x10, local copies, waits for them, and re-layouts, swap(): return lax.ppermute(block, AXIS, [(i, i ^ mask) for i in range(size)])  16.7 us
    dot_general x7, matrix products, forward_product(): return jnp.dot(left_side, weight, preferred_element_type=jnp.float32)  12.8 us
    another operation x8, local copies, waits for them, and re-layouts, local(): jnp.stack([swap(pick(grad_pair, member ^ r, 1).astype(LINK), masks[r]).as...  11.9 us
    dot_general x5, matrix products, outer_sum(): lax.dot_general(left_side, right_side, (((0,), (0,)), ((), ())), preferre...  11.7 us
  transfers between devices with their start and end apart: 67, of which 22 were waited for; matrix products, arithmetic and copies ran while one was open for 39% of the time, Pallas kernels for 0%

profile of v1, /device:TPU:0, one launch (start us, length us, event | category | flops | bytes accessed | tf_op | source)
XLA Modules:
  0.0 443.4 jit_solution(478596133939683106)
XLA Ops:
  4.0 3.1 collective-permute-start
  11.5 3.0 collective-permute-start.21
  37.8 5.9 %collective-permute-start.26 = (bf16[2,80,960]{2,1,0:T(8,128)(2,1)}, bf16[2,80,960]{2,1,0:T(8,128)(2,1)}, u32[]{:S(2)}, u32[]{:S(2)}) collective-permute-start(bf16[2,80,960]{2,1,0:T(8,128)(2,1)} %pad_maximum_fusion.11), channel_id=1, source_target_pairs={{0,16},{1,17},{2,18},{3,19},{4,20},{5,21},{6,22},{7,23},{8,24},{9,... | collective-permute-start | bytes 921608 | tf_op jit(solution)/shard_map/ppermute | solution.py:25
  50.2 4.8 %collective-permute-done.1 = bf16[64,1600]{1,0:T(8,128)(2,1)S(1)} collective-permute-done((bf16[64,1600]{1,0:T(8,128)(2,1)}, bf16[64,1600]{1,0:T(8,128)(2,1)S(1)}, u32[]{:S(2)}, u32[]{:S(2)}) %collective-permute-start.1) | collective-permute-done | bytes 204832 | tf_op jit(solution)/shard_map/ppermute | solution.py:25
  64.4 4.1 collective-permute-done.13
  77.5 9.3 %collective-permute-done.3 = bf16[128,1600]{1,0:T(8,128)(2,1)S(1)} collective-permute-done((bf16[128,1600]{1,0:T(8,128)(2,1)}, bf16[128,1600]{1,0:T(8,128)(2,1)S(1)}, u32[]{:S(2)}, u32[]{:S(2)}) %collective-permute-start.3) | collective-permute-done | bytes 409632 | tf_op jit(solution)/shard_map/ppermute | solution.py:25
  90.6 3.6 copy.112
  116.2 4.8 %concatenate.90 = bf16[1024,960]{0,1:T(8,128)(2,1)} concatenate(bf16[32,960]{0,1:T(8,128)(2,1)} %copy.121, bf16[32,960]{0,1:T(8,128)(2,1)} %copy.122, bf16[64,960]{0,1:T(8,128)(2,1)} %copy.123, bf16[128,960]{0,1:T(8,128)(2,1)} %copy.124, bf16[128,960]{0,1:T(8,128)(2,1)} %copy.125, bf16[128,960]{0,1:T(8,128)(2,1)} %copy.126, bf16[512,960]{0,1:T(8,128)(2,1)} %collective-permute-done.15), dimensions={0} | concatenate | bytes 3932160 | tf_op jit(solution)/shard_map/concatenate | solution.py:227
  128.0 5.2 %concatenate.83 = bf16[1024,1600]{0,1:T(8,128)(2,1)S(1)} concatenate(bf16[32,1600]{0,1:T(8,128)(2,1)} %copy.113, bf16[32,1600]{0,1:T(8,128)(2,1)} %copy.114, bf16[64,1600]{0,1:T(8,128)(2,1)} %copy.115, bf16[128,1600]{0,1:T(8,128)(2,1)} %copy.116, bf16[128,1600]{0,1:T(8,128)(2,1)} %copy.117, bf16[128,1600]{0,1:T(8,128)(2,1)} %copy.118, bf16[512,1600]{0,1:T(8,128)(2,1)} %collective-permute-done.5), dimensions={0} | concatenate | bytes 6553600 | tf_op jit(solution)/shard_map/concatenate | solution.py:227
  137.5 5.9 %collective-permute-start.7 = (bf16[128,640]{0,1:T(8,128)(2,1)S(1)}, bf16[128,640]{0,1:T(8,128)(2,1)S(1)}, u32[]{:S(2)}, u32[]{:S(2)}) collective-permute-start(bf16[128,640]{0,1:T(8,128)(2,1)S(1)} %pad_maximum_fusion.17), channel_id=1, source_target_pairs={{0,3},{1,4},{2,5},{3,6},{4,7},{5,8},{6,9},{7,10},{8,11},{9,12},{10... | collective-permute-start | bytes 491528 | tf_op jit(solution)/shard_map/ppermute | solution.py:31
  160.0 4.3 collective-permute-start.18
  200.2 3.7 fusion.111
  203.8 3.0 reshape.431
  206.8 3.9 fusion.110
  210.7 3.4 reshape.432
  222.2 3.6 collective-permute-done.28
  228.4 3.5 fusion.21
  233.1 3.8 fusion.95
  236.9 4.2 fusion.2
  250.2 3.6 collective-permute-done.38
  264.1 3.1 collective-permute-start.43
  277.8 15.2 %collective-permute-done.65 = bf16[2,80,960]{2,1,0:T(8,128)(2,1)S(1)} collective-permute-done((bf16[2,80,960]{2,1,0:T(8,128)(2,1)S(1)}, bf16[2,80,960]{2,1,0:T(8,128)(2,1)S(1)}, u32[]{:S(2)}, u32[]{:S(2)}) %collective-permute-start.65) | collective-permute-done | bytes 307232 | tf_op jit(solution)/shard_map/ppermute | solution.py:25
  297.4 3.2 bitcast_add_fusion
  300.6 3.1 collective-permute-done.55
  303.6 4.3 collective-permute-done.54
  312.3 24.2 %collective-permute-done.56 = bf16[64,960]{0,1:T(8,128)(2,1)S(1)} collective-permute-done((bf16[64,960]{0,1:T(8,128)(2,1)S(1)}, bf16[64,960]{0,1:T(8,128)(2,1)S(1)}, u32[]{:S(2)}, u32[]{:S(2)}) %collective-permute-start.56) | collective-permute-done | bytes 122912 | tf_op jit(solution)/shard_map/ppermute | solution.py:25
  338.2 15.7 %collective-permute-done.57 = bf16[32,960]{0,1:T(8,128)(2,1)S(1)} collective-permute-done((bf16[32,960]{0,1:T(8,128)(2,1)}, bf16[32,960]{0,1:T(8,128)(2,1)S(1)}, u32[]{:S(2)}, u32[]{:S(2)}) %collective-permute-start.57) | collective-permute-done | bytes 61472 | tf_op jit(solution)/shard_map/ppermute | solution.py:25
  358.2 3.0 fusion.115
  361.2 6.1 %collective-permute-done.60 = bf16[1,2,4,30,640]{4,2,3,1,0:T(4,128)(2,1)S(1)} collective-permute-done((bf16[1,2,4,30,640]{4,2,3,1,0:T(4,128)(2,1)S(1)}, bf16[1,2,4,30,640]{4,2,3,1,0:T(4,128)(2,1)S(1)}, u32[]{:S(2)}, u32[]{:S(2)}) %collective-permute-start.60) | collective-permute-done | bytes 307232 | tf_op jit(solution)/shard_map/ppermute | solution.py:25
  386.4 8.7 %collective-permute-done.62 = bf16[2,30,640]{2,0,1:T(2,128)(2,1)} collective-permute-done((bf16[2,30,640]{2,0,1:T(2,128)(2,1)}, bf16[2,30,640]{2,0,1:T(2,128)(2,1)}, u32[]{:S(2)}, u32[]{:S(2)}) %collective-permute-start.62) | collective-permute-done | bytes 76832 | tf_op jit(solution)/shard_map/ppermute | solution.py:25
  409.5 19.5 %collective-permute-done.50 = bf16[64,1600]{0,1:T(8,128)(2,1)S(1)} collective-permute-done((bf16[64,1600]{0,1:T(8,128)(2,1)S(1)}, bf16[64,1600]{0,1:T(8,128)(2,1)S(1)}, u32[]{:S(2)}, u32[]{:S(2)}) %collective-permute-start.50) | collective-permute-done | bytes 204832 | tf_op jit(solution)/shard_map/ppermute | solution.py:25
  432.2 8.3 %collective-permute-done.51 = bf16[32,1600]{0,1:T(8,128)(2,1)S(1)} collective-permute-done((bf16[32,1600]{0,1:T(8,128)(2,1)S(1)}, bf16[32,1600]{0,1:T(8,128)(2,1)S(1)}, u32[]{:S(2)}, u32[]{:S(2)}) %collective-permute-start.51) | collective-permute-done | bytes 102432 | tf_op jit(solution)/shard_map/ppermute | solution.py:25
  (466 shorter events, 239.8 us)
Async XLA Ops:
  4.0 29.4 %collective-permute-start = (bf16[32,1600]{1,0:T(8,128)(2,1)S(1)}, bf16[32,1600]{1,0:T(8,128)(2,1)S(1)}, u32[]{:S(2)}, u32[]{:S(2)}) collective-permute-start(bf16[32,1600]{1,0:T(8,128)(2,1)S(1)} %get-tuple-element.85), channel_id=1, source_target_pairs={{0,8},{1,9},{2,10},{3,11},{4,12},{5,13},{6,14},{7,15},{8,0},{9,1},... | collective-permute-start | bytes 307208 | tf_op jit(solution)/shard_map/ppermute | solution.py:25
  15.2 79.1 %collective-permute-start.31 = (bf16[128,960]{0,1:T(8,128)(2,1)}, bf16[128,960]{0,1:T(8,128)(2,1)}, u32[]{:S(2)}, u32[]{:S(2)}) collective-permute-start(bf16[128,960]{0,1:T(8,128)(2,1)} %param.25), channel_id=1, source_target_pairs={{0,2},{1,3},{2,0},{3,1},{4,6},{5,7},{6,4},{7,5},{8,10},{9,11},{10,... | collective-permute-start | bytes 737288 | tf_op jit(solution)/shard_map/ppermute | solution.py:25
  32.9 25.2 %collective-permute-start.22 = (bf16[1,2,4,30,640]{4,3,1,2,0:T(8,128)(2,1)S(1)}, bf16[1,2,4,30,640]{4,3,1,2,0:T(8,128)(2,1)S(1)}, u32[]{:S(2)}, u32[]{:S(2)}) collective-permute-start(bf16[1,2,4,30,640]{4,3,1,2,0:T(8,128)(2,1)S(1)} %constant_dynamic-update-slice_fusion.19), channel_id=1, source_target_pairs={{0,8},{1,9},{2,10},{3,11},{4,12},{5,13},{6,14},{7,15},{8,0},{9,1},... | collective-permute-start | bytes 921608 | tf_op jit(solution)/shard_map/ppermute | solution.py:25
  34.1 20.9 %collective-permute-start.1 = (bf16[64,1600]{1,0:T(8,128)(2,1)}, bf16[64,1600]{1,0:T(8,128)(2,1)S(1)}, u32[]{:S(2)}, u32[]{:S(2)}) collective-permute-start(bf16[64,1600]{1,0:T(8,128)(2,1)} %pad_maximum_fusion.16), channel_id=1, source_target_pairs={{0,16},{1,17},{2,18},{3,19},{4,20},{5,21},{6,22},{7,23},{8,24},{9,... | collective-permute-start | bytes 614408 | tf_op jit(solution)/shard_map/ppermute | solution.py:25
  37.8 37.1 %collective-permute-start.26 = (bf16[2,80,960]{2,1,0:T(8,128)(2,1)}, bf16[2,80,960]{2,1,0:T(8,128)(2,1)}, u32[]{:S(2)}, u32[]{:S(2)}) collective-permute-start(bf16[2,80,960]{2,1,0:T(8,128)(2,1)} %pad_maximum_fusion.11), channel_id=1, source_target_pairs={{0,16},{1,17},{2,18},{3,19},{4,20},{5,21},{6,22},{7,23},{8,24},{9,... | collective-permute-start | bytes 921608 | tf_op jit(solution)/shard_map/ppermute | solution.py:25
  68.5 18.3 %collective-permute-start.3 = (bf16[128,1600]{1,0:T(8,128)(2,1)}, bf16[128,1600]{1,0:T(8,128)(2,1)S(1)}, u32[]{:S(2)}, u32[]{:S(2)}) collective-permute-start(bf16[128,1600]{1,0:T(8,128)(2,1)} %pad_maximum_fusion.7), channel_id=1, source_target_pairs={{0,4},{1,5},{2,6},{3,7},{4,0},{5,1},{6,2},{7,3},{8,12},{9,13},{10,... | collective-permute-start | bytes 1228808 | tf_op jit(solution)/shard_map/ppermute | solution.py:25
  71.0 16.7 %collective-permute-start.23 = (bf16[2,2,4,30,640]{4,2,3,1,0:T(4,128)(2,1)}, bf16[2,2,4,30,640]{4,2,3,1,0:T(4,128)(2,1)}, u32[]{:S(2)}, u32[]{:S(2)}) collective-permute-start(bf16[2,2,4,30,640]{4,2,3,1,0:T(4,128)(2,1)} %copy.135), channel_id=1, source_target_pairs={{0,16},{1,17},{2,18},{3,19},{4,20},{5,21},{6,22},{7,23},{8,24},{9,... | collective-permute-start | bytes 1843208 | tf_op jit(solution)/shard_map/ppermute | solution.py:25
  74.9 19.9 %collective-permute-start.32 = (bf16[128,960]{0,1:T(8,128)(2,1)}, bf16[128,960]{0,1:T(8,128)(2,1)}, u32[]{:S(2)}, u32[]{:S(2)}) collective-permute-start(bf16[128,960]{0,1:T(8,128)(2,1)} %param.25), channel_id=1, source_target_pairs={{0,4},{1,5},{2,6},{3,7},{4,0},{5,1},{6,2},{7,3},{8,12},{9,13},{10,... | collective-permute-start | bytes 737288 | tf_op jit(solution)/shard_map/ppermute | solution.py:25
  87.7 25.4 %collective-permute-start.27 = (bf16[4,80,960]{2,1,0:T(8,128)(2,1)S(1)}, bf16[4,80,960]{2,1,0:T(8,128)(2,1)}, u32[]{:S(2)}, u32[]{:S(2)}) collective-permute-start(bf16[4,80,960]{2,1,0:T(8,128)(2,1)S(1)} %constant_dynamic-update-slice_fusion.24), channel_id=1, source_target_pairs={{0,1},{1,0},{2,3},{3,2},{4,5},{5,4},{6,7},{7,6},{8,9},{9,8},{10,11... | collective-permute-start | bytes 1843208 | tf_op jit(solution)/shard_map/ppermute | solution.py:25
  89.1 31.9 %collective-permute-start.24 = (bf16[4,2,4,30,640]{4,2,3,1,0:T(4,128)(2,1)S(1)}, bf16[4,2,4,30,640]{4,2,3,1,0:T(4,128)(2,1)S(1)}, u32[]{:S(2)}, u32[]{:S(2)}) collective-permute-start(bf16[4,2,4,30,640]{4,2,3,1,0:T(4,128)(2,1)S(1)} %constant_dynamic-update-slice_fusion.23), channel_id=1, source_target_pairs={{0,1},{1,0},{2,3},{3,2},{4,5},{5,4},{6,7},{7,6},{8,9},{9,8},{10,11... | collective-permute-start | bytes 3686408 | tf_op jit(solution)/shard_map/ppermute | solution.py:25
  94.3 21.9 %collective-permute-start.15 = (bf16[512,960]{0,1:T(8,128)(2,1)}, bf16[512,960]{0,1:T(8,128)(2,1)}, u32[]{:S(2)}, u32[]{:S(2)}) collective-permute-start(bf16[512,960]{0,1:T(8,128)(2,1)} %copy.120), channel_id=1, source_target_pairs={{0,1},{1,0},{2,3},{3,2},{4,5},{5,4},{6,7},{7,6},{8,9},{9,8},{10,11... | collective-permute-start | bytes 2949128 | tf_op jit(solution)/shard_map/ppermute | solution.py:25
  94.8 33.2 %collective-permute-start.5 = (bf16[512,1600]{0,1:T(8,128)(2,1)}, bf16[512,1600]{0,1:T(8,128)(2,1)}, u32[]{:S(2)}, u32[]{:S(2)}) collective-permute-start(bf16[512,1600]{0,1:T(8,128)(2,1)} %copy.112), channel_id=1, source_target_pairs={{0,1},{1,0},{2,3},{3,2},{4,5},{5,4},{6,7},{7,6},{8,9},{9,8},{10,11... | collective-permute-start | bytes 4915208 | tf_op jit(solution)/shard_map/ppermute | solution.py:25
  160.0 16.7 %collective-permute-start.18 = (bf16[128,960]{0,1:T(8,128)(2,1)}, bf16[128,960]{0,1:T(8,128)(2,1)}, u32[]{:S(2)}, u32[]{:S(2)}) collective-permute-start(bf16[128,960]{0,1:T(8,128)(2,1)} %multiply_convert_fusion.3), channel_id=1, source_target_pairs={{0,6},{1,7},{2,4},{3,5},{4,2},{5,3},{6,0},{7,1},{8,14},{9,15},{10,... | collective-permute-start | bytes 737288 | tf_op jit(solution)/shard_map/ppermute | solution.py:25
  192.4 27.2 %collective-permute-start.36 = (bf16[128,960]{0,1:T(8,128)(2,1)}, bf16[128,960]{0,1:T(8,128)(2,1)}, u32[]{:S(2)}, u32[]{:S(2)}) collective-permute-start(bf16[128,960]{0,1:T(8,128)(2,1)} %get-tuple-element.52), channel_id=1, source_target_pairs={{0,6},{1,7},{2,4},{3,5},{4,2},{5,3},{6,0},{7,1},{8,14},{9,15},{10,... | collective-permute-start | bytes 737288 | tf_op jit(solution)/shard_map/ppermute | solution.py:25
  194.3 25.5 %collective-permute-start.35 = (bf16[128,960]{0,1:T(8,128)(2,1)}, bf16[128,960]{0,1:T(8,128)(2,1)}, u32[]{:S(2)}, u32[]{:S(2)}) collective-permute-start(bf16[128,960]{0,1:T(8,128)(2,1)} %get-tuple-element.53), channel_id=1, source_target_pairs={{0,4},{1,5},{2,6},{3,7},{4,0},{5,1},{6,2},{7,3},{8,12},{9,13},{10,... | collective-permute-start | bytes 737288 | tf_op jit(solution)/shard_map/ppermute | solution.py:25
  195.7 24.0 %collective-permute-start.34 = (bf16[128,960]{0,1:T(8,128)(2,1)}, bf16[128,960]{0,1:T(8,128)(2,1)}, u32[]{:S(2)}, u32[]{:S(2)}) collective-permute-start(bf16[128,960]{0,1:T(8,128)(2,1)} %get-tuple-element.51), channel_id=1, source_target_pairs={{0,2},{1,3},{2,0},{3,1},{4,6},{5,7},{6,4},{7,5},{8,10},{9,11},{10,... | collective-permute-start | bytes 737288 | tf_op jit(solution)/shard_map/ppermute | solution.py:25
  196.8 25.4 %collective-permute-start.30 = (bf16[128,960]{0,1:T(8,128)(2,1)}, bf16[128,960]{0,1:T(8,128)(2,1)}, u32[]{:S(2)}, u32[]{:S(2)}) collective-permute-start(bf16[128,960]{0,1:T(8,128)(2,1)} %get-tuple-element.55), channel_id=1, source_target_pairs={{0,6},{1,7},{2,4},{3,5},{4,2},{5,3},{6,0},{7,1},{8,14},{9,15},{10,... | collective-permute-start | bytes 737288 | tf_op jit(solution)/shard_map/ppermute | solution.py:25
  198.7 23.5 %collective-permute-start.29 = (bf16[128,960]{0,1:T(8,128)(2,1)}, bf16[128,960]{0,1:T(8,128)(2,1)}, u32[]{:S(2)}, u32[]{:S(2)}) collective-permute-start(bf16[128,960]{0,1:T(8,128)(2,1)} %get-tuple-element.56), channel_id=1, source_target_pairs={{0,4},{1,5},{2,6},{3,7},{4,0},{5,1},{6,2},{7,3},{8,12},{9,13},{10,... | collective-permute-start | bytes 737288 | tf_op jit(solution)/shard_map/ppermute | solution.py:25
  219.8 77.6 %collective-permute-start.58 = (bf16[4,2,4,30,640]{4,2,3,1,0:T(4,128)(2,1)}, bf16[4,2,4,30,640]{4,2,3,1,0:T(4,128)(2,1)}, u32[]{:S(2)}, u32[]{:S(2)}) collective-permute-start(bf16[4,2,4,30,640]{4,2,3,1,0:T(4,128)(2,1)} %copy.148), channel_id=1, source_target_pairs={{0,1},{1,0},{2,3},{3,2},{4,5},{5,4},{6,7},{7,6},{8,9},{9,8},{10,11... | collective-permute-start | bytes 3686408 | tf_op jit(solution)/shard_map/ppermute | solution.py:25
  258.8 16.8 %collective-permute-start.64 = (bf16[4,80,960]{2,1,0:T(8,128)(2,1)S(1)}, bf16[4,80,960]{2,1,0:T(8,128)(2,1)S(1)}, u32[]{:S(2)}, u32[]{:S(2)}) collective-permute-start(bf16[4,80,960]{2,1,0:T(8,128)(2,1)S(1)} %fusion.28), channel_id=1, source_target_pairs={{0,1},{1,0},{2,3},{3,2},{4,5},{5,4},{6,7},{7,6},{8,9},{9,8},{10,11... | collective-permute-start | bytes 1843208 | tf_op jit(solution)/shard_map/ppermute | solution.py:25
  263.3 30.0 %collective-permute-start.52 = (bf16[512,960]{0,1:T(8,128)(2,1)S(1)}, bf16[512,960]{0,1:T(8,128)(2,1)S(1)}, u32[]{:S(2)}, u32[]{:S(2)}) collective-permute-start(bf16[512,960]{0,1:T(8,128)(2,1)S(1)} %slice.375), channel_id=1, source_target_pairs={{0,1},{1,0},{2,3},{3,2},{4,5},{5,4},{6,7},{7,6},{8,9},{9,8},{10,11... | collective-permute-start | bytes 2949128 | tf_op jit(solution)/shard_map/ppermute | solution.py:25
  272.5 85.7 %collective-permute-start.46 = (bf16[512,1600]{0,1:T(8,128)(2,1)}, bf16[512,1600]{0,1:T(8,128)(2,1)}, u32[]{:S(2)}, u32[]{:S(2)}) collective-permute-start(bf16[512,1600]{0,1:T(8,128)(2,1)} %slice.374), channel_id=1, source_target_pairs={{0,1},{1,0},{2,3},{3,2},{4,5},{5,4},{6,7},{7,6},{8,9},{9,8},{10,11... | collective-permute-start | bytes 4915208 | tf_op jit(solution)/shard_map/ppermute | solution.py:25
  275.8 17.2 %collective-permute-start.65 = (bf16[2,80,960]{2,1,0:T(8,128)(2,1)S(1)}, bf16[2,80,960]{2,1,0:T(8,128)(2,1)S(1)}, u32[]{:S(2)}, u32[]{:S(2)}) collective-permute-start(bf16[2,80,960]{2,1,0:T(8,128)(2,1)S(1)} %fusion.47), channel_id=1, source_target_pairs={{0,16},{1,17},{2,18},{3,19},{4,20},{5,21},{6,22},{7,23},{8,24},{9,... | collective-permute-start | bytes 921608 | tf_op jit(solution)/shard_map/ppermute | solution.py:25
  293.2 44.1 %collective-permute-start.66 = (bf16[1,80,960]{2,1,0:T(8,128)(2,1)S(1)}, bf16[1,80,960]{2,1,0:T(8,128)(2,1)S(1)}, u32[]{:S(2)}, u32[]{:S(2)}) collective-permute-start(bf16[1,80,960]{2,1,0:T(8,128)(2,1)S(1)} %dynamic-slice_convert_fusion.4), channel_id=1, source_target_pairs={{0,8},{1,9},{2,10},{3,11},{4,12},{5,13},{6,14},{7,15},{8,0},{9,1},... | collective-permute-start | bytes 460808 | tf_op jit(solution)/shard_map/ppermute | solution.py:25
  308.2 28.2 %collective-permute-start.56 = (bf16[64,960]{0,1:T(8,128)(2,1)S(1)}, bf16[64,960]{0,1:T(8,128)(2,1)S(1)}, u32[]{:S(2)}, u32[]{:S(2)}) collective-permute-start(bf16[64,960]{0,1:T(8,128)(2,1)S(1)} %slice.379), channel_id=1, source_target_pairs={{0,16},{1,17},{2,18},{3,19},{4,20},{5,21},{6,22},{7,23},{8,24},{9,... | collective-permute-start | bytes 368648 | tf_op jit(solution)/shard_map/ppermute | solution.py:25
  309.4 47.2 %collective-permute-start.59 = (bf16[2,2,4,30,640]{4,2,3,1,0:T(4,128)(2,1)}, bf16[2,2,4,30,640]{4,2,3,1,0:T(4,128)(2,1)}, u32[]{:S(2)}, u32[]{:S(2)}) collective-permute-start(bf16[2,2,4,30,640]{4,2,3,1,0:T(4,128)(2,1)} %fusion.29), channel_id=1, source_target_pairs={{0,16},{1,17},{2,18},{3,19},{4,20},{5,21},{6,22},{7,23},{8,24},{9,... | collective-permute-start | bytes 1843208 | tf_op jit(solution)/shard_map/ppermute | solution.py:25
  371.1 34.6 %collective-permute-start.49 = (bf16[128,1600]{0,1:T(8,128)(2,1)}, bf16[128,1600]{0,1:T(8,128)(2,1)}, u32[]{:S(2)}, u32[]{:S(2)}) collective-permute-start(bf16[128,1600]{0,1:T(8,128)(2,1)} %get-tuple-element.34), channel_id=1, source_target_pairs={{0,6},{1,7},{2,4},{3,5},{4,2},{5,3},{6,0},{7,1},{8,14},{9,15},{10,... | collective-permute-start | bytes 1228808 | tf_op jit(solution)/shard_map/ppermute | solution.py:25
  373.1 32.6 %collective-permute-start.48 = (bf16[128,1600]{0,1:T(8,128)(2,1)}, bf16[128,1600]{0,1:T(8,128)(2,1)}, u32[]{:S(2)}, u32[]{:S(2)}) collective-permute-start(bf16[128,1600]{0,1:T(8,128)(2,1)} %get-tuple-element.35), channel_id=1, source_target_pairs={{0,4},{1,5},{2,6},{3,7},{4,0},{5,1},{6,2},{7,3},{8,12},{9,13},{10,... | collective-permute-start | bytes 1228808 | tf_op jit(solution)/shard_map/ppermute | solution.py:25
  374.2 31.6 %collective-permute-start.47 = (bf16[128,1600]{0,1:T(8,128)(2,1)}, bf16[128,1600]{0,1:T(8,128)(2,1)}, u32[]{:S(2)}, u32[]{:S(2)}) collective-permute-start(bf16[128,1600]{0,1:T(8,128)(2,1)} %get-tuple-element.33), channel_id=1, source_target_pairs={{0,2},{1,3},{2,0},{3,1},{4,6},{5,7},{6,4},{7,5},{8,10},{9,11},{10,... | collective-permute-start | bytes 1228808 | tf_op jit(solution)/shard_map/ppermute | solution.py:25
  378.4 16.7 %collective-permute-start.62 = (bf16[2,30,640]{2,0,1:T(2,128)(2,1)}, bf16[2,30,640]{2,0,1:T(2,128)(2,1)}, u32[]{:S(2)}, u32[]{:S(2)}) collective-permute-start(bf16[2,30,640]{2,0,1:T(2,128)(2,1)} %bitcast.205), channel_id=1, source_target_pairs={{0,4},{1,5},{2,6},{3,7},{4,0},{5,1},{6,2},{7,3},{8,12},{9,13},{10,... | collective-permute-start | bytes 230408 | tf_op jit(solution)/shard_map/ppermute | solution.py:25
  381.4 17.0 %collective-permute-start.63 = (bf16[2,30,640]{2,0,1:T(2,128)(2,1)}, bf16[2,30,640]{2,0,1:T(2,128)(2,1)}, u32[]{:S(2)}, u32[]{:S(2)}) collective-permute-start(bf16[2,30,640]{2,0,1:T(2,128)(2,1)} %bitcast.204), channel_id=1, source_target_pairs={{0,6},{1,7},{2,4},{3,5},{4,2},{5,3},{6,0},{7,1},{8,14},{9,15},{10,... | collective-permute-start | bytes 230408 | tf_op jit(solution)/shard_map/ppermute | solution.py:25
  408.3 20.7 %collective-permute-start.50 = (bf16[64,1600]{0,1:T(8,128)(2,1)S(1)}, bf16[64,1600]{0,1:T(8,128)(2,1)S(1)}, u32[]{:S(2)}, u32[]{:S(2)}) collective-permute-start(bf16[64,1600]{0,1:T(8,128)(2,1)S(1)} %slice.377), channel_id=1, source_target_pairs={{0,16},{1,17},{2,18},{3,19},{4,20},{5,21},{6,22},{7,23},{8,24},{9,... | collective-permute-start | bytes 614408 | tf_op jit(solution)/shard_map/ppermute | solution.py:25
  (100 other events, 646.0 us)

commit v2 on v1

v2 whole, which is shorter than its diff:
```python
import math

import jax
import jax.numpy as jnp
from jax import lax
from jax.experimental import pallas as pl
from jax.experimental.pallas import tpu as pltpu
from jax.sharding import PartitionSpec as P

KV_HEADS = 5
HEAD_DIM = 64
MAXLEN = 512


EPS = 1e-05
NEG_FILL = -1e30
AXIS = "fsdp"
TEAM_BITS = (1, 2)
TEAM = 1 << len(TEAM_BITS)
LOW_BITS = 3
ROW_TILE = 16
LINK = jnp.bfloat16


def swap(block, mask):
    size = lax.axis_size(AXIS)
    return lax.ppermute(block, AXIS, [(i, i ^ mask) for i in range(size)])


def passed_along(block, distance):
    devices = range(lax.axis_size(AXIS))
    route = [(i - distance, i) for i in devices if i - distance in devices]
    return lax.ppermute(block, AXIS, route)


def pick(stack, index, axis=0):
    return lax.dynamic_index_in_dim(stack, index, axis, keepdims=False)


def team_masks():
    masks = []
    for member in range(TEAM):
        masks.append(sum(((member >> j) & 1) << bit for j, bit in enumerate(TEAM_BITS)))
    return masks


def rotary_tables(positions):
    half_width = HEAD_DIM // 2
    frequency = jnp.exp(
        jnp.arange(half_width, dtype=jnp.float32) * (-2.0 * math.log(10000.0) / HEAD_DIM)
    )
    angles = positions.astype(jnp.float32)[:, None] * frequency[None, :]
    return (jnp.cos(angles), jnp.sin(angles))


def rotate(matrix, cosine, sine_table):
    row_count = matrix.shape[0]
    half_width = HEAD_DIM // 2
    shaped = matrix.reshape(row_count, -1, HEAD_DIM)
    first_half = shaped[:, :, :half_width]
    second_half = shaped[:, :, half_width:]
    cosine_rows = cosine[:, None, :]
    sine_rows = sine_table[:, None, :]
    turned = jnp.concatenate(
        [
            first_half * cosine_rows - second_half * sine_rows,
            second_half * cosine_rows + first_half * sine_rows,
        ],
        axis=2,
    )
    return turned.reshape(row_count, -1)


def norm_scale(matrix):
    return lax.rsqrt(jnp.mean(matrix * matrix, axis=1, keepdims=True) + EPS)


def norm_backward(matrix, scale_rows, gain, grad_normed):
    unit_rows = matrix * scale_rows
    weighted = grad_normed * gain[None, :]
    grad_gain = jnp.sum(grad_normed * unit_rows, axis=0)
    grad_rows = scale_rows * (
        weighted - unit_rows * jnp.mean(weighted * unit_rows, axis=1, keepdims=True)
    )
    return (grad_rows, grad_gain)


def outer_sum(left_side, right_side):
    return lax.dot_general(
        left_side, right_side, (((0,), (0,)), ((), ())), preferred_element_type=jnp.float32
    )


def back_product(left_side, weight):
    return lax.dot_general(
        left_side, weight, (((1,), (1,)), ((), ())), preferred_element_type=jnp.float32
    )


def forward_product(left_side, weight):
    return jnp.dot(left_side, weight, preferred_element_type=jnp.float32)


def score_block(query_block, key_block, position_block, prefix):
    row_count = query_block.shape[0]
    key_count = key_block.shape[0]
    grouped = query_block.reshape(row_count, KV_HEADS, -1, HEAD_DIM)
    key_heads = key_block.reshape(key_count, KV_HEADS, HEAD_DIM)
    scores = jnp.einsum(
        "qkgd,skd->kgqs", grouped, key_heads, preferred_element_type=jnp.float32
    ) * HEAD_DIM ** (-0.5)
    key_offset = jnp.arange(key_count, dtype=jnp.int32) - prefix
    row_index = jnp.arange(row_count, dtype=jnp.int32)
    allowed = (key_offset[None, :] <= row_index[:, None]) & (
        key_offset[None, :] >= row_index[:, None] - position_block[:, None]
    )
    return jnp.where(allowed[None, None], scores, NEG_FILL)


def attend(query_block, key_block, value_block, position_block, prefix):
    row_count = query_block.shape[0]
    key_count = key_block.shape[0]
    scores = score_block(query_block, key_block, position_block, prefix)
    row_max = jnp.max(scores, axis=3, keepdims=True)
    log_total = row_max + jnp.log(jnp.sum(jnp.exp(scores - row_max), axis=3, keepdims=True))
    prob_low = jnp.exp(scores - log_total).astype(jnp.bfloat16)
    value_heads = value_block.reshape(key_count, KV_HEADS, HEAD_DIM)
    mixed_out = jnp.einsum(
        "kgqs,skd->qkgd", prob_low, value_heads, preferred_element_type=jnp.float32
    )
    return (mixed_out.reshape(row_count, -1).astype(jnp.bfloat16), log_total)


def attend_back(
    query_block,
    key_block,
    value_block,
    position_block,
    prefix,
    log_total,
    attended_block,
    grad_block,
):
    row_count = query_block.shape[0]
    key_count = key_block.shape[0]
    scores = score_block(query_block, key_block, position_block, prefix)
    prob_full = jnp.exp(scores - log_total)
    prob_low = prob_full.astype(jnp.bfloat16)
    grouped = query_block.reshape(row_count, KV_HEADS, -1, HEAD_DIM)
    grad_grouped = grad_block.reshape(row_count, KV_HEADS, -1, HEAD_DIM)
    out_grouped = attended_block.reshape(row_count, KV_HEADS, -1, HEAD_DIM)
    key_heads = key_block.reshape(key_count, KV_HEADS, HEAD_DIM)
    value_heads = value_block.reshape(key_count, KV_HEADS, HEAD_DIM)
    grad_prob = jnp.einsum(
        "qkgd,skd->kgqs", grad_grouped, value_heads, preferred_element_type=jnp.float32
    )
    delta_sum = jnp.einsum(
        "qkgd,qkgd->kgq", grad_grouped, out_grouped, preferred_element_type=jnp.float32
    )[..., None]
    grad_score = (prob_full * (grad_prob - delta_sum) * HEAD_DIM ** (-0.5)).astype(jnp.bfloat16)
    grad_query = jnp.einsum(
        "kgqs,skd->qkgd", grad_score, key_heads, preferred_element_type=jnp.float32
    ).reshape(row_count, -1)
    grad_key = jnp.einsum(
        "kgqs,qkgd->skd", grad_score, grouped, preferred_element_type=jnp.float32
    ).reshape(key_count, -1)
    grad_value = jnp.einsum(
        "kgqs,qkgd->skd", prob_low, grad_grouped, preferred_element_type=jnp.float32
    ).reshape(key_count, -1)
    return (grad_query, grad_key, grad_value)


def product(left_side, right_side, left_dim, right_dim):
    return lax.dot_general(
        left_side,
        right_side,
        (((left_dim,), (right_dim,)), ((), ())),
        preferred_element_type=jnp.float32,
    )


def kernel_call(body, outs, operands):
    return pl.pallas_call(
        body,
        out_shape=[jax.ShapeDtypeStruct(shape, dtype) for shape, dtype in outs],
        compiler_params=pltpu.CompilerParams(vmem_limit_bytes=60 * 1024 * 1024),
    )(*operands)


def tie(*values):
    return lax.optimization_barrier(values)


def bit_groups(bits):
    return [bits[i : i + 2] for i in range(0, len(bits), 2)]


def group_masks(bits):
    masks = [0]
    for bit in bits:
        masks += [m | (1 << bit) for m in masks]
    return masks


def spread(block, masks):
    return [block] + [swap(block, mask) for mask in masks[1:]]


def reduce_split(own, received, count):
    rows = own.shape[0] // count
    width = own.shape[1]

    def body(*refs):
        total = refs[0][...]
        for ref in refs[1 : 1 + len(received)]:
            total = total + ref[...].astype(jnp.float32)
        for i, out in enumerate(refs[1 + len(received) :]):
            out[...] = total[i * rows : (i + 1) * rows].astype(out.dtype)

    outs = [((rows, width), jnp.float32 if i == 0 else LINK) for i in range(count)]
    return kernel_call(body, outs, [own] + list(received))


class RowPlan:
    def __init__(self, row_total):
        size = lax.axis_size(AXIS)
        self.unit = size // math.gcd(size, row_total)
        self.rows = self.unit * row_total // size
        self.pitch = -(-self.rows // ROW_TILE) * ROW_TILE
        self.row_total = row_total
        unit_bits = self.unit.bit_length() - 1
        self.low = list(range(unit_bits))
        free = list(range(unit_bits, size.bit_length() - 1))
        self.outer = bit_groups([b for b in free if b >= LOW_BITS])
        self.team = group_masks([b for b in free if b in TEAM_BITS])
        self.last = group_masks([b for b in free if b < LOW_BITS and b not in TEAM_BITS])
        self.outer_set = group_masks([b for group in self.outer for b in group])

    def selector(self, place, distances):
        start = jnp.repeat(
            jnp.array([m // self.unit for m in distances], jnp.int32), self.pitch
        )
        within = jnp.tile(jnp.arange(self.pitch, dtype=jnp.int32), len(distances))
        row = ((place // self.unit) ^ start) * self.rows + within
        row = jnp.where(within < self.rows, row, -1)
        return (jnp.arange(self.row_total, dtype=jnp.int32)[:, None] == row[None, :]).astype(
            jnp.bfloat16
        )

    def whole_rows(self, flat, place):
        for bit in self.low:
            other = swap(flat, 1 << bit)
            high = (place >> bit) & 1
            flat = jnp.concatenate(
                [jnp.where(high == 1, other, flat), jnp.where(high == 1, flat, other)]
            )
        return flat.reshape(self.rows, -1)

    def own_share(self, block, place):
        flat = block.reshape(-1)
        for bit in reversed(self.low):
            high = (place >> bit) & 1
            halves = flat.reshape(2, -1)
            flat = pick(halves, high) + swap(
                pick(halves, 1 - high).astype(LINK), 1 << bit
            ).astype(jnp.float32)
        return flat

    def padded(self, block):
        return jnp.pad(block, ((0, self.pitch - self.rows), (0, 0)))

    def outer_pieces(self, block):
        pieces = [block]
        for group in self.outer:
            block = jnp.concatenate(pieces) if len(pieces) > 1 else pieces[0]
            pieces = spread(block, group_masks(group))
        return pieces

    def outer_sum(self, own, blocks):
        for step, group in enumerate(reversed(self.outer)):
            masks = group_masks(group)
            arrived = [swap(b, m) for b, m in zip(blocks, masks[1:])]
            following = self.outer[len(self.outer) - 2 - step] if step + 1 < len(self.outer) else []
            own, *blocks = reduce_split(own, arrived, 1 << len(following))
        return own


def pair_project(tokens, select, pieces):
    rows = tokens[0].shape[0]
    count = len(tokens)
    width = pieces[0].shape[1]
    depth = pieces[0].shape[0]

    def body(*refs):
        select_ref = refs[count]
        weights = refs[count + 1 : count + 1 + len(pieces)]
        outs = refs[count + 1 + len(pieces) :]
        for i in range(count):
            placed = product(refs[i][...], select_ref[...], 1, 0).astype(jnp.bfloat16)
            outs[count][i * rows : (i + 1) * rows, :] = placed
            total = product(placed[:, :depth], weights[0][...], 1, 0)
            for j in range(1, len(pieces)):
                total += product(placed[:, j * depth : (j + 1) * depth], weights[j][...], 1, 0)
            outs[i][...] = total

    outs = [((rows, width), jnp.float32)] * count
    outs.append(((count * rows, select.shape[1]), jnp.bfloat16))
    results = kernel_call(body, outs, list(tokens) + [select] + list(pieces))
    return results[:count], results[count]


def pair_back(grads, placed, select, pieces):
    count = len(grads)
    rows = grads[0].shape[0]
    width = pieces[0].shape[1]
    depth = pieces[0].shape[0]
    features = select.shape[0]

    def body(*refs):
        placed_ref, select_ref = refs[count : count + 2]
        weights = refs[count + 2 : count + 2 + len(pieces)]
        outs = refs[count + 2 + len(pieces) :]
        for j in range(len(pieces)):
            total = None
            for i in range(count):
                part = product(
                    placed_ref[i * rows : (i + 1) * rows, j * depth : (j + 1) * depth],
                    refs[i][...],
                    0,
                    0,
                )
                total = part if total is None else total + part
            outs[j][...] = total.astype(outs[j].dtype)
        for i in range(count):
            total = None
            for j in range(len(pieces)):
                back = product(refs[i][...], weights[j][...], 1, 1)
                high = back.astype(jnp.bfloat16)
                rest = (back - high.astype(jnp.float32)).astype(jnp.bfloat16)
                chosen = select_ref[:, j * depth : (j + 1) * depth]
                part = product(high, chosen, 1, 1) + product(rest, chosen, 1, 1)
                total = part if total is None else total + part
            outs[len(pieces) + i][...] = total

    outs = [((depth, width), jnp.float32 if j == 0 else LINK) for j in range(len(pieces))]
    outs += [((rows, features), jnp.float32)] * count
    results = kernel_call(body, outs, list(grads) + [placed, select] + list(pieces))
    return results[: len(pieces)], results[len(pieces) :]


def feed_forward(normed_blocks, cotangent_blocks, select, pair_pieces, down_pieces, order):
    count = len(normed_blocks)
    rows, features = normed_blocks[0].shape
    total_rows = count * rows
    depth, both = pair_pieces[0].shape
    width = both // 2
    down_rows = down_pieces[0].shape[0]
    pair_count = len(pair_pieces)
    down_count = len(down_pieces)

    def body(*refs):
        at = 0
        normed = refs[at : at + count]
        at += count
        grads = refs[at : at + count]
        at += count
        select_ref = refs[at]
        at += 1
        weights = refs[at : at + pair_count]
        at += pair_count
        downs = refs[at : at + down_count]
        at += down_count
        order_ref = refs[at]
        placed_out, hidden_out, low_out, *back_outs = refs[at + 1 :]
        down = product(
            order_ref[...], jnp.concatenate([d[...] for d in downs], axis=0), 1, 0
        ).astype(jnp.bfloat16)
        for i in range(count):
            span = slice(i * rows, (i + 1) * rows)
            placed = product(normed[i][...], select_ref[...], 1, 0).astype(jnp.bfloat16)
            placed_out[span, :] = placed
            total = product(placed[:, :depth], weights[0][...], 1, 0)
            for j in range(1, pair_count):
                total += product(placed[:, j * depth : (j + 1) * depth], weights[j][...], 1, 0)
            gate_pre = total[:, :width]
            up_pre = total[:, width:]
            sigmoid_gate = 1.0 / (1.0 + jnp.exp(-gate_pre))
            silu_gate = gate_pre * sigmoid_gate
            hidden = (silu_gate * up_pre).astype(jnp.bfloat16)
            hidden_out[span, :] = product(hidden, order_ref[...], 1, 0).astype(jnp.bfloat16)
            grad_hidden = product(grads[i][...], down, 1, 1)
            low_out[span, :width] = (
                grad_hidden * up_pre * sigmoid_gate * (1.0 + gate_pre * (1.0 - sigmoid_gate))
            ).astype(jnp.bfloat16)
            low_out[span, width:] = (grad_hidden * silu_gate).astype(jnp.bfloat16)
        for i in range(count):
            low = low_out[i * rows : (i + 1) * rows, :]
            total = None
            for j in range(pair_count):
                back = product(low, weights[j][...], 1, 1).astype(jnp.bfloat16)
                part = product(back, select_ref[:, j * depth : (j + 1) * depth], 1, 1)
                total = part if total is None else total + part
            back_outs[i][...] = total.astype(LINK)

    outs = [
        ((total_rows, select.shape[1]), jnp.bfloat16),
        ((total_rows, width), jnp.bfloat16),
        ((total_rows, both), jnp.bfloat16),
    ] + [((rows, features), LINK)] * count
    operands = list(normed_blocks) + list(cotangent_blocks) + [select]
    operands += list(pair_pieces) + list(down_pieces) + [order]
    results = kernel_call(body, outs, operands)
    return results[0], results[1], results[2], results[3:]


def split_products(left_side, right_blocks, first_rows):
    count = len(right_blocks)
    all_rows = left_side.shape[1]
    width = right_blocks[0].shape[1]
    step = right_blocks[0].shape[0]

    def body(*refs):
        left_ref = refs[0]
        outs = refs[1 + count :]
        for j, out in enumerate(outs):
            span = slice(0, first_rows) if j == 0 else slice(first_rows, all_rows)
            total = None
            for i in range(count):
                part = product(
                    left_ref[i * step : (i + 1) * step, span], refs[1 + i][...], 0, 0
                )
                total = part if total is None else total + part
            out[...] = total.astype(out.dtype)

    outs = [((first_rows, width), jnp.float32)]
    if first_rows < all_rows:
        outs.append(((all_rows - first_rows, width), LINK))
    return kernel_call(body, outs, [left_side] + list(right_blocks))


def block_products(left_side, down_pieces, count):
    rows = left_side.shape[0] // count
    width = down_pieces[0].shape[1]

    def body(*refs):
        down = jnp.concatenate([d[...] for d in refs[1 : 1 + len(down_pieces)]], axis=0)
        for i, out in enumerate(refs[1 + len(down_pieces) :]):
            part = product(refs[0][i * rows : (i + 1) * rows, :], down, 1, 0)
            out[...] = part.astype(out.dtype)

    outs = [((rows, width), jnp.float32 if i == 0 else LINK) for i in range(count)]
    return kernel_call(body, outs, [left_side] + list(down_pieces))


def local(
    hidden_in,
    positions,
    norm1_gain,
    q_weight,
    k_weight,
    v_weight,
    o_weight,
    norm2_gain,
    gate_weight,
    up_weight,
    down_weight,
    cotangent,
):
    tok_rows = hidden_in.shape[0]
    model_width = hidden_in.shape[1]
    device_count = lax.axis_size(AXIS)
    place = lax.axis_index(AXIS)
    member = (place >> TEAM_BITS[0]) & (TEAM - 1)
    outer_index = place >> LOW_BITS
    core = place & 1
    outer_bits = device_count.bit_length() - 1 - LOW_BITS
    top_shift = outer_bits - len(TEAM_BITS)
    window_span = (MAXLEN + tok_rows - 2) // tok_rows
    prefix = window_span * tok_rows
    q_width = q_weight.shape[0] * device_count // model_width
    k_width = k_weight.shape[0] * device_count // model_width
    ff_width = gate_weight.shape[0] * device_count // model_width
    team_width = ff_width // TEAM
    down_rows = ff_width // device_count
    masks = team_masks()

    in_plan = RowPlan(model_width)
    out_plan = RowPlan(q_width)
    paired = len(in_plan.last) > 1

    def both_cores(block):
        return [block, swap(block, 1)] if paired else [block]

    def pair_total(outs):
        return outs[0] + swap(outs[1], 1) if paired else outs[0]

    def distances(plan):
        return [t ^ o for t in plan.team for o in plan.outer_set]

    input_rows = hidden_in.astype(jnp.float32)
    scale_one = norm_scale(input_rows)
    normed_one = (input_rows * scale_one * norm1_gain[None, :]).astype(jnp.bfloat16)
    normed_pair = both_cores(normed_one)

    in_block = in_plan.padded(
        jnp.concatenate([in_plan.whole_rows(w, place) for w in (q_weight, k_weight, v_weight)], 1)
    )
    in_outer = jnp.concatenate(in_plan.outer_pieces(in_block))
    in_outer, o_flat, gate_flat, up_flat, down_flat = tie(
        in_outer, o_weight, gate_weight, up_weight, down_weight
    )
    weight_in = spread(in_outer, in_plan.team)
    select_in = in_plan.selector(place, distances(in_plan))
    out_outer = jnp.concatenate(
        out_plan.outer_pieces(out_plan.padded(out_plan.whole_rows(o_flat, place)))
    )
    select_out = out_plan.selector(place, distances(out_plan))

    def traded(i):
        outer, mem, c = i >> LOW_BITS, (i >> TEAM_BITS[0]) & (TEAM - 1), i & 1
        inner = outer & ((1 << top_shift) - 1)
        return (((mem << top_shift) | inner) << LOW_BITS) | ((outer >> top_shift) << TEAM_BITS[0]) | c

    trade_route = [(i, traded(i)) for i in range(device_count)]
    chunk_start = []
    for c in range(2):
        for o in in_plan.outer_set:
            o_from = outer_index ^ (o >> LOW_BITS)
            inner = o_from & ((1 << top_shift) - 1)
            chunk = (inner << LOW_BITS) | ((o_from >> top_shift) << TEAM_BITS[0]) | (core ^ c)
            chunk_start.append(chunk * down_rows)
    column = jnp.repeat(jnp.stack(chunk_start), down_rows) + jnp.tile(
        jnp.arange(down_rows, dtype=jnp.int32), len(chunk_start)
    )
    select_unit = (
        jnp.arange(team_width, dtype=jnp.int32)[:, None] == column[None, :]
    ).astype(jnp.bfloat16)

    def slabs(flat):
        whole = in_plan.whole_rows(flat, place)
        parts = jnp.concatenate(
            [whole[:, t * team_width : (t + 1) * team_width] for t in range(TEAM)]
        )
        return parts.reshape(TEAM, -1, team_width)

    gap = in_plan.pitch - in_plan.rows
    pair_slabs = jnp.pad(
        jnp.concatenate([slabs(gate_flat), slabs(up_flat)], axis=2), ((0, 0), (0, gap), (0, 0))
    )
    member_shift = [m >> TEAM_BITS[0] for m in in_plan.team]
    arrived = [
        swap(pick(pair_slabs, member ^ s), m) if m else pick(pair_slabs, member)
        for s, m in zip(member_shift, in_plan.team)
    ]
    pair_outer = in_plan.outer_pieces(jnp.concatenate(arrived))
    weight_pair = pair_outer + [swap(p, m) for m in in_plan.last[1:] for p in pair_outer]
    ff_distances = [c ^ o ^ t for c in in_plan.last for o in in_plan.outer_set for t in in_plan.team]
    select_ff = in_plan.selector(place, ff_distances)
    down_block = lax.ppermute(down_flat.reshape(down_rows, model_width), AXIS, trade_route)
    down_half = jnp.concatenate(in_plan.outer_pieces(down_block))
    weight_down = [down_half, swap(down_half, 1)]

    cosine, sine_table = rotary_tables(positions)
    projected_pair, placed_one = pair_project(normed_pair, select_in, weight_in)
    projected = pair_total(projected_pair)
    out_outer, cotangent_late, projected = tie(out_outer, cotangent, projected)
    weight_out = spread(out_outer, out_plan.team)
    rotated = rotate(projected[:, : q_width + k_width], cosine, sine_table).astype(jnp.bfloat16)
    query_low = rotated[:, :q_width]
    key_value = jnp.concatenate(
        [rotated[:, q_width:], projected[:, q_width + k_width :].astype(jnp.bfloat16)], axis=1
    )
    pieces = [passed_along(key_value, distance) for distance in range(window_span, 0, -1)]
    window = jnp.concatenate(pieces + [key_value], axis=0)
    cotangent_blocks = spread(cotangent_late, masks)
    key_window = window[:, :k_width]
    value_window = window[:, k_width:]
    attended_low, log_total = attend(query_low, key_window, value_window, positions, prefix)
    mixed_pair, placed_attended = pair_project(both_cores(attended_low), select_out, weight_out)
    mid_rows = input_rows + pair_total(mixed_pair)
    scale_two = norm_scale(mid_rows)
    normed_two = (mid_rows * scale_two * norm2_gain[None, :]).astype(jnp.bfloat16)

    normed_blocks = spread(normed_two, masks)
    placed_two, hidden_low, grad_low, back_blocks = feed_forward(
        normed_blocks, cotangent_blocks, select_ff, weight_pair, weight_down, select_unit
    )
    grad_normed_two = back_blocks[0].astype(jnp.float32)
    for block, mask in zip(back_blocks[1:], masks[1:]):
        grad_normed_two = grad_normed_two + swap(block, mask).astype(jnp.float32)

    low_blocks = [grad_low]
    pair_rows = placed_two.shape[1] // len(in_plan.last)
    pair_grads = split_products(placed_two, low_blocks, pair_rows)
    pair_arrived = [swap(g, m) for g, m in zip(pair_grads[1:], in_plan.last[1:])]
    down_grads = split_products(
        hidden_low, [jnp.concatenate(cotangent_blocks)], team_width // 2
    )
    down_arrived = [swap(down_grads[1], 1)]
    outer_group = 1 << len(in_plan.outer[-1])
    pair_own, *pair_blocks = reduce_split(pair_grads[0], pair_arrived, outer_group)
    down_own, *down_blocks = reduce_split(down_grads[0], down_arrived, outer_group)
    grad_mid_norm, grad_gain_two = norm_backward(mid_rows, scale_two, norm2_gain, grad_normed_two)
    grad_mid = cotangent.astype(jnp.float32) + grad_mid_norm
    grad_mid, pair_blocks, down_blocks, hidden_late = tie(
        grad_mid, pair_blocks, down_blocks, hidden_low
    )
    out_blocks = block_products(hidden_late, weight_down, TEAM)
    out_total = out_blocks[0]
    for block, mask in zip(out_blocks[1:], masks[1:]):
        out_total = out_total + swap(block, mask).astype(jnp.float32)
    block_out = (mid_rows + out_total).astype(jnp.bfloat16)

    pair_sum = in_plan.outer_sum(pair_own, pair_blocks)
    down_sum = in_plan.outer_sum(down_own, down_blocks)
    grad_down = lax.ppermute(down_sum.astype(LINK), AXIS, trade_route).astype(jnp.float32).reshape(-1)
    pair_blocks_t = pair_sum.reshape(len(in_plan.team), in_plan.pitch, 2 * team_width)
    returned = [
        swap(pair_blocks_t[i].astype(LINK), m) if m else pair_blocks_t[i].astype(LINK)
        for i, m in enumerate(in_plan.team)
    ]
    back_stack = jnp.stack(returned)[:, : in_plan.rows]
    natural = (back_stack[:, :, :team_width], back_stack[:, :, team_width:])

    def owned(grad_slabs):
        columns = []
        for t in range(TEAM):
            column_part = jnp.zeros_like(grad_slabs[0])
            for i, s in enumerate(member_shift):
                column_part = jnp.where((member ^ s) == t, grad_slabs[i], column_part)
            columns.append(column_part)
        return in_plan.own_share(
            jnp.concatenate(columns, axis=1).astype(jnp.float32), place
        )

    grad_gate = owned(natural[0])
    grad_up = owned(natural[1])

    grad_mid_low = grad_mid.astype(jnp.bfloat16)
    out_grads, attended_pair = pair_back(
        both_cores(grad_mid_low), placed_attended, select_out, weight_out
    )
    grad_attended_low = pair_total(attended_pair).astype(jnp.bfloat16)

    def weight_share(plan, grads):
        arrived_blocks = [swap(g, m) for g, m in zip(grads[1:], plan.team[1:])]
        own, *blocks = reduce_split(grads[0], arrived_blocks, 1 << len(plan.outer[-1]))
        return plan.outer_sum(own, blocks)[: plan.rows]

    grad_out = out_plan.own_share(weight_share(out_plan, out_grads), place)
    grad_query, grad_key_window, grad_value_window = attend_back(
        query_low,
        key_window,
        value_window,
        positions,
        prefix,
        log_total,
        attended_low,
        grad_attended_low,
    )
    grad_window = jnp.concatenate([grad_key_window, grad_value_window], axis=1)
    own_pair = grad_window[prefix:]
    for distance in range(1, window_span + 1):
        start_row = prefix - distance * tok_rows
        part = grad_window[start_row : start_row + tok_rows].astype(LINK)
        own_pair = own_pair + passed_along(part, -distance).astype(jnp.float32)
    turned_back = rotate(
        jnp.concatenate([grad_query, own_pair[:, :k_width]], axis=1), cosine, -sine_table
    )
    grad_projected = jnp.concatenate([turned_back, own_pair[:, k_width:]], axis=1).astype(
        jnp.bfloat16
    )
    in_grads, normed_grads = pair_back(
        both_cores(grad_projected), placed_one, select_in, weight_in
    )
    in_share = weight_share(in_plan, in_grads)
    grad_query_weight = in_plan.own_share(in_share[:, :q_width], place)
    grad_key_weight = in_plan.own_share(in_share[:, q_width : q_width + k_width], place)
    grad_value_weight = in_plan.own_share(in_share[:, q_width + k_width :], place)
    grad_normed_one = pair_total(normed_grads)
    grad_in_norm, grad_gain_one = norm_backward(input_rows, scale_one, norm1_gain, grad_normed_one)
    grad_in = (grad_mid + grad_in_norm).astype(jnp.bfloat16)
    gains = jnp.stack([grad_gain_one, grad_gain_two])
    for bit in range(device_count.bit_length() - 1):
        gains = gains + swap(gains, 1 << bit)
    return (
        block_out,
        grad_in,
        gains[0],
        grad_query_weight,
        grad_key_weight,
        grad_value_weight,
        grad_out,
        gains[1],
        grad_gate,
        grad_up,
        grad_down,
    )


def solution(mesh):
    placed = (
        P("fsdp", None),
        P("fsdp"),
        P(),
        P("fsdp"),
        P("fsdp"),
        P("fsdp"),
        P("fsdp"),
        P(),
        P("fsdp"),
        P("fsdp"),
        P("fsdp"),
        P("fsdp", None),
    )
    return jax.shard_map(
        local,
        mesh=mesh,
        in_specs=placed,
        out_specs=(
            P("fsdp", None),
            P("fsdp", None),
            P(),
            P("fsdp"),
            P("fsdp"),
            P("fsdp"),
            P("fsdp"),
            P(),
            P("fsdp"),
            P("fsdp"),
            P("fsdp"),
        ),
        check_vma=False,
    )
```

time: 452 us -> 427 us (0.945)
  local copies, waits for them, and re-layouts: 127 us -> 41.5 us
  Pallas kernels: 0 us -> 72.5 us
  starting transfers between devices: 84.5 us -> 127 us
  matrix products: 47 us -> 18.8 us
  other arithmetic: 45.6 us -> 31.1 us
  waiting for transfers between devices: 137 us -> 128 us
    pallas_call x0 -> x16, Pallas kernels: none -> 72.5 us  [kernel_call(): pl.pallas_call(body, out_shape=[jax.ShapeDtypeStruct(shape, dtype) for sh...]
    ppermute x59 -> x74, starting transfers between devices: 66.9 us -> 105 us  [swap(): return lax.ppermute(block, AXIS, [(i, i ^ mask) for i in range(size)])]
    dot_general x18 -> x0, matrix products: 35.3 us -> none  [the longest x7 12.8 us: forward_product(): return jnp.dot(left_side, weight, preferred_element_type=jnp.float32)]
    concatenate x11 -> x2, local copies, waits for them, and re-layouts: 23.1 us -> 0.11 us  [the longest x1 0.1 us: local(): jnp.concatenate([in_plan.whole_rows(w, place) for w in (q_weight, k_weigh...]
    another operation x22 -> x1, local copies, waits for them, and re-layouts: 22.3 us -> 0.08 us  [local(): jnp.stack(chunk_start)]
    ppermute x10 -> x1, local copies, waits for them, and re-layouts: 16.7 us -> 1.54 us  [swap(): return lax.ppermute(block, AXIS, [(i, i ^ mask) for i in range(size)])]
    another operation x16 -> x4, other arithmetic: 16.2 us -> 3.91 us  [the longest x6 7.61 us: in_order(): return jnp.stack(blocks)]
    slice x22 -> x6, local copies, waits for them, and re-layouts: 13 us -> 2.21 us  [the longest x1 1 us: local(): in_share[:, q_width + k_width:]]
  transfers between devices with their start and end apart: 67 -> 84, of which waited for: 22 -> 24; matrix products, arithmetic and copies ran while one was open for 39% -> 18% of each run, Pallas kernels for 0% -> 9%
where the time goes in v2:
time: 427 us; the launch traced here: 421 us
  waiting for transfers between devices  128 us (30%)
  starting transfers between devices  127 us (30%)
  Pallas kernels  72.5 us (17%)
  local copies, waits for them, and re-layouts  41.5 us (10%)
  other arithmetic  31.1 us (7%)
  matrix products  18.8 us (4%)
    ppermute x74, waiting for transfers between devices, swap(): return lax.ppermute(block, AXIS, [(i, i ^ mask) for i in range(size)])  121 us
    ppermute x74, starting transfers between devices, swap(): return lax.ppermute(block, AXIS, [(i, i ^ mask) for i in range(size)])  105 us
    pallas_call x16, Pallas kernels, kernel_call(): pl.pallas_call(body, out_shape=[jax.ShapeDtypeStruct(shape, dtype) for sh...  72.5 us
    ppermute x8, starting transfers between devices, passed_along(): return lax.ppermute(block, AXIS, route)  16.7 us
    unnamed x144, local copies, waits for them, and re-layouts  15 us
  transfers between devices with their start and end apart: 84, of which 24 were waited for; matrix products, arithmetic and copies ran while one was open for 18% of the time, Pallas kernels for 9%

profile of v2, /device:TPU:0, one launch (start us, length us, event | category | flops | bytes accessed | tf_op | source)
XLA Modules:
  0.0 420.5 jit_solution(3554780458080012352)
XLA Ops:
  32.8 4.6 %collective-permute-done.8.refs_5_.refs_6_ = bf16[128,1600]{1,0:T(8,128)(2,1)S(1)} collective-permute-done((bf16[128,1600]{1,0:T(8,128)(2,1)S(1)}, bf16[128,1600]{1,0:T(8,128)(2,1)S(1)}, u32[]{:S(2)}, u32[]{:S(2)}) %collective-permute-start.8) | collective-permute-done | bytes 409632 | tf_op jit(solution)/shard_map/ppermute | solution.py:27
  38.9 4.4 %shard_map.230 = (f32[128,1600]{1,0:T(8,128)}, f32[128,1600]{1,0:T(8,128)}, bf16[256,512]{1,0:T(8,128)(2,1)}) custom-call(bf16[128,960]{1,0:T(8,128)(2,1)} %copy-done.19, bf16[128,960]{1,0:T(8,128)(2,1)} %copy-done.45, bf16[960,512]{1,0:T(8,128)(2,1)} %fusion.6.refs_2_.refs_3_, bf16[128,1600]{1,0:T(8,128)(2,1)} %copy-done.5, bf16[128,1600]{1,0:T(8,128)(2,1)} %copy-done.12, ...), custom_call_target="tpu_custom_call" | custom-call | tf_op jit(solution)/shard_map/pallas_call | solution.py:183
  49.7 3.4 collective-permute-start.11
  56.2 3.6 collective-permute-start.26
  65.0 4.4 %collective-permute-start.13 = (bf16[128,640]{1,0:T(8,128)(2,1)S(1)}, bf16[128,640]{1,0:T(8,128)(2,1)S(1)}, u32[]{:S(2)}, u32[]{:S(2)}) collective-permute-start(bf16[128,640]{1,0:T(8,128)(2,1)S(1)} %pad_maximum_fusion.9), channel_id=1, source_target_pairs={{0,2},{1,3},{2,4},{3,5},{4,6},{5,7},{6,8},{7,9},{8,10},{9,11},{10,... | collective-permute-start | bytes 491528 | tf_op jit(solution)/shard_map/ppermute | solution.py:33
  71.0 6.9 %collective-permute-done.13 = bf16[128,640]{1,0:T(8,128)(2,1)S(1)} collective-permute-done((bf16[128,640]{1,0:T(8,128)(2,1)S(1)}, bf16[128,640]{1,0:T(8,128)(2,1)S(1)}, u32[]{:S(2)}, u32[]{:S(2)}) %collective-permute-start.13) | collective-permute-done | bytes 163872 | tf_op jit(solution)/shard_map/ppermute | solution.py:33
  88.1 3.7 convolution_convert_fusion
  97.9 5.2 %collective-permute-done.18.refs_6_.refs_7_ = bf16[128,960]{1,0:T(8,128)(2,1)S(1)} collective-permute-done((bf16[128,960]{1,0:T(8,128)(2,1)S(1)}, bf16[128,960]{1,0:T(8,128)(2,1)S(1)}, u32[]{:S(2)}, u32[]{:S(2)}) %collective-permute-start.18) | collective-permute-done | bytes 245792 | tf_op jit(solution)/shard_map/ppermute | solution.py:27
  106.5 3.8 shard_map.231
  117.7 21.5 %collective-permute-done.39 = bf16[80,960]{1,0:T(8,128)(2,1)S(1)} collective-permute-done((bf16[80,960]{1,0:T(8,128)(2,1)}, bf16[80,960]{1,0:T(8,128)(2,1)S(1)}, u32[]{:S(2)}, u32[]{:S(2)}) %collective-permute-start.39) | collective-permute-done | bytes 153632 | tf_op jit(solution)/shard_map/ppermute | solution.py:27
  147.5 4.1 collective-permute-done.23.refs_5_
  153.7 4.7 %collective-permute-done.24.refs_6_ = bf16[128,960]{1,0:T(8,128)(2,1)} collective-permute-done((bf16[128,960]{1,0:T(8,128)(2,1)S(1)}, bf16[128,960]{1,0:T(8,128)(2,1)}, u32[]{:S(2)}, u32[]{:S(2)}) %collective-permute-start.24) | collective-permute-done | bytes 245792 | tf_op jit(solution)/shard_map/ppermute | solution.py:27
  158.4 4.6 %collective-permute-done.20.refs_1_ = bf16[128,960]{1,0:T(8,128)(2,1)} collective-permute-done((bf16[128,960]{1,0:T(8,128)(2,1)S(1)}, bf16[128,960]{1,0:T(8,128)(2,1)}, u32[]{:S(2)}, u32[]{:S(2)}) %collective-permute-start.20) | collective-permute-done | bytes 245792 | tf_op jit(solution)/shard_map/ppermute | solution.py:27
  163.0 5.8 %collective-permute-done.21.refs_2_ = bf16[128,960]{1,0:T(8,128)(2,1)} collective-permute-done((bf16[128,960]{1,0:T(8,128)(2,1)S(1)}, bf16[128,960]{1,0:T(8,128)(2,1)}, u32[]{:S(2)}, u32[]{:S(2)}) %collective-permute-start.21) | collective-permute-done | bytes 245792 | tf_op jit(solution)/shard_map/ppermute | solution.py:27
  168.9 21.8 %shard_map.232 = (bf16[512,1024]{1,0:T(8,128)(2,1)}, bf16[512,640]{1,0:T(8,128)(2,1)}, bf16[512,1280]{1,0:T(8,128)(2,1)}, bf16[128,960]{1,0:T(8,128)(2,1)}, bf16...) custom-call(bf16[128,960]{1,0:T(8,128)(2,1)} %copy-done.21, ...), custom_call_target="tpu_custom_call" | custom-call | tf_op jit(solution)/shard_map/pallas_call | solution.py:183
  190.6 4.7 %shard_map.233 = (f32[512,1280]{1,0:T(8,128)}, bf16[512,1280]{1,0:T(8,128)(2,1)}) custom-call(bf16[512,1024]{1,0:T(8,128)(2,1)} %get-tuple-element.92.refs_0_, bf16[512,1280]{1,0:T(8,128)(2,1)} %get-tuple-element.93.refs_1_), custom_call_target="tpu_custom_call" | custom-call | tf_op jit(solution)/shard_map/pallas_call | solution.py:183
  202.3 3.3 shard_map.235
  205.6 5.3 %collective-permute-done.42 = bf16[128,960]{1,0:T(8,128)(2,1)S(1)} collective-permute-done((bf16[128,960]{1,0:T(8,128)(2,1)}, bf16[128,960]{1,0:T(8,128)(2,1)S(1)}, u32[]{:S(2)}, u32[]{:S(2)}) %collective-permute-start.42) | collective-permute-done | bytes 245792 | tf_op jit(solution)/shard_map/ppermute | solution.py:27
  217.0 3.3 shard_map.234
  222.7 6.2 %shard_map.238 = (f32[128,960]{1,0:T(8,128)}, bf16[128,960]{1,0:T(8,128)(2,1)}, bf16[128,960]{1,0:T(8,128)(2,1)}, bf16[128,960]{1,0:T(8,128)(2,1)}, f32[128,960]{1,0:T(8,128)}, /*index=5*/f32[128,960]{1,0:T(8,128)}) custom-call(bf16[128,960]{1,0:T(8,128)(2,1)} %copy-done.26, bf16[128,960]{1,0:T(8,128)(2,1)} %copy-done.50, ...), custom_call_target="tpu_custom_call" | custom-call | tf_op jit(solution)/shard_map/pallas_call | solution.py:183
  229.1 11.3 %collective-permute-start.80 = (bf16[80,960]{1,0:T(8,128)(2,1)S(1)}, bf16[80,960]{1,0:T(8,128)(2,1)S(1)}, u32[]{:S(2)}, u32[]{:S(2)}) collective-permute-start(bf16[80,960]{1,0:T(8,128)(2,1)S(1)} %copy-done.65), channel_id=1, source_target_pairs={{0,8},{1,9},{2,10},{3,11},{4,12},{5,13},{6,14},{7,15},{8,0},{9,1},... | collective-permute-start | bytes 460808 | tf_op jit(solution)/shard_map/ppermute | solution.py:27
  244.8 7.7 %collective-permute-done.80.refs_1_ = bf16[80,960]{1,0:T(8,128)(2,1)S(1)} collective-permute-done((bf16[80,960]{1,0:T(8,128)(2,1)S(1)}, bf16[80,960]{1,0:T(8,128)(2,1)S(1)}, u32[]{:S(2)}, u32[]{:S(2)}) %collective-permute-start.80) | collective-permute-done | bytes 153632 | tf_op jit(solution)/shard_map/ppermute | solution.py:27
  252.5 26.9 %collective-permute-done.81.refs_2_ = bf16[80,960]{1,0:T(8,128)(2,1)S(1)} collective-permute-done((bf16[80,960]{1,0:T(8,128)(2,1)}, bf16[80,960]{1,0:T(8,128)(2,1)S(1)}, u32[]{:S(2)}, u32[]{:S(2)}) %collective-permute-start.81) | collective-permute-done | bytes 153632 | tf_op jit(solution)/shard_map/ppermute | solution.py:27
  281.1 3.2 shard_map.237
  297.1 4.6 %fusion.31 = f32[5,64,640,1]{2,1,3,0:T(8,128)} fusion(bf16[128,5,3,64]{0,3,2,1:T(8,128)(2,1)S(1)} %bitcast.138, f32[5,640,128,3]{2,1,3,0:T(8,128)} %copy-done, f32[5,3,128]{2,1,0:T(4,128)S(1)} %log_add_fusion, pred[128,640]{0,1:T(8,128)(4,1)S(1)} %copy-done.33), kind=kOutput, calls=%fused_computation.99 | convolution fusion | flops 162201600 | bytes 6069760 | tf_op jit(solution)/shard_map/kgqs,qkgd->skd/dot_general | solution.py:167
  301.6 4.4 %fusion.2 = bf16[5,3,128,640]{2,3,1,0:T(8,128)(2,1)S(1)} fusion(f32[5,640,128,3]{2,1,3,0:T(8,128)} %copy-done, f32[5,3,128]{2,1,0:T(4,128)S(1)} %fusion.23, f32[5,3,128]{2,1,0:T(4,128)S(1)} %log_add_fusion, pred[128,640]{0,1:T(8,128)(4,1)} %fusion.30, bf16[640,5,64,1]{0,2,3,1:T(8,128)(2,1)} %bitcast.143, bf16[128,5,3,64]{0,3,2,1:T(8,128)(2,1)} %bitcast.139), kind=kOutput, calls=%fused_computation.3 | convolution fusion | flops 165888000 | bytes 8125440 | tf_op jit(solution)/shard_map/qkgd,skd->kgqs/dot_general | solution.py:154
  322.2 5.4 %collective-permute-start.47 = (bf16[128,960]{1,0:T(8,128)(2,1)}, bf16[128,960]{1,0:T(8,128)(2,1)S(1)}, u32[]{:S(2)}, u32[]{:S(2)}) collective-permute-start(bf16[128,960]{1,0:T(8,128)(2,1)} %get-tuple-element.108), channel_id=1, source_target_pairs={{0,4},{1,5},{2,6},{3,7},{4,0},{5,1},{6,2},{7,3},{8,12},{9,13},{10,... | collective-permute-start | bytes 737288 | tf_op jit(solution)/shard_map/ppermute | solution.py:27
  333.4 9.3 %collective-permute-start.77 = (bf16[32,1280]{1,0:T(8,128)(2,1)S(1)}, bf16[32,1280]{1,0:T(8,128)(2,1)S(1)}, u32[]{:S(2)}, u32[]{:S(2)}) collective-permute-start(bf16[32,1280]{1,0:T(8,128)(2,1)S(1)} %get-tuple-element.198), channel_id=1, source_target_pairs={{0,6},{1,7},{2,4},{3,5},{4,2},{5,3},{6,0},{7,1},{8,14},{9,15},{10,... | collective-permute-start | bytes 245768 | tf_op jit(solution)/shard_map/ppermute | solution.py:27
  342.8 5.7 %collective-permute-done.47 = bf16[128,960]{1,0:T(8,128)(2,1)S(1)} collective-permute-done((bf16[128,960]{1,0:T(8,128)(2,1)}, bf16[128,960]{1,0:T(8,128)(2,1)S(1)}, u32[]{:S(2)}, u32[]{:S(2)}) %collective-permute-start.47) | collective-permute-done | bytes 245792 | tf_op jit(solution)/shard_map/ppermute | solution.py:27
  356.6 7.0 %shard_map.239 = (f32[128,1600]{1,0:T(8,128)}, bf16[128,1600]{1,0:T(8,128)(2,1)}, bf16[128,1600]{1,0:T(8,128)(2,1)}, bf16[128,1600]{1,0:T(8,128)(2,1)}, f32[128,960]{1,0:T(8,128)}, /*index=5*/f32[128,960]{1,0:T(8,128)}) custom-call(bf16[128,1600]{1,0:T(8,128)(2,1)} %copy-done.15, bf16[128,1600]{1,0:T(8,128)(2,1)} %copy-done.38, ...), custom_call_target="tpu_custom_call" | custom-call | tf_op jit(solution)/shard_map/pallas_call | solution.py:183
  379.6 3.4 collective-permute-start.73
  389.6 7.3 %collective-permute-done.64.refs_3_ = bf16[128,1600]{1,0:T(8,128)(2,1)} collective-permute-done((bf16[128,1600]{1,0:T(8,128)(2,1)}, bf16[128,1600]{1,0:T(8,128)(2,1)}, u32[]{:S(2)}, u32[]{:S(2)}) %collective-permute-start.64) | collective-permute-done | bytes 409632 | tf_op jit(solution)/shard_map/ppermute | solution.py:27
  (415 shorter events, 197.1 us)
Async XLA Ops:
  19.1 18.2 %collective-permute-start.8 = (bf16[128,1600]{1,0:T(8,128)(2,1)S(1)}, bf16[128,1600]{1,0:T(8,128)(2,1)S(1)}, u32[]{:S(2)}, u32[]{:S(2)}) collective-permute-start(bf16[128,1600]{1,0:T(8,128)(2,1)S(1)} %pad_maximum_fusion.3.refs_3_.refs_4_), channel_id=1, source_target_pairs={{0,4},{1,5},{2,6},{3,7},{4,0},{5,1},{6,2},{7,3},{8,12},{9,13},{10,... | collective-permute-start | bytes 1228808 | tf_op jit(solution)/shard_map/ppermute | solution.py:27
  24.7 21.7 %collective-permute-start.3 = (bf16[32,960]{1,0:T(8,128)(2,1)S(1)}, bf16[32,960]{1,0:T(8,128)(2,1)}, u32[]{:S(2)}, u32[]{:S(2)}) collective-permute-start(bf16[32,960]{1,0:T(8,128)(2,1)S(1)} %pad.13), channel_id=1, source_target_pairs={{0,8},{1,9},{2,10},{3,11},{4,12},{5,13},{6,14},{7,15},{8,0},{9,1},... | collective-permute-start | bytes 184328 | tf_op jit(solution)/shard_map/ppermute | solution.py:27
  26.4 19.9 %collective-permute-start.4 = (bf16[32,960]{1,0:T(8,128)(2,1)S(1)}, bf16[32,960]{1,0:T(8,128)(2,1)}, u32[]{:S(2)}, u32[]{:S(2)}) collective-permute-start(bf16[32,960]{1,0:T(8,128)(2,1)S(1)} %pad.13), channel_id=1, source_target_pairs={{0,16},{1,17},{2,18},{3,19},{4,20},{5,21},{6,22},{7,23},{8,24},{9,... | collective-permute-start | bytes 184328 | tf_op jit(solution)/shard_map/ppermute | solution.py:27
  56.2 54.1 %collective-permute-start.26 = (bf16[32,1280]{1,0:T(8,128)(2,1)}, bf16[32,1280]{1,0:T(8,128)(2,1)}, u32[]{:S(2)}, u32[]{:S(2)}) collective-permute-start(bf16[32,1280]{1,0:T(8,128)(2,1)} %get-tuple-element.204), channel_id=1, source_target_pairs={{0,2},{1,3},{2,0},{3,1},{4,6},{5,7},{6,4},{7,5},{8,10},{9,11},{10,... | collective-permute-start | bytes 245768 | tf_op jit(solution)/shard_map/ppermute | solution.py:27
  59.7 50.5 %collective-permute-start.27 = (bf16[32,1280]{1,0:T(8,128)(2,1)}, bf16[32,1280]{1,0:T(8,128)(2,1)}, u32[]{:S(2)}, u32[]{:S(2)}) collective-permute-start(bf16[32,1280]{1,0:T(8,128)(2,1)} %get-tuple-element.203), channel_id=1, source_target_pairs={{0,4},{1,5},{2,6},{3,7},{4,0},{5,1},{6,2},{7,3},{8,12},{9,13},{10,... | collective-permute-start | bytes 245768 | tf_op jit(solution)/shard_map/ppermute | solution.py:27
  62.1 30.0 %collective-permute-start.36 = (bf16[80,960]{1,0:T(8,128)(2,1)}, bf16[80,960]{1,0:T(8,128)(2,1)}, u32[]{:S(2)}, u32[]{:S(2)}) collective-permute-start(bf16[80,960]{1,0:T(8,128)(2,1)} %reshape.456), channel_id=1, source_target_pairs={{0,0},{1,1},{2,8},{3,9},{4,16},{5,17},{6,24},{7,25},{8,2},{9,3},{1... | collective-permute-start | bytes 460808 | tf_op jit(solution)/shard_map/ppermute | solution.py:559
  77.8 17.3 %collective-permute-start.16 = (bf16[128,960]{1,0:T(8,128)(2,1)S(1)}, bf16[128,960]{1,0:T(8,128)(2,1)S(1)}, u32[]{:S(2)}, u32[]{:S(2)}) collective-permute-start(bf16[128,960]{1,0:T(8,128)(2,1)S(1)} %pad_maximum_fusion.8.refs_3_.refs_4_), channel_id=1, source_target_pairs={{0,2},{1,3},{2,0},{3,1},{4,6},{5,7},{6,4},{7,5},{8,10},{9,11},{10,... | collective-permute-start | bytes 737288 | tf_op jit(solution)/shard_map/ppermute | solution.py:27
  92.1 18.2 %collective-permute-start.28 = (bf16[32,1280]{1,0:T(8,128)(2,1)S(1)}, bf16[32,1280]{1,0:T(8,128)(2,1)S(1)}, u32[]{:S(2)}, u32[]{:S(2)}) collective-permute-start(bf16[32,1280]{1,0:T(8,128)(2,1)S(1)} %copy-done.58), channel_id=1, source_target_pairs={{0,6},{1,7},{2,4},{3,5},{4,2},{5,3},{6,0},{7,1},{8,14},{9,15},{10,... | collective-permute-start | bytes 245768 | tf_op jit(solution)/shard_map/ppermute | solution.py:27
  110.2 30.9 %collective-permute-start.19 = (f32[128,960]{1,0:T(8,128)}, f32[128,960]{1,0:T(8,128)S(1)}, u32[]{:S(2)}, u32[]{:S(2)}) collective-permute-start(f32[128,960]{1,0:T(8,128)} %get-tuple-element.83), channel_id=1, source_target_pairs={{0,1},{1,0},{2,3},{3,2},{4,5},{5,4},{6,7},{7,6},{8,9},{9,8},{10,11... | collective-permute-start | bytes 1474568 | tf_op jit(solution)/shard_map/ppermute | solution.py:27
  111.2 28.1 %collective-permute-start.29 = (bf16[128,1280]{1,0:T(8,128)(2,1)S(1)}, bf16[128,1280]{1,0:T(8,128)(2,1)}, u32[]{:S(2)}, u32[]{:S(2)}) collective-permute-start(bf16[128,1280]{1,0:T(8,128)(2,1)S(1)} %pad_maximum_fusion.6.refs_9_), channel_id=1, source_target_pairs={{0,8},{1,9},{2,10},{3,11},{4,12},{5,13},{6,14},{7,15},{8,0},{9,1},... | collective-permute-start | bytes 983048 | tf_op jit(solution)/shard_map/ppermute | solution.py:27
  111.4 29.2 %collective-permute-start.30 = (bf16[128,1280]{1,0:T(8,128)(2,1)S(1)}, bf16[128,1280]{1,0:T(8,128)(2,1)}, u32[]{:S(2)}, u32[]{:S(2)}) collective-permute-start(bf16[128,1280]{1,0:T(8,128)(2,1)S(1)} %pad_maximum_fusion.6.refs_9_), channel_id=1, source_target_pairs={{0,16},{1,17},{2,18},{3,19},{4,20},{5,21},{6,22},{7,23},{8,24},{9,... | collective-permute-start | bytes 983048 | tf_op jit(solution)/shard_map/ppermute | solution.py:27
  113.8 26.8 %collective-permute-start.31 = (bf16[128,1280]{1,0:T(8,128)(2,1)S(1)}, bf16[128,1280]{1,0:T(8,128)(2,1)}, u32[]{:S(2)}, u32[]{:S(2)}) collective-permute-start(bf16[128,1280]{1,0:T(8,128)(2,1)S(1)} %pad_maximum_fusion.6.refs_9_), channel_id=1, source_target_pairs={{0,24},{1,25},{2,26},{3,27},{4,28},{5,29},{6,30},{7,31},{8,16},{9,... | collective-permute-start | bytes 983048 | tf_op jit(solution)/shard_map/ppermute | solution.py:27
  116.7 22.5 %collective-permute-start.39 = (bf16[80,960]{1,0:T(8,128)(2,1)}, bf16[80,960]{1,0:T(8,128)(2,1)S(1)}, u32[]{:S(2)}, u32[]{:S(2)}) collective-permute-start(bf16[80,960]{1,0:T(8,128)(2,1)} %collective-permute-done.36), channel_id=1, source_target_pairs={{0,24},{1,25},{2,26},{3,27},{4,28},{5,29},{6,30},{7,31},{8,16},{9,... | collective-permute-start | bytes 460808 | tf_op jit(solution)/shard_map/ppermute | solution.py:27
  146.2 16.8 %collective-permute-start.20 = (bf16[128,960]{1,0:T(8,128)(2,1)S(1)}, bf16[128,960]{1,0:T(8,128)(2,1)}, u32[]{:S(2)}, u32[]{:S(2)}) collective-permute-start(bf16[128,960]{1,0:T(8,128)(2,1)S(1)} %multiply_convert_fusion.refs_0_), channel_id=1, source_target_pairs={{0,2},{1,3},{2,0},{3,1},{4,6},{5,7},{6,4},{7,5},{8,10},{9,11},{10,... | collective-permute-start | bytes 737288 | tf_op jit(solution)/shard_map/ppermute | solution.py:27
  147.0 21.8 %collective-permute-start.21 = (bf16[128,960]{1,0:T(8,128)(2,1)S(1)}, bf16[128,960]{1,0:T(8,128)(2,1)}, u32[]{:S(2)}, u32[]{:S(2)}) collective-permute-start(bf16[128,960]{1,0:T(8,128)(2,1)S(1)} %multiply_convert_fusion.refs_0_), channel_id=1, source_target_pairs={{0,4},{1,5},{2,6},{3,7},{4,0},{5,1},{6,2},{7,3},{8,12},{9,13},{10,... | collective-permute-start | bytes 737288 | tf_op jit(solution)/shard_map/ppermute | solution.py:27
  151.6 17.2 %collective-permute-start.22 = (bf16[128,960]{1,0:T(8,128)(2,1)S(1)}, bf16[128,960]{1,0:T(8,128)(2,1)}, u32[]{:S(2)}, u32[]{:S(2)}) collective-permute-start(bf16[128,960]{1,0:T(8,128)(2,1)S(1)} %multiply_convert_fusion.refs_0_), channel_id=1, source_target_pairs={{0,6},{1,7},{2,4},{3,5},{4,2},{5,3},{6,0},{7,1},{8,14},{9,15},{10,... | collective-permute-start | bytes 737288 | tf_op jit(solution)/shard_map/ppermute | solution.py:27
  195.3 20.6 %collective-permute-start.44 = (bf16[512,1280]{1,0:T(8,128)(2,1)}, bf16[512,1280]{1,0:T(8,128)(2,1)S(1)}, u32[]{:S(2)}, u32[]{:S(2)}) collective-permute-start(bf16[512,1280]{1,0:T(8,128)(2,1)} %get-tuple-element.95), channel_id=1, source_target_pairs={{0,1},{1,0},{2,3},{3,2},{4,5},{5,4},{6,7},{7,6},{8,9},{9,8},{10,11... | collective-permute-start | bytes 3932168 | tf_op jit(solution)/shard_map/ppermute | solution.py:27
  228.9 67.2 %collective-permute-start.50 = (f32[128,960]{1,0:T(8,128)}, f32[128,960]{1,0:T(8,128)S(1)}, u32[]{:S(2)}, u32[]{:S(2)}) collective-permute-start(f32[128,960]{1,0:T(8,128)} %get-tuple-element.113), channel_id=1, source_target_pairs={{0,1},{1,0},{2,3},{3,2},{4,5},{5,4},{6,7},{7,6},{8,9},{9,8},{10,11... | collective-permute-start | bytes 1474568 | tf_op jit(solution)/shard_map/ppermute | solution.py:27
  229.1 23.4 %collective-permute-start.80 = (bf16[80,960]{1,0:T(8,128)(2,1)S(1)}, bf16[80,960]{1,0:T(8,128)(2,1)S(1)}, u32[]{:S(2)}, u32[]{:S(2)}) collective-permute-start(bf16[80,960]{1,0:T(8,128)(2,1)S(1)} %copy-done.65), channel_id=1, source_target_pairs={{0,8},{1,9},{2,10},{3,11},{4,12},{5,13},{6,14},{7,15},{8,0},{9,1},... | collective-permute-start | bytes 460808 | tf_op jit(solution)/shard_map/ppermute | solution.py:27
  240.4 50.8 %collective-permute-start.74 = (bf16[128,1280]{1,0:T(8,128)(2,1)}, bf16[128,1280]{1,0:T(8,128)(2,1)S(1)}, u32[]{:S(2)}, u32[]{:S(2)}) collective-permute-start(bf16[128,1280]{1,0:T(8,128)(2,1)} %get-tuple-element.134), channel_id=1, source_target_pairs={{0,8},{1,9},{2,10},{3,11},{4,12},{5,13},{6,14},{7,15},{8,0},{9,1},... | collective-permute-start | bytes 983048 | tf_op jit(solution)/shard_map/ppermute | solution.py:27
  240.4 50.7 %collective-permute-start.75 = (bf16[128,1280]{1,0:T(8,128)(2,1)}, bf16[128,1280]{1,0:T(8,128)(2,1)}, u32[]{:S(2)}, u32[]{:S(2)}) collective-permute-start(bf16[128,1280]{1,0:T(8,128)(2,1)} %get-tuple-element.135), channel_id=1, source_target_pairs={{0,16},{1,17},{2,18},{3,19},{4,20},{5,21},{6,22},{7,23},{8,24},{9,... | collective-permute-start | bytes 983048 | tf_op jit(solution)/shard_map/ppermute | solution.py:27
  242.7 48.4 %collective-permute-start.76 = (bf16[128,1280]{1,0:T(8,128)(2,1)}, bf16[128,1280]{1,0:T(8,128)(2,1)}, u32[]{:S(2)}, u32[]{:S(2)}) collective-permute-start(bf16[128,1280]{1,0:T(8,128)(2,1)} %get-tuple-element.136), channel_id=1, source_target_pairs={{0,24},{1,25},{2,26},{3,27},{4,28},{5,29},{6,30},{7,31},{8,16},{9,... | collective-permute-start | bytes 983048 | tf_op jit(solution)/shard_map/ppermute | solution.py:27
  252.5 26.9 %collective-permute-start.81 = (bf16[80,960]{1,0:T(8,128)(2,1)}, bf16[80,960]{1,0:T(8,128)(2,1)S(1)}, u32[]{:S(2)}, u32[]{:S(2)}) collective-permute-start(bf16[80,960]{1,0:T(8,128)(2,1)} %get-tuple-element.139), channel_id=1, source_target_pairs={{0,16},{1,17},{2,18},{3,19},{4,20},{5,21},{6,22},{7,23},{8,24},{9,... | collective-permute-start | bytes 460808 | tf_op jit(solution)/shard_map/ppermute | solution.py:27
  286.8 46.6 %collective-permute-start.46 = (bf16[128,960]{1,0:T(8,128)(2,1)}, bf16[128,960]{1,0:T(8,128)(2,1)}, u32[]{:S(2)}, u32[]{:S(2)}) collective-permute-start(bf16[128,960]{1,0:T(8,128)(2,1)} %get-tuple-element.107), channel_id=1, source_target_pairs={{0,2},{1,3},{2,0},{3,1},{4,6},{5,7},{6,4},{7,5},{8,10},{9,11},{10,... | collective-permute-start | bytes 737288 | tf_op jit(solution)/shard_map/ppermute | solution.py:27
  322.2 26.2 %collective-permute-start.47 = (bf16[128,960]{1,0:T(8,128)(2,1)}, bf16[128,960]{1,0:T(8,128)(2,1)S(1)}, u32[]{:S(2)}, u32[]{:S(2)}) collective-permute-start(bf16[128,960]{1,0:T(8,128)(2,1)} %get-tuple-element.108), channel_id=1, source_target_pairs={{0,4},{1,5},{2,6},{3,7},{4,0},{5,1},{6,2},{7,3},{8,12},{9,13},{10,... | collective-permute-start | bytes 737288 | tf_op jit(solution)/shard_map/ppermute | solution.py:27
  327.6 23.2 %collective-permute-start.48 = (bf16[128,960]{1,0:T(8,128)(2,1)}, bf16[128,960]{1,0:T(8,128)(2,1)}, u32[]{:S(2)}, u32[]{:S(2)}) collective-permute-start(bf16[128,960]{1,0:T(8,128)(2,1)} %get-tuple-element.109), channel_id=1, source_target_pairs={{0,6},{1,7},{2,4},{3,5},{4,2},{5,3},{6,0},{7,1},{8,14},{9,15},{10,... | collective-permute-start | bytes 737288 | tf_op jit(solution)/shard_map/ppermute | solution.py:27
  329.7 24.7 %collective-permute-start.83 = (bf16[80,960]{1,0:T(8,128)(2,1)}, bf16[80,960]{1,0:T(8,128)(2,1)S(1)}, u32[]{:S(2)}, u32[]{:S(2)}) collective-permute-start(bf16[80,960]{1,0:T(8,128)(2,1)} %convert_element_type.163), channel_id=1, source_target_pairs={{0,0},{1,1},{2,8},{3,9},{4,16},{5,17},{6,24},{7,25},{8,2},{9,3},{1... | collective-permute-start | bytes 460808 | tf_op jit(solution)/shard_map/ppermute | solution.py:616
  333.3 22.6 %collective-permute-start.55 = (bf16[128,1600]{1,0:T(8,128)(2,1)S(1)}, bf16[128,1600]{1,0:T(8,128)(2,1)S(1)}, u32[]{:S(2)}, u32[]{:S(2)}) collective-permute-start(bf16[128,1600]{1,0:T(8,128)(2,1)S(1)} %pad_maximum_fusion.4.refs_0_), channel_id=1, source_target_pairs={{0,1},{1,0},{2,3},{3,2},{4,5},{5,4},{6,7},{7,6},{8,9},{9,8},{10,11... | collective-permute-start | bytes 1228808 | tf_op jit(solution)/shard_map/ppermute | solution.py:27
  333.4 30.2 %collective-permute-start.77 = (bf16[32,1280]{1,0:T(8,128)(2,1)S(1)}, bf16[32,1280]{1,0:T(8,128)(2,1)S(1)}, u32[]{:S(2)}, u32[]{:S(2)}) collective-permute-start(bf16[32,1280]{1,0:T(8,128)(2,1)S(1)} %get-tuple-element.198), channel_id=1, source_target_pairs={{0,6},{1,7},{2,4},{3,5},{4,2},{5,3},{6,0},{7,1},{8,14},{9,15},{10,... | collective-permute-start | bytes 245768 | tf_op jit(solution)/shard_map/ppermute | solution.py:27
  348.5 17.4 %collective-permute-start.78 = (bf16[32,1280]{1,0:T(8,128)(2,1)S(1)}, bf16[32,1280]{1,0:T(8,128)(2,1)S(1)}, u32[]{:S(2)}, u32[]{:S(2)}) collective-permute-start(bf16[32,1280]{1,0:T(8,128)(2,1)S(1)} %get-tuple-element.201), channel_id=1, source_target_pairs={{0,4},{1,5},{2,6},{3,7},{4,0},{5,1},{6,2},{7,3},{8,12},{9,13},{10,... | collective-permute-start | bytes 245768 | tf_op jit(solution)/shard_map/ppermute | solution.py:27
  378.9 18.1 %collective-permute-start.64 = (bf16[128,1600]{1,0:T(8,128)(2,1)}, bf16[128,1600]{1,0:T(8,128)(2,1)}, u32[]{:S(2)}, u32[]{:S(2)}) collective-permute-start(bf16[128,1600]{1,0:T(8,128)(2,1)} %get-tuple-element.120), channel_id=1, source_target_pairs={{0,6},{1,7},{2,4},{3,5},{4,2},{5,3},{6,0},{7,1},{8,14},{9,15},{10,... | collective-permute-start | bytes 1228808 | tf_op jit(solution)/shard_map/ppermute | solution.py:27
  383.4 20.3 %collective-permute-start.58 = (f32[2,960]{1,0:T(2,128)S(1)}, f32[2,960]{1,0:T(2,128)S(1)}, u32[]{:S(2)}, u32[]{:S(2)}) collective-permute-start(f32[2,960]{1,0:T(2,128)S(1)} %fusion.39), channel_id=1, source_target_pairs={{0,2},{1,3},{2,0},{3,1},{4,6},{5,7},{6,4},{7,5},{8,10},{9,11},{10,... | collective-permute-start | bytes 23048 | tf_op jit(solution)/shard_map/ppermute | solution.py:27
  (118 other events, 1618.6 us)

commit v3 on v2

v3 whole, which is shorter than its diff:
```python
import math

import jax
import jax.numpy as jnp
from jax import lax
from jax.experimental import pallas as pl
from jax.experimental.pallas import tpu as pltpu
from jax.sharding import PartitionSpec as P


KV_HEADS = 5
HEAD_DIM = 64
MAXLEN = 512


EPS = 1e-05
NEG_FILL = -1e30
AXIS = "fsdp"
TEAM_BITS = (1, 2)
TEAM = 1 << len(TEAM_BITS)
LOW_BITS = 3
ROW_TILE = 16
LINK = jnp.bfloat16
LANES = 128


def swap(block, mask):
    size = lax.axis_size(AXIS)
    return lax.ppermute(block, AXIS, [(i, i ^ mask) for i in range(size)])


def passed_along(block, distance):
    devices = range(lax.axis_size(AXIS))
    route = [(i - distance, i) for i in devices if i - distance in devices]
    return lax.ppermute(block, AXIS, route)


def pick(stack, index, axis=0):
    return lax.dynamic_index_in_dim(stack, index, axis, keepdims=False)


def team_masks():
    masks = []
    for member in range(TEAM):
        masks.append(sum(((member >> j) & 1) << bit for j, bit in enumerate(TEAM_BITS)))
    return masks


def rotary_tables(positions):
    half_width = HEAD_DIM // 2
    frequency = jnp.exp(
        jnp.arange(half_width, dtype=jnp.float32) * (-2.0 * math.log(10000.0) / HEAD_DIM)
    )
    angles = positions.astype(jnp.float32)[:, None] * frequency[None, :]
    repeats = LANES // half_width
    return (jnp.tile(jnp.cos(angles), (1, repeats)), jnp.tile(jnp.sin(angles), (1, repeats)))


def rotate(matrix, cosine, sine_table):
    half_width = HEAD_DIM // 2
    lane = lax.broadcasted_iota(jnp.int32, cosine.shape, 1)
    first_half = lane % HEAD_DIM < half_width
    signed = jnp.where(first_half, -sine_table, sine_table)
    turned = []
    for start in range(0, matrix.shape[1], LANES):
        part = matrix[:, start : start + LANES]
        other = jnp.where(
            first_half,
            pltpu.roll(part, LANES - half_width, 1),
            pltpu.roll(part, half_width, 1),
        )
        turned.append(part * cosine + other * signed)
    return jnp.concatenate(turned, axis=1)


def norm_scale(matrix):
    return lax.rsqrt(jnp.mean(matrix * matrix, axis=1, keepdims=True) + EPS)


def norm_backward(matrix, scale_rows, gain, grad_normed):
    unit_rows = matrix * scale_rows
    weighted = grad_normed * gain[None, :]
    grad_gain = jnp.sum(grad_normed * unit_rows, axis=0)
    grad_rows = scale_rows * (
        weighted - unit_rows * jnp.mean(weighted * unit_rows, axis=1, keepdims=True)
    )
    return (grad_rows, grad_gain)


def back_product(left_side, weight):
    return lax.dot_general(
        left_side, weight, (((1,), (1,)), ((), ())), preferred_element_type=jnp.float32
    )


def forward_product(left_side, weight):
    return jnp.dot(left_side, weight, preferred_element_type=jnp.float32)


def product(left_side, right_side, left_dim, right_dim):
    return lax.dot_general(
        left_side,
        right_side,
        (((left_dim,), (right_dim,)), ((), ())),
        preferred_element_type=jnp.float32,
    )


def kernel_call(body, outs, operands):
    return pl.pallas_call(
        body,
        out_shape=[jax.ShapeDtypeStruct(shape, dtype) for shape, dtype in outs],
        compiler_params=pltpu.CompilerParams(vmem_limit_bytes=60 * 1024 * 1024),
    )(*operands)


def tie(*values):
    return lax.optimization_barrier(values)


def bit_groups(bits):
    return [bits[i : i + 2] for i in range(0, len(bits), 2)]


def group_masks(bits):
    masks = [0]
    for bit in bits:
        masks += [m | (1 << bit) for m in masks]
    return masks


def spread(block, masks):
    return [block] + [swap(block, mask) for mask in masks[1:]]


def reduce_split(own, received, count):
    rows = own.shape[0] // count
    width = own.shape[1]

    def body(*refs):
        total = refs[0][...]
        for ref in refs[1 : 1 + len(received)]:
            total = total + ref[...].astype(jnp.float32)
        for i, out in enumerate(refs[1 + len(received) :]):
            out[...] = total[i * rows : (i + 1) * rows].astype(out.dtype)

    outs = [((rows, width), jnp.float32 if i == 0 else LINK) for i in range(count)]
    return kernel_call(body, outs, [own] + list(received))


class RowPlan:
    def __init__(self, row_total):
        size = lax.axis_size(AXIS)
        self.unit = size // math.gcd(size, row_total)
        self.rows = self.unit * row_total // size
        self.pitch = -(-self.rows // ROW_TILE) * ROW_TILE
        self.row_total = row_total
        unit_bits = self.unit.bit_length() - 1
        self.low = list(range(unit_bits))
        free = list(range(unit_bits, size.bit_length() - 1))
        self.outer = bit_groups([b for b in free if b >= LOW_BITS])
        self.team = group_masks([b for b in free if b in TEAM_BITS])
        self.last = group_masks([b for b in free if b < LOW_BITS and b not in TEAM_BITS])
        self.outer_set = group_masks([b for group in self.outer for b in group])

    def selector(self, base, distances):
        start = jnp.repeat(
            jnp.array([m // self.unit for m in distances], jnp.int32), self.pitch
        )
        within = jnp.tile(jnp.arange(self.pitch, dtype=jnp.int32), len(distances))
        row = ((base // self.unit) ^ start) * self.rows + within
        row = jnp.where(within < self.rows, row, -1)
        return (jnp.arange(self.row_total, dtype=jnp.int32)[:, None] == row[None, :]).astype(
            jnp.bfloat16
        )

    def whole_rows(self, flat, place):
        for bit in self.low:
            other = swap(flat, 1 << bit)
            high = (place >> bit) & 1
            flat = jnp.concatenate(
                [jnp.where(high == 1, other, flat), jnp.where(high == 1, flat, other)]
            )
        return flat.reshape(self.rows, -1)

    def own_share(self, block, place):
        flat = block.reshape(-1)
        for bit in reversed(self.low):
            high = (place >> bit) & 1
            halves = flat.reshape(2, -1)
            flat = pick(halves, high) + swap(
                pick(halves, 1 - high).astype(LINK), 1 << bit
            ).astype(jnp.float32)
        return flat

    def padded(self, block):
        return jnp.pad(block, ((0, self.pitch - self.rows), (0, 0)))

    def outer_pieces(self, block):
        pieces = [block]
        for group in self.outer:
            block = jnp.concatenate(pieces) if len(pieces) > 1 else pieces[0]
            pieces = spread(block, group_masks(group))
        return pieces

    def outer_send(self, blocks):
        return [swap(b, m) for b, m in zip(blocks, group_masks(self.outer[-1])[1:])]

    def outer_sum(self, own, arrived):
        for step, group in enumerate(reversed(self.outer)):
            following = self.outer[len(self.outer) - 2 - step] if step + 1 < len(self.outer) else []
            own, *blocks = reduce_split(own, arrived, 1 << len(following))
            arrived = [swap(b, m) for b, m in zip(blocks, group_masks(following)[1:])]
        return own


def pair_project(tokens, select, pieces):
    rows = tokens[0].shape[0]
    count = len(tokens)
    width = pieces[0].shape[1]
    depth = pieces[0].shape[0]

    def body(*refs):
        select_ref = refs[count]
        weights = refs[count + 1 : count + 1 + len(pieces)]
        outs = refs[count + 1 + len(pieces) :]
        tokens_all = jnp.concatenate([refs[i][...] for i in range(count)], axis=0)
        placed = product(tokens_all, select_ref[...], 1, 0).astype(jnp.bfloat16)
        outs[count][...] = placed
        total = product(placed[:, :depth], weights[0][...], 1, 0)
        for j in range(1, len(pieces)):
            total += product(placed[:, j * depth : (j + 1) * depth], weights[j][...], 1, 0)
        for i in range(count):
            outs[i][...] = total[i * rows : (i + 1) * rows]

    outs = [((rows, width), jnp.float32)] * count
    outs.append(((count * rows, select.shape[1]), jnp.bfloat16))
    results = kernel_call(body, outs, list(tokens) + [select] + list(pieces))
    return results[:count], results[count]


def pair_back(grads, placed, select, pieces):
    count = len(grads)
    rows = grads[0].shape[0]
    width = pieces[0].shape[1]
    depth = pieces[0].shape[0]
    features = select.shape[0]

    def body(*refs):
        placed_ref, select_ref = refs[count : count + 2]
        weights = refs[count + 2 : count + 2 + len(pieces)]
        outs = refs[count + 2 + len(pieces) :]
        grads_all = jnp.concatenate([refs[i][...] for i in range(count)], axis=0)
        total = None
        for j in range(len(pieces)):
            span = slice(j * depth, (j + 1) * depth)
            outs[j][...] = product(placed_ref[:, span], grads_all, 0, 0).astype(outs[j].dtype)
            back = product(grads_all, weights[j][...], 1, 1)
            high = back.astype(jnp.bfloat16)
            rest = (back - high.astype(jnp.float32)).astype(jnp.bfloat16)
            chosen = select_ref[:, span]
            part = product(high, chosen, 1, 1) + product(rest, chosen, 1, 1)
            total = part if total is None else total + part
        for i in range(count):
            outs[len(pieces) + i][...] = total[i * rows : (i + 1) * rows]

    outs = [((depth, width), jnp.float32 if j == 0 else LINK) for j in range(len(pieces))]
    outs += [((rows, features), jnp.float32)] * count
    results = kernel_call(body, outs, list(grads) + [placed, select] + list(pieces))
    return results[: len(pieces)], results[len(pieces) :]


def feed_forward(normed_blocks, cotangent_blocks, pair_pieces, down):
    count = len(normed_blocks)
    rows, features = normed_blocks[0].shape
    total_rows = count * rows
    depth, both = pair_pieces[0].shape
    width = both // 2
    pair_count = len(pair_pieces)

    def body(*refs):
        weights = refs[2 * count : 2 * count + pair_count]
        down_ref = refs[2 * count + pair_count]
        hidden_out, low_out, *back_outs = refs[2 * count + pair_count + 1 :]
        placed = jnp.concatenate([refs[i][...] for i in range(count)], axis=0)
        grads = jnp.concatenate([refs[count + i][...] for i in range(count)], axis=0)
        total = product(placed[:, :depth], weights[0][...], 1, 0)
        for j in range(1, pair_count):
            total += product(placed[:, j * depth : (j + 1) * depth], weights[j][...], 1, 0)
        gate_pre = total[:, :width]
        up_pre = total[:, width:]
        sigmoid_gate = 1.0 / (1.0 + jnp.exp(-gate_pre))
        silu_gate = gate_pre * sigmoid_gate
        hidden_out[...] = (silu_gate * up_pre).astype(jnp.bfloat16)
        grad_hidden = product(grads, down_ref[...], 1, 1)
        low_out[:, :width] = (
            grad_hidden * up_pre * sigmoid_gate * (1.0 + gate_pre * (1.0 - sigmoid_gate))
        ).astype(jnp.bfloat16)
        low_out[:, width:] = (grad_hidden * silu_gate).astype(jnp.bfloat16)
        low = low_out[...]
        for j in range(pair_count):
            back = product(low, weights[j][...], 1, 1)
            for i in range(count):
                part = back[i * rows : (i + 1) * rows]
                back_outs[i][:, j * depth : (j + 1) * depth] = part.astype(back_outs[i].dtype)

    outs = [((total_rows, width), jnp.bfloat16), ((total_rows, both), jnp.bfloat16)]
    outs += [((rows, features), jnp.float32 if i == 0 else LINK) for i in range(count)]
    operands = list(normed_blocks) + list(cotangent_blocks) + list(pair_pieces) + [down]
    results = kernel_call(body, outs, operands)
    return results[0], results[1], results[2:]


def split_products(left_blocks, right_side, first_rows):
    count = len(left_blocks)
    all_rows = left_blocks[0].shape[1]
    width = right_side.shape[1]

    def body(*refs):
        left = jnp.concatenate([refs[i][...] for i in range(count)], axis=0)
        right = refs[count][...]
        refs[count + 1][...] = product(left[:, :first_rows], right, 0, 0)
        if first_rows < all_rows:
            refs[count + 2][...] = product(left[:, first_rows:], right, 0, 0).astype(LINK)

    outs = [((first_rows, width), jnp.float32)]
    if first_rows < all_rows:
        outs.append(((all_rows - first_rows, width), LINK))
    return kernel_call(body, outs, list(left_blocks) + [right_side])


def turn(projected_parts, tables, q_width, k_width):
    rows = projected_parts[0].shape[0]
    count = len(projected_parts)

    def body(*refs):
        cosine_ref, sine_ref, query_out, pair_out = refs[count:]
        total = refs[0][...]
        for ref in refs[1:count]:
            total = total + ref[...]
        turned = rotate(total[:, : q_width + k_width], cosine_ref[...], sine_ref[...])
        query_out[...] = turned[:, :q_width].astype(jnp.bfloat16)
        pair_out[...] = jnp.concatenate(
            [turned[:, q_width:], total[:, q_width + k_width :]], axis=1
        ).astype(jnp.bfloat16)

    outs = [((rows, q_width), jnp.bfloat16), ((rows, 2 * k_width), jnp.bfloat16)]
    return kernel_call(body, outs, list(projected_parts) + list(tables))


def turn_back(grad_query, pair_parts, tables):
    rows, q_width = grad_query.shape
    k_width = pair_parts[0].shape[1] // 2

    def body(query_ref, cosine_ref, sine_ref, *refs):
        *parts, out = refs
        total = parts[0][...]
        for ref in parts[1:]:
            total = total + ref[...].astype(jnp.float32)
        heads = jnp.concatenate([query_ref[...], total[:, :k_width]], axis=1)
        turned = rotate(heads, cosine_ref[...], -sine_ref[...])
        out[...] = jnp.concatenate([turned, total[:, k_width:]], axis=1).astype(jnp.bfloat16)

    outs = [((rows, q_width + 2 * k_width), jnp.bfloat16)]
    return kernel_call(body, outs, [grad_query] + list(tables) + list(pair_parts))[0]


def allowed_pairs(position_ref, row_count, key_count, prefix):
    key_offset = lax.broadcasted_iota(jnp.int32, (row_count, key_count), 1) - prefix
    row_index = lax.broadcasted_iota(jnp.int32, (row_count, key_count), 0)
    return (key_offset <= row_index) & (key_offset >= row_index - position_ref[...])


def group_rows(ref, group, size):
    start = group * size * HEAD_DIM
    return jnp.concatenate(
        [ref[:, start + h * HEAD_DIM : start + (h + 1) * HEAD_DIM] for h in range(size)], axis=0
    )


def side_by_side(stacked, row_count):
    return [stacked[h * row_count : (h + 1) * row_count] for h in range(stacked.shape[0] // row_count)]


def attend(query_block, window_blocks, position_block, prefix):
    row_count, q_width = query_block.shape
    k_width = window_blocks[0].shape[1] // 2
    key_count = len(window_blocks) * row_count
    group_size = q_width // k_width

    def body(query_ref, position_ref, *refs):
        *window_refs, out_ref, log_ref = refs
        window = jnp.concatenate([ref[...] for ref in window_refs], axis=0)
        allowed = allowed_pairs(position_ref, row_count, key_count, prefix)
        fill = jnp.where(allowed, 0.0, NEG_FILL)
        fill = jnp.concatenate([fill] * group_size, axis=0)
        columns = []
        for g in range(KV_HEADS):
            span = slice(g * HEAD_DIM, (g + 1) * HEAD_DIM)
            scores = product(group_rows(query_ref, g, group_size), window[:, span], 1, 1)
            scores = jnp.where(fill < 0.0, NEG_FILL, scores * HEAD_DIM ** (-0.5))
            row_max = jnp.max(scores, axis=1, keepdims=True)
            total = jnp.sum(jnp.exp(scores - row_max), axis=1, keepdims=True)
            log_total = row_max + jnp.log(total)
            log_ref[g] = log_total
            prob_low = jnp.exp(scores - log_total).astype(jnp.bfloat16)
            values = window[:, k_width + g * HEAD_DIM : k_width + (g + 1) * HEAD_DIM]
            columns += side_by_side(product(prob_low, values, 1, 0), row_count)
        out_ref[...] = jnp.concatenate(columns, axis=1).astype(jnp.bfloat16)

    outs = [
        ((row_count, q_width), jnp.bfloat16),
        ((KV_HEADS, group_size * row_count, 1), jnp.float32),
    ]
    operands = [query_block, position_block[:, None]] + list(window_blocks)
    return kernel_call(body, outs, operands)


def attend_back(
    query_block, window_blocks, position_block, prefix, log_total, attended_block, grad_block
):
    row_count, q_width = query_block.shape
    k_width = window_blocks[0].shape[1] // 2
    count = len(window_blocks)
    key_count = count * row_count
    group_size = q_width // k_width

    def body(query_ref, position_ref, log_ref, attended_ref, grad_ref, *refs):
        window_refs = refs[:count]
        query_out, *window_outs = refs[count:]
        window = jnp.concatenate([ref[...] for ref in window_refs], axis=0)
        allowed = allowed_pairs(position_ref, row_count, key_count, prefix)
        fill = jnp.where(allowed, 0.0, NEG_FILL)
        fill = jnp.concatenate([fill] * group_size, axis=0)
        query_columns = []
        key_columns = []
        value_columns = []
        for g in range(KV_HEADS):
            span = slice(g * HEAD_DIM, (g + 1) * HEAD_DIM)
            keys = window[:, span]
            values = window[:, k_width + g * HEAD_DIM : k_width + (g + 1) * HEAD_DIM]
            queries = group_rows(query_ref, g, group_size)
            grads = group_rows(grad_ref, g, group_size)
            outputs = group_rows(attended_ref, g, group_size)
            scores = product(queries, keys, 1, 1)
            scores = jnp.where(fill < 0.0, NEG_FILL, scores * HEAD_DIM ** (-0.5))
            prob_full = jnp.exp(scores - log_ref[g])
            grad_prob = product(grads, values, 1, 1)
            delta_sum = jnp.sum(
                grads.astype(jnp.float32) * outputs.astype(jnp.float32), axis=1, keepdims=True
            )
            grad_score = (prob_full * (grad_prob - delta_sum) * HEAD_DIM ** (-0.5)).astype(
                jnp.bfloat16
            )
            query_columns += side_by_side(product(grad_score, keys, 1, 0), row_count)
            key_columns.append(product(grad_score, queries, 0, 0))
            value_columns.append(product(prob_full.astype(jnp.bfloat16), grads, 0, 0))
        query_out[...] = jnp.concatenate(query_columns, axis=1)
        total = jnp.concatenate(key_columns + value_columns, axis=1)
        for i, out in enumerate(window_outs):
            out[...] = total[i * row_count : (i + 1) * row_count].astype(out.dtype)

    outs = [((row_count, q_width), jnp.float32)]
    outs += [
        ((row_count, 2 * k_width), jnp.float32 if i == count - 1 else LINK) for i in range(count)
    ]
    operands = [query_block, position_block[:, None], log_total, attended_block, grad_block]
    results = kernel_call(body, outs, operands + list(window_blocks))
    return results[0], results[1:]


def starts_call(body, outs, starts, operands, scratch=()):
    return pl.pallas_call(
        body,
        out_shape=[jax.ShapeDtypeStruct(shape, dtype) for shape, dtype in outs],
        in_specs=[pl.BlockSpec(memory_space=pltpu.SMEM)]
        + [pl.BlockSpec(memory_space=pltpu.VMEM)] * len(operands),
        scratch_shapes=list(scratch),
        compiler_params=pltpu.CompilerParams(vmem_limit_bytes=60 * 1024 * 1024),
    )(starts, *operands)


def arrange_rows(pieces, starts, chunk, order):
    total = sum(piece.shape[0] for piece in pieces)
    width = pieces[0].shape[1]
    if chunk % ROW_TILE:
        stacked = jnp.concatenate(pieces)
        return forward_product(order, stacked).astype(jnp.bfloat16)
    per_piece = pieces[0].shape[0] // chunk

    def body(starts_ref, *refs):
        for j in range(total // chunk):
            at = pl.multiple_of(starts_ref[j], ROW_TILE)
            start = (j % per_piece) * chunk
            refs[-1][pl.ds(at, chunk), :] = refs[j // per_piece][start : start + chunk, :]

    return starts_call(body, [((total, width), jnp.bfloat16)], starts, list(pieces))[0]


def down_products(hidden, grads, starts, chunk, order):
    if chunk % ROW_TILE:
        placed = forward_product(hidden, order).astype(jnp.bfloat16)
        return split_products([placed], jnp.concatenate(grads), hidden.shape[1] // 2)
    half = hidden.shape[1] // 2
    width = grads[0].shape[1]
    count = len(grads)

    def body(starts_ref, *refs):
        hidden_ref = refs[0]
        own, other, total_ref = refs[1 + count :]
        right = jnp.concatenate([refs[1 + i][...] for i in range(count)], axis=0)
        total_ref[...] = product(hidden_ref[...], right, 0, 0)
        for j in range(2 * half // chunk):
            rows = total_ref[pl.ds(pl.multiple_of(starts_ref[j], ROW_TILE), chunk), :]
            target = own if j * chunk < half else other
            start = j * chunk % half
            target[start : start + chunk, :] = rows.astype(target.dtype)

    outs = [((half, width), jnp.float32), ((half, width), LINK)]
    scratch = [pltpu.VMEM((2 * half, width), jnp.float32)]
    return starts_call(body, outs, starts, [hidden] + list(grads), scratch)


def block_products(left_side, down, count):
    rows = left_side.shape[0] // count
    width = down.shape[1]

    def body(left_ref, down_ref, *outs):
        total = product(left_ref[...], down_ref[...], 1, 0)
        for i, out in enumerate(outs):
            out[...] = total[i * rows : (i + 1) * rows].astype(out.dtype)

    outs = [((rows, width), jnp.float32 if i == 0 else LINK) for i in range(count)]
    return kernel_call(body, outs, [left_side, down])


def local(
    hidden_in,
    positions,
    norm1_gain,
    q_weight,
    k_weight,
    v_weight,
    o_weight,
    norm2_gain,
    gate_weight,
    up_weight,
    down_weight,
    cotangent,
):
    tok_rows = hidden_in.shape[0]
    model_width = hidden_in.shape[1]
    device_count = lax.axis_size(AXIS)
    place = lax.axis_index(AXIS)
    member = (place >> TEAM_BITS[0]) & (TEAM - 1)
    outer_index = place >> LOW_BITS
    core = place & 1
    outer_bits = device_count.bit_length() - 1 - LOW_BITS
    top_shift = outer_bits - len(TEAM_BITS)
    window_span = (MAXLEN + tok_rows - 2) // tok_rows
    prefix = window_span * tok_rows
    q_width = q_weight.shape[0] * device_count // model_width
    k_width = k_weight.shape[0] * device_count // model_width
    ff_width = gate_weight.shape[0] * device_count // model_width
    team_width = ff_width // TEAM
    down_rows = ff_width // device_count
    masks = team_masks()

    in_plan = RowPlan(model_width)
    out_plan = RowPlan(q_width)
    paired = len(in_plan.last) > 1

    def both_cores(block):
        return [block, swap(block, 1)] if paired else [block]

    def pair_total(outs):
        return outs[0] + swap(outs[1], 1) if paired else outs[0]

    def distances(plan):
        return [t ^ o for t in plan.team for o in plan.outer_set]

    input_rows = hidden_in.astype(jnp.float32)
    scale_one = norm_scale(input_rows)
    normed_one = (input_rows * scale_one * norm1_gain[None, :]).astype(jnp.bfloat16)
    normed_pair = both_cores(normed_one)

    in_block = in_plan.padded(
        jnp.concatenate([in_plan.whole_rows(w, place) for w in (q_weight, k_weight, v_weight)], 1)
    )
    in_outer = jnp.concatenate(in_plan.outer_pieces(in_block))
    select_in = in_plan.selector(place, distances(in_plan))
    select_out = out_plan.selector(place, distances(out_plan))

    def traded(i):
        outer, mem, c = i >> LOW_BITS, (i >> TEAM_BITS[0]) & (TEAM - 1), i & 1
        inner = outer & ((1 << top_shift) - 1)
        return (((mem << top_shift) | inner) << LOW_BITS) | ((outer >> top_shift) << TEAM_BITS[0]) | c

    trade_route = [(i, traded(i)) for i in range(device_count)]
    chunk_start = []
    for c in range(2):
        for o in in_plan.outer_set:
            o_from = outer_index ^ (o >> LOW_BITS)
            inner = o_from & ((1 << top_shift) - 1)
            chunk = (inner << LOW_BITS) | ((o_from >> top_shift) << TEAM_BITS[0]) | (core ^ c)
            chunk_start.append(chunk * down_rows)
    column = jnp.repeat(jnp.stack(chunk_start), down_rows) + jnp.tile(
        jnp.arange(down_rows, dtype=jnp.int32), len(chunk_start)
    )
    unit_starts = jnp.stack(chunk_start).astype(jnp.int32)
    select_unit = (
        jnp.arange(team_width, dtype=jnp.int32)[:, None] == column[None, :]
    ).astype(jnp.bfloat16)

    def slabs(flat):
        whole = in_plan.whole_rows(flat, place)
        parts = jnp.concatenate(
            [whole[:, t * team_width : (t + 1) * team_width] for t in range(TEAM)]
        )
        return parts.reshape(TEAM, -1, team_width)

    gap = in_plan.pitch - in_plan.rows
    pair_slabs = jnp.pad(
        jnp.concatenate([slabs(gate_weight), slabs(up_weight)], axis=2), ((0, 0), (0, gap), (0, 0))
    )
    member_shift = [m >> TEAM_BITS[0] for m in in_plan.team]
    arrived = [
        swap(pick(pair_slabs, member ^ s), m) if m else pick(pair_slabs, member)
        for s, m in zip(member_shift, in_plan.team)
    ]
    team_index = sum(
        ((place >> (m.bit_length() - 1)) & 1) << i
        for i, m in enumerate(m for m in in_plan.team if m & (m - 1) == 0 and m)
    )
    arrived = jnp.stack(arrived)
    pair_block = jnp.concatenate(
        [pick(arrived, team_index ^ i) for i in range(len(in_plan.team))]
    )
    down_block = lax.ppermute(down_weight.reshape(down_rows, model_width), AXIS, trade_route)
    _, pair_block, down_block, o_flat = tie(in_outer, pair_block, down_block, o_weight)
    weight_in = spread(in_outer, in_plan.team)
    out_pieces = out_plan.outer_pieces(out_plan.padded(out_plan.whole_rows(o_flat, place)))
    pair_outer = in_plan.outer_pieces(pair_block)
    down_outer = in_plan.outer_pieces(down_block)
    out_outer = jnp.concatenate(out_pieces)
    weight_pair = pair_outer + [swap(p, m) for m in in_plan.last[1:] for p in pair_outer]
    ff_distances = [c ^ o ^ t for c in in_plan.last for o in in_plan.outer_set for t in in_plan.team]
    select_ff = in_plan.selector(place & ~in_plan.team[-1], ff_distances)
    weight_down = arrange_rows(
        down_outer + [swap(piece, 1) for piece in down_outer], unit_starts, down_rows, select_unit
    )

    tables = rotary_tables(positions)
    projected_pair, placed_one = pair_project(normed_pair, select_in, weight_in)
    projected_parts = list(projected_pair[:1]) + [swap(part, 1) for part in projected_pair[1:]]
    out_outer, cotangent_late, _ = tie(out_outer, cotangent, projected_parts)
    weight_out = spread(out_outer, out_plan.team)
    query_low, key_value = turn(projected_parts, tables, q_width, k_width)
    pieces = [passed_along(key_value, distance) for distance in range(window_span, 0, -1)]
    cotangent_blocks = spread(cotangent_late, masks)
    window_blocks = pieces + [key_value]
    attended_low, log_total = attend(query_low, window_blocks, positions, prefix)
    mixed_pair, placed_attended = pair_project(both_cores(attended_low), select_out, weight_out)
    mid_rows = input_rows + pair_total(mixed_pair)
    scale_two = norm_scale(mid_rows)
    normed_two = (mid_rows * scale_two * norm2_gain[None, :]).astype(jnp.bfloat16)

    placed_two = forward_product(normed_two, select_ff).astype(jnp.bfloat16)
    normed_blocks = spread(placed_two, masks)
    hidden_low, grad_low, back_blocks = feed_forward(
        normed_blocks, cotangent_blocks, weight_pair, weight_down
    )
    back_total = back_blocks[0]
    for block, mask in zip(back_blocks[1:], masks[1:]):
        back_total = back_total + swap(block, mask).astype(jnp.float32)
    back_high = lax.reduce_precision(back_total, 8, 7)
    grad_normed_two = back_product(back_high.astype(jnp.bfloat16), select_ff) + back_product(
        (back_total - back_high).astype(jnp.bfloat16), select_ff
    )

    pair_rows = placed_two.shape[1] // len(in_plan.last)
    pair_grads = split_products(normed_blocks, grad_low, pair_rows)
    pair_arrived = [swap(g, m) for g, m in zip(pair_grads[1:], in_plan.last[1:])]
    down_grads = down_products(
        hidden_low, cotangent_blocks, unit_starts, down_rows, select_unit
    )
    down_arrived = [swap(down_grads[1], 1)]
    outer_group = 1 << len(in_plan.outer[-1])
    pair_own, *pair_blocks = reduce_split(pair_grads[0], pair_arrived, outer_group)
    down_own, *down_blocks = reduce_split(down_grads[0], down_arrived, outer_group)
    pair_sent = in_plan.outer_send(pair_blocks)
    down_sent = in_plan.outer_send(down_blocks)
    grad_mid_norm, grad_gain_two = norm_backward(mid_rows, scale_two, norm2_gain, grad_normed_two)
    grad_mid = cotangent.astype(jnp.float32) + grad_mid_norm
    grad_mid_low = grad_mid.astype(jnp.bfloat16)
    grad_mid_pair = both_cores(grad_mid_low)
    out_grads, attended_pair = pair_back(
        grad_mid_pair, placed_attended, select_out, weight_out
    )
    grad_attended_low = pair_total(attended_pair).astype(jnp.bfloat16)

    out_arrived = [swap(g, m) for g, m in zip(out_grads[1:], out_plan.team[1:])]
    grad_query, grad_windows = attend_back(
        query_low, window_blocks, positions, prefix, log_total, attended_low, grad_attended_low
    )
    pair_parts = [grad_windows[-1]]
    for distance in range(1, window_span + 1):
        pair_parts.append(passed_along(grad_windows[window_span - distance], -distance))
    hidden_late, _ = tie(hidden_low, grad_query)
    out_blocks = block_products(hidden_late, weight_down, TEAM)
    out_total = out_blocks[0]
    for block, mask in zip(out_blocks[1:], masks[1:]):
        out_total = out_total + swap(block, mask).astype(jnp.float32)
    block_out = (mid_rows + out_total).astype(jnp.bfloat16)
    grad_projected = turn_back(grad_query, pair_parts, tables)
    in_grads, normed_grads = pair_back(
        both_cores(grad_projected), placed_one, select_in, weight_in
    )
    in_arrived = [swap(g, m) for g, m in zip(in_grads[1:], in_plan.team[1:])]
    pair_sent, down_sent, out_arrived, _ = tie(pair_sent, down_sent, out_arrived, in_grads[0])
    pair_sum = in_plan.outer_sum(pair_own, pair_sent)
    down_sum = in_plan.outer_sum(down_own, down_sent)
    grad_down = lax.ppermute(down_sum.astype(LINK), AXIS, trade_route).astype(jnp.float32).reshape(-1)
    pair_blocks_t = pair_sum.reshape(len(in_plan.team), in_plan.pitch, 2 * team_width)
    pair_low = pair_blocks_t.astype(LINK)
    returned = [
        swap(pick(pair_low, team_index ^ i), m) if m else pick(pair_low, team_index)
        for i, m in enumerate(in_plan.team)
    ]
    back_stack = jnp.stack(returned)[:, : in_plan.rows]
    natural = (back_stack[:, :, :team_width], back_stack[:, :, team_width:])

    def owned(grad_slabs):
        columns = []
        for t in range(TEAM):
            column_part = jnp.zeros_like(grad_slabs[0])
            for i, s in enumerate(member_shift):
                column_part = jnp.where((member ^ s) == t, grad_slabs[i], column_part)
            columns.append(column_part)
        return in_plan.own_share(
            jnp.concatenate(columns, axis=1).astype(jnp.float32), place
        )

    grad_gate = owned(natural[0])
    grad_up = owned(natural[1])

    def weight_share(plan, own, arrived_blocks):
        own, *blocks = reduce_split(own, arrived_blocks, 1 << len(plan.outer[-1]))
        return plan.outer_sum(own, plan.outer_send(blocks))[: plan.rows]

    out_share = weight_share(out_plan, out_grads[0], out_arrived)
    grad_out = out_plan.own_share(out_share, place)
    in_share = weight_share(in_plan, in_grads[0], in_arrived)
    grad_query_weight = in_plan.own_share(in_share[:, :q_width], place)
    grad_key_weight = in_plan.own_share(in_share[:, q_width : q_width + k_width], place)
    grad_value_weight = in_plan.own_share(in_share[:, q_width + k_width :], place)
    grad_normed_one = pair_total(normed_grads)
    grad_in_norm, grad_gain_one = norm_backward(input_rows, scale_one, norm1_gain, grad_normed_one)
    grad_in = (grad_mid + grad_in_norm).astype(jnp.bfloat16)
    gains = jnp.stack([grad_gain_one, grad_gain_two])
    for bit in range(device_count.bit_length() - 1):
        gains = gains + swap(gains, 1 << bit)
    return (
        block_out,
        grad_in,
        gains[0],
        grad_query_weight,
        grad_key_weight,
        grad_value_weight,
        grad_out,
        gains[1],
        grad_gate,
        grad_up,
        grad_down,
    )


def solution(mesh):
    placed = (
        P("fsdp", None),
        P("fsdp"),
        P(),
        P("fsdp"),
        P("fsdp"),
        P("fsdp"),
        P("fsdp"),
        P(),
        P("fsdp"),
        P("fsdp"),
        P("fsdp"),
        P("fsdp", None),
    )
    return jax.shard_map(
        local,
        mesh=mesh,
        in_specs=placed,
        out_specs=(
            P("fsdp", None),
            P("fsdp", None),
            P(),
            P("fsdp"),
            P("fsdp"),
            P("fsdp"),
            P("fsdp"),
            P(),
            P("fsdp"),
            P("fsdp"),
            P("fsdp"),
        ),
        check_vma=False,
    )
```

time: 427 us -> 391 us (0.916)
  other arithmetic: 31.1 us -> 13.9 us
  matrix products: 18.8 us -> 4.1 us
  Pallas kernels: 72.5 us -> 83.1 us
  local copies, waits for them, and re-layouts: 41.5 us -> 31.7 us
    dot_general x6 -> x3, matrix products: 18.8 us -> 4.1 us  [the longest x2 3.2 us: back_product(): lax.dot_general(left_side, weight, (((1,), (1,)), ((), ())), preferred_el...]
    pallas_call x0 -> x2, Pallas kernels: none -> 6.25 us  [starts_call(): pl.pallas_call(body, out_shape=[jax.ShapeDtypeStruct(shape, dtype) for sh...]
    reshape x4 -> x1, local copies, waits for them, and re-layouts: 5.9 us -> 0.16 us  [local(): down_weight.reshape(down_rows, model_width)]
    concatenate x10 -> x3, other arithmetic: 5.61 us -> 0.08 us  [the longest x1 0.03 us: local(): jnp.concatenate([slabs(gate_weight), slabs(up_weight)], axis=2)]
    unnamed x144, local copies, waits for them, and re-layouts: 15 us -> 10.4 us
    pallas_call x16 -> x19, Pallas kernels: 72.5 us -> 76.9 us  [kernel_call(): pl.pallas_call(body, out_shape=[jax.ShapeDtypeStruct(shape, dtype) for sh...]
    ppermute x74 -> x77, waiting for transfers between devices: 121 us -> 119 us  [swap(): return lax.ppermute(block, AXIS, [(i, i ^ mask) for i in range(size)])]
    ppermute x74 -> x77, starting transfers between devices: 105 us -> 105 us  [swap(): return lax.ppermute(block, AXIS, [(i, i ^ mask) for i in range(size)])]
  transfers between devices with their start and end apart: 84 -> 87, of which waited for: 24 -> 22; matrix products, arithmetic and copies ran while one was open for 18% -> 9% of each run, Pallas kernels for 9% -> 17%
where the time goes in v3:
time: 391 us; the launch traced here: 385 us
  starting transfers between devices  126 us (32%)
  waiting for transfers between devices  124 us (32%)
  Pallas kernels  83.1 us (21%)
  local copies, waits for them, and re-layouts  31.7 us (8%)
  other arithmetic  13.9 us (4%)
  matrix products  4.1 us (1%)
    ppermute x77, waiting for transfers between devices, swap(): return lax.ppermute(block, AXIS, [(i, i ^ mask) for i in range(size)])  119 us
    ppermute x77, starting transfers between devices, swap(): return lax.ppermute(block, AXIS, [(i, i ^ mask) for i in range(size)])  105 us
    pallas_call x19, Pallas kernels, kernel_call(): pl.pallas_call(body, out_shape=[jax.ShapeDtypeStruct(shape, dtype) for sh...  76.9 us
    ppermute x8, starting transfers between devices, passed_along(): return lax.ppermute(block, AXIS, route)  17.5 us
    unnamed x144, local copies, waits for them, and re-layouts  10.4 us
  transfers between devices with their start and end apart: 87, of which 22 were waited for; matrix products, arithmetic and copies ran while one was open for 9% of the time, Pallas kernels for 17%

profile of v3, /device:TPU:0, one launch (start us, length us, event | category | flops | bytes accessed | tf_op | source)
XLA Modules:
  0.0 384.9 jit_solution(6017822091380241894)
XLA Ops:
  3.4 5.1 %collective-permute-start.3 = (bf16[32,1600]{1,0:T(8,128)(2,1)S(1)}, bf16[32,1600]{1,0:T(8,128)(2,1)S(1)}, u32[]{:S(2)}, u32[]{:S(2)}) collective-permute-start(bf16[32,1600]{1,0:T(8,128)(2,1)S(1)} %pad.12), channel_id=1, source_target_pairs={{0,24},{1,25},{2,26},{3,27},{4,28},{5,29},{6,30},{7,31},{8,16},{9,... | collective-permute-start | bytes 307208 | tf_op jit(solution)/shard_map/ppermute | solution.py:29
  24.4 5.9 %collective-permute-done.4.refs_4_.refs_5_ = bf16[128,1600]{1,0:T(8,128)(2,1)S(1)} collective-permute-done((bf16[128,1600]{1,0:T(8,128)(2,1)S(1)}, bf16[128,1600]{1,0:T(8,128)(2,1)S(1)}, u32[]{:S(2)}, u32[]{:S(2)}) %collective-permute-start.4) | collective-permute-done | bytes 409632 | tf_op jit(solution)/shard_map/ppermute | solution.py:29
  31.8 8.7 %collective-permute-done.5.refs_5_.refs_6_ = bf16[128,1600]{1,0:T(8,128)(2,1)S(1)} collective-permute-done((bf16[128,1600]{1,0:T(8,128)(2,1)S(1)}, bf16[128,1600]{1,0:T(8,128)(2,1)S(1)}, u32[]{:S(2)}, u32[]{:S(2)}) %collective-permute-start.5) | collective-permute-done | bytes 409632 | tf_op jit(solution)/shard_map/ppermute | solution.py:29
  42.7 4.5 %shard_map.230 = (f32[128,1600]{1,0:T(8,128)}, f32[128,1600]{1,0:T(8,128)}, bf16[256,512]{1,0:T(8,128)(2,1)}) custom-call(bf16[128,960]{1,0:T(8,128)(2,1)} %copy-done.16, bf16[128,960]{1,0:T(8,128)(2,1)} %copy-done.38, bf16[960,512]{1,0:T(8,128)(2,1)} %fusion.6.refs_2_.refs_3_, bf16[128,1600]{1,0:T(8,128)(2,1)} %copy-done, bf16[128,1600]{1,0:T(8,128)(2,1)} %copy-done.4, ...), custom_call_target="tpu_custom_call" | custom-call | tf_op jit(solution)/shard_map/pallas_call | solution.py:110
  50.6 4.3 %collective-permute-start.19 = (bf16[32,960]{1,0:T(8,128)(2,1)S(1)}, bf16[32,960]{1,0:T(8,128)(2,1)S(1)}, u32[]{:S(2)}, u32[]{:S(2)}) collective-permute-start(bf16[32,960]{1,0:T(8,128)(2,1)S(1)} %pad.14), channel_id=1, source_target_pairs={{0,24},{1,25},{2,26},{3,27},{4,28},{5,29},{6,30},{7,31},{8,16},{9,... | collective-permute-start | bytes 184328 | tf_op jit(solution)/shard_map/ppermute | solution.py:29
  62.2 4.9 %collective-permute-start.8 = (bf16[128,640]{1,0:T(8,128)(2,1)}, bf16[128,640]{1,0:T(8,128)(2,1)S(1)}, u32[]{:S(2)}, u32[]{:S(2)}) collective-permute-start(bf16[128,640]{1,0:T(8,128)(2,1)} %get-tuple-element.87.refs_4_), channel_id=1, source_target_pairs={{0,4},{1,5},{2,6},{3,7},{4,8},{5,9},{6,10},{7,11},{8,12},{9,13},{1... | collective-permute-start | bytes 491528 | tf_op jit(solution)/shard_map/ppermute | solution.py:35
  68.6 3.1 collective-permute-start.10
  80.2 5.7 %shard_map.232 = (bf16[128,960]{1,0:T(8,128)(2,1)}, f32[5,384,1]{2,1,0:T(8,128)}) custom-call(bf16[128,960]{1,0:T(8,128)(2,1)} %get-tuple-element.86.query_ref, s32[128,1]{1,0:T(8,128)} %copy.61.position_ref, bf16[128,640]{1,0:T(8,128)(2,1)} %copy-done.23, bf16[128,640]{1,0:T(8,128)(2,1)} %copy-done.24, bf16[128,640]{1,0:T(8,128)(2,1)} %copy-done.25, ...), custom_call_target="tpu_custom_call" | custom-call | tf_op jit(solution)/shard_map/pallas_call | solution.py:110
  86.0 4.9 %collective-permute-done.21.refs_5_.refs_6_ = bf16[128,960]{1,0:T(8,128)(2,1)S(1)} collective-permute-done((bf16[128,960]{1,0:T(8,128)(2,1)S(1)}, bf16[128,960]{1,0:T(8,128)(2,1)S(1)}, u32[]{:S(2)}, u32[]{:S(2)}) %collective-permute-start.21) | collective-permute-done | bytes 245792 | tf_op jit(solution)/shard_map/ppermute | solution.py:29
  93.2 3.8 shard_map.233
  103.0 4.5 %collective-permute-done.37.refs_1_ = bf16[80,960]{1,0:T(8,128)(2,1)S(1)} collective-permute-done((bf16[80,960]{1,0:T(8,128)(2,1)}, bf16[80,960]{1,0:T(8,128)(2,1)S(1)}, u32[]{:S(2)}, u32[]{:S(2)}) %collective-permute-start.37) | collective-permute-done | bytes 153632 | tf_op jit(solution)/shard_map/ppermute | solution.py:29
  109.4 5.4 %collective-permute-done.38.refs_2_ = bf16[80,960]{1,0:T(8,128)(2,1)} collective-permute-done((bf16[80,960]{1,0:T(8,128)(2,1)}, bf16[80,960]{1,0:T(8,128)(2,1)}, u32[]{:S(2)}, u32[]{:S(2)}) %collective-permute-start.38) | collective-permute-done | bytes 153632 | tf_op jit(solution)/shard_map/ppermute | solution.py:29
  121.4 18.0 %collective-permute-done.31.refs_10_ = bf16[128,1280]{1,0:T(8,128)(2,1)S(1)} collective-permute-done((bf16[128,1280]{1,0:T(8,128)(2,1)S(1)}, bf16[128,1280]{1,0:T(8,128)(2,1)S(1)}, u32[]{:S(2)}, u32[]{:S(2)}) %collective-permute-start.31) | collective-permute-done | bytes 327712 | tf_op jit(solution)/shard_map/ppermute | solution.py:29
  145.3 3.9 %collective-permute-done.27.refs_5_.refs_2_ = bf16[128,960]{1,0:T(8,128)(2,1)S(1)} collective-permute-done((bf16[128,960]{1,0:T(8,128)(2,1)S(1)}, bf16[128,960]{1,0:T(8,128)(2,1)S(1)}, u32[]{:S(2)}, u32[]{:S(2)}) %collective-permute-start.27) | collective-permute-done | bytes 245792 | tf_op jit(solution)/shard_map/ppermute | solution.py:29
  152.5 15.1 %collective-permute-done.28.refs_6_.refs_3_ = bf16[128,960]{1,0:T(8,128)(2,1)S(1)} collective-permute-done((bf16[128,960]{1,0:T(8,128)(2,1)S(1)}, bf16[128,960]{1,0:T(8,128)(2,1)S(1)}, u32[]{:S(2)}, u32[]{:S(2)}) %collective-permute-start.28) | collective-permute-done | bytes 245792 | tf_op jit(solution)/shard_map/ppermute | solution.py:29
  169.3 10.6 %shard_map.235 = (bf16[512,640]{1,0:T(8,128)(2,1)}, bf16[512,1280]{1,0:T(8,128)(2,1)}, f32[128,1024]{1,0:T(8,128)}, bf16[128,1024]{1,0:T(8,128)(2,1)}, bf16[128,...) custom-call(bf16[128,1024]{1,0:T(8,128)(2,1)} %copy-done.12, bf16[128,1024]{1,0:T(8,128)(2,1)} %copy-done.13, ...), custom_call_target="tpu_custom_call" | custom-call | tf_op jit(solution)/shard_map/pallas_call | solution.py:110
  183.7 6.7 %collective-permute-done.46 = bf16[128,1024]{1,0:T(8,128)(2,1)S(1)} collective-permute-done((bf16[128,1024]{1,0:T(8,128)(2,1)}, bf16[128,1024]{1,0:T(8,128)(2,1)S(1)}, u32[]{:S(2)}, u32[]{:S(2)}) %collective-permute-start.46) | collective-permute-done | bytes 262176 | tf_op jit(solution)/shard_map/ppermute | solution.py:29
  196.5 4.7 %shard_map.243 = (f32[512,1280]{1,0:T(8,128)}, bf16[512,1280]{1,0:T(8,128)(2,1)}) custom-call(bf16[128,1024]{1,0:T(8,128)(2,1)} %copy-done.12, bf16[128,1024]{1,0:T(8,128)(2,1)} %copy-done.13, bf16[128,1024]{1,0:T(8,128)(2,1)} %copy-done.14, bf16[128,1024]{1,0:T(8,128)(2,1)} %copy-done.15, bf16[512,1280]{1,0:T(8,128)(2,1)} %get-tuple-element.128.refs_4_), custom_call_target="tpu_custom_call" | custom-call | tf_op jit(solution)/shard_map/pallas_call | solution.py:110
  202.3 5.8 %shard_map.236 = (f32[128,960]{1,0:T(8,128)}, bf16[128,960]{1,0:T(8,128)(2,1)}, bf16[128,960]{1,0:T(8,128)(2,1)}, bf16[128,960]{1,0:T(8,128)(2,1)}, f32[128,960]{1,0:T(8,128)}, /*index=5*/f32[128,960]{1,0:T(8,128)}) custom-call(bf16[128,960]{1,0:T(8,128)(2,1)} %copy-done.20, bf16[128,960]{1,0:T(8,128)(2,1)} %copy-done.40, ...), custom_call_target="tpu_custom_call" | custom-call | tf_op jit(solution)/shard_map/pallas_call | solution.py:110
  208.1 3.7 shard_map.245
  214.1 8.3 %shard_map.237 = (f32[128,960]{1,0:T(8,128)}, bf16[128,640]{1,0:T(8,128)(2,1)}, bf16[128,640]{1,0:T(8,128)(2,1)}, bf16[128,640]{1,0:T(8,128)(2,1)}, bf16[128,640]{1,0:T(8,128)(2,1)}, /*index=5*/f32[128,640]{1,0:T(8,128)}) custom-call(bf16[128,960]{1,0:T(8,128)(2,1)} %get-tuple-element.86.query_ref, s32[128,1]{1,0:T(8,128)} %copy.61.position_ref, ...), custom_call_target="tpu_custom_call" | custom-call | tf_op jit(solution)/shard_map/pallas_call | solution.py:110
  227.5 5.5 %collective-permute-done.53.refs_2_ = bf16[128,640]{1,0:T(8,128)(2,1)S(1)} collective-permute-done((bf16[128,640]{1,0:T(8,128)(2,1)}, bf16[128,640]{1,0:T(8,128)(2,1)S(1)}, u32[]{:S(2)}, u32[]{:S(2)}) %collective-permute-start.53) | collective-permute-done | bytes 163872 | tf_op jit(solution)/shard_map/ppermute | solution.py:35
  236.1 6.4 %collective-permute-start.78 = (bf16[128,960]{1,0:T(8,128)(2,1)}, bf16[128,960]{1,0:T(8,128)(2,1)}, u32[]{:S(2)}, u32[]{:S(2)}) collective-permute-start(bf16[128,960]{1,0:T(8,128)(2,1)} %get-tuple-element.140), channel_id=1, source_target_pairs={{0,4},{1,5},{2,6},{3,7},{4,0},{5,1},{6,2},{7,3},{8,12},{9,13},{10,... | collective-permute-start | bytes 737288 | tf_op jit(solution)/shard_map/ppermute | solution.py:29
  245.6 4.9 %collective-permute-start.79 = (bf16[128,960]{1,0:T(8,128)(2,1)}, bf16[128,960]{1,0:T(8,128)(2,1)}, u32[]{:S(2)}, u32[]{:S(2)}) collective-permute-start(bf16[128,960]{1,0:T(8,128)(2,1)} %get-tuple-element.141), channel_id=1, source_target_pairs={{0,6},{1,7},{2,4},{3,5},{4,2},{5,3},{6,0},{7,1},{8,14},{9,15},{10,... | collective-permute-start | bytes 737288 | tf_op jit(solution)/shard_map/ppermute | solution.py:29
  250.5 3.3 shard_map.244
  262.3 19.9 %collective-permute-done.74.refs_1_ = bf16[80,960]{1,0:T(8,128)(2,1)S(1)} collective-permute-done((bf16[80,960]{1,0:T(8,128)(2,1)}, bf16[80,960]{1,0:T(8,128)(2,1)S(1)}, u32[]{:S(2)}, u32[]{:S(2)}) %collective-permute-start.74) | collective-permute-done | bytes 153632 | tf_op jit(solution)/shard_map/ppermute | solution.py:29
  286.4 6.5 %shard_map.240 = (f32[128,1600]{1,0:T(8,128)}, bf16[128,1600]{1,0:T(8,128)(2,1)}, bf16[128,1600]{1,0:T(8,128)(2,1)}, bf16[128,1600]{1,0:T(8,128)(2,1)}, f32[128,960]{1,0:T(8,128)}, /*index=5*/f32[128,960]{1,0:T(8,128)}) custom-call(bf16[128,1600]{1,0:T(8,128)(2,1)} %shard_map.239.refs_0_, bf16[128,1600]{1,0:T(8,128)(2,1)} %copy-done.27, ...), custom_call_target="tpu_custom_call" | custom-call | tf_op jit(solution)/shard_map/pallas_call | solution.py:110
  292.9 6.9 %collective-permute-done.75.refs_2_ = bf16[80,960]{1,0:T(8,128)(2,1)S(1)} collective-permute-done((bf16[80,960]{1,0:T(8,128)(2,1)}, bf16[80,960]{1,0:T(8,128)(2,1)S(1)}, u32[]{:S(2)}, u32[]{:S(2)}) %collective-permute-start.75) | collective-permute-done | bytes 153632 | tf_op jit(solution)/shard_map/ppermute | solution.py:29
  315.3 3.5 shard_map.238
  339.0 5.1 %collective-permute-start.51 = (bf16[128,960]{1,0:T(8,128)(2,1)}, bf16[128,960]{1,0:T(8,128)(2,1)S(1)}, u32[]{:S(2)}, u32[]{:S(2)}) collective-permute-start(bf16[128,960]{1,0:T(8,128)(2,1)} %get-tuple-element.110), channel_id=1, source_target_pairs={{0,6},{1,7},{2,4},{3,5},{4,2},{5,3},{6,0},{7,1},{8,14},{9,15},{10,... | collective-permute-start | bytes 737288 | tf_op jit(solution)/shard_map/ppermute | solution.py:29
  345.9 4.4 %collective-permute-start.50 = (bf16[128,960]{1,0:T(8,128)(2,1)}, bf16[128,960]{1,0:T(8,128)(2,1)S(1)}, u32[]{:S(2)}, u32[]{:S(2)}) collective-permute-start(bf16[128,960]{1,0:T(8,128)(2,1)} %get-tuple-element.109), channel_id=1, source_target_pairs={{0,4},{1,5},{2,6},{3,7},{4,0},{5,1},{6,2},{7,3},{8,12},{9,13},{10,... | collective-permute-start | bytes 737288 | tf_op jit(solution)/shard_map/ppermute | solution.py:29
  350.2 6.9 %collective-permute-done.64.refs_2_ = bf16[128,1600]{1,0:T(8,128)(2,1)} collective-permute-done((bf16[128,1600]{1,0:T(8,128)(2,1)}, bf16[128,1600]{1,0:T(8,128)(2,1)}, u32[]{:S(2)}, u32[]{:S(2)}) %collective-permute-start.64) | collective-permute-done | bytes 409632 | tf_op jit(solution)/shard_map/ppermute | solution.py:29
  (387 shorter events, 172.1 us)
Async XLA Ops:
  13.7 34.9 %collective-permute-start.15 = (bf16[32,1280]{1,0:T(8,128)(2,1)}, bf16[32,1280]{1,0:T(8,128)(2,1)}, u32[]{:S(2)}, u32[]{:S(2)}) collective-permute-start(bf16[32,1280]{1,0:T(8,128)(2,1)} %get-tuple-element.216), channel_id=1, source_target_pairs={{0,6},{1,7},{2,4},{3,5},{4,2},{5,3},{6,0},{7,1},{8,14},{9,15},{10,... | collective-permute-start | bytes 245768 | tf_op jit(solution)/shard_map/ppermute | solution.py:29
  19.1 21.4 %collective-permute-start.5 = (bf16[128,1600]{1,0:T(8,128)(2,1)S(1)}, bf16[128,1600]{1,0:T(8,128)(2,1)S(1)}, u32[]{:S(2)}, u32[]{:S(2)}) collective-permute-start(bf16[128,1600]{1,0:T(8,128)(2,1)S(1)} %pad_maximum_fusion.refs_3_.refs_4_), channel_id=1, source_target_pairs={{0,4},{1,5},{2,6},{3,7},{4,0},{5,1},{6,2},{7,3},{8,12},{9,13},{10,... | collective-permute-start | bytes 1228808 | tf_op jit(solution)/shard_map/ppermute | solution.py:29
  20.7 21.2 %collective-permute-start.6 = (bf16[128,1600]{1,0:T(8,128)(2,1)S(1)}, bf16[128,1600]{1,0:T(8,128)(2,1)S(1)}, u32[]{:S(2)}, u32[]{:S(2)}) collective-permute-start(bf16[128,1600]{1,0:T(8,128)(2,1)S(1)} %pad_maximum_fusion.refs_3_.refs_4_), channel_id=1, source_target_pairs={{0,6},{1,7},{2,4},{3,5},{4,2},{5,3},{6,0},{7,1},{8,14},{9,15},{10,... | collective-permute-start | bytes 1228808 | tf_op jit(solution)/shard_map/ppermute | solution.py:29
  22.8 25.8 %collective-permute-start.14 = (bf16[32,1280]{1,0:T(8,128)(2,1)S(1)}, bf16[32,1280]{1,0:T(8,128)(2,1)S(1)}, u32[]{:S(2)}, u32[]{:S(2)}) collective-permute-start(bf16[32,1280]{1,0:T(8,128)(2,1)S(1)} %get-tuple-element.214), channel_id=1, source_target_pairs={{0,4},{1,5},{2,6},{3,7},{4,0},{5,1},{6,2},{7,3},{8,12},{9,13},{10,... | collective-permute-start | bytes 245768 | tf_op jit(solution)/shard_map/ppermute | solution.py:29
  56.2 19.1 %collective-permute-start.17 = (bf16[32,960]{1,0:T(8,128)(2,1)S(1)}, bf16[32,960]{1,0:T(8,128)(2,1)S(1)}, u32[]{:S(2)}, u32[]{:S(2)}) collective-permute-start(bf16[32,960]{1,0:T(8,128)(2,1)S(1)} %pad.14), channel_id=1, source_target_pairs={{0,8},{1,9},{2,10},{3,11},{4,12},{5,13},{6,14},{7,15},{8,0},{9,1},... | collective-permute-start | bytes 184328 | tf_op jit(solution)/shard_map/ppermute | solution.py:29
  97.0 21.4 %collective-permute-start.23 = (f32[128,960]{1,0:T(8,128)}, f32[128,960]{1,0:T(8,128)S(1)}, u32[]{:S(2)}, u32[]{:S(2)}) collective-permute-start(f32[128,960]{1,0:T(8,128)} %get-tuple-element.92), channel_id=1, source_target_pairs={{0,1},{1,0},{2,3},{3,2},{4,5},{5,4},{6,7},{7,6},{8,9},{9,8},{10,11... | collective-permute-start | bytes 1474568 | tf_op jit(solution)/shard_map/ppermute | solution.py:29
  101.8 19.5 %collective-permute-start.30 = (bf16[128,1280]{1,0:T(8,128)(2,1)S(1)}, bf16[128,1280]{1,0:T(8,128)(2,1)S(1)}, u32[]{:S(2)}, u32[]{:S(2)}) collective-permute-start(bf16[128,1280]{1,0:T(8,128)(2,1)S(1)} %pad_maximum_fusion.2.refs_8_), channel_id=1, source_target_pairs={{0,8},{1,9},{2,10},{3,11},{4,12},{5,13},{6,14},{7,15},{8,0},{9,1},... | collective-permute-start | bytes 983048 | tf_op jit(solution)/shard_map/ppermute | solution.py:29
  107.5 31.9 %collective-permute-start.31 = (bf16[128,1280]{1,0:T(8,128)(2,1)S(1)}, bf16[128,1280]{1,0:T(8,128)(2,1)S(1)}, u32[]{:S(2)}, u32[]{:S(2)}) collective-permute-start(bf16[128,1280]{1,0:T(8,128)(2,1)S(1)} %pad_maximum_fusion.2.refs_8_), channel_id=1, source_target_pairs={{0,16},{1,17},{2,18},{3,19},{4,20},{5,21},{6,22},{7,23},{8,24},{9,... | collective-permute-start | bytes 983048 | tf_op jit(solution)/shard_map/ppermute | solution.py:29
  114.8 24.5 %collective-permute-start.32 = (bf16[128,1280]{1,0:T(8,128)(2,1)S(1)}, bf16[128,1280]{1,0:T(8,128)(2,1)S(1)}, u32[]{:S(2)}, u32[]{:S(2)}) collective-permute-start(bf16[128,1280]{1,0:T(8,128)(2,1)S(1)} %pad_maximum_fusion.2.refs_8_), channel_id=1, source_target_pairs={{0,24},{1,25},{2,26},{3,27},{4,28},{5,29},{6,30},{7,31},{8,16},{9,... | collective-permute-start | bytes 983048 | tf_op jit(solution)/shard_map/ppermute | solution.py:29
  120.2 20.8 %collective-permute-start.33 = (bf16[128,1280]{1,0:T(8,128)(2,1)S(1)}, bf16[128,1280]{1,0:T(8,128)(2,1)S(1)}, u32[]{:S(2)}, u32[]{:S(2)}) collective-permute-start(bf16[128,1280]{1,0:T(8,128)(2,1)S(1)} %pad_maximum_fusion.2.refs_8_), channel_id=1, source_target_pairs={{0,1},{1,0},{2,3},{3,2},{4,5},{5,4},{6,7},{7,6},{8,9},{9,8},{10,11... | collective-permute-start | bytes 983048 | tf_op jit(solution)/shard_map/ppermute | solution.py:29
  120.4 19.5 %collective-permute-start.43 = (bf16[80,960]{1,0:T(8,128)(2,1)}, bf16[80,960]{1,0:T(8,128)(2,1)}, u32[]{:S(2)}, u32[]{:S(2)}) collective-permute-start(bf16[80,960]{1,0:T(8,128)(2,1)} %copy-done.42), channel_id=1, source_target_pairs={{0,1},{1,0},{2,3},{3,2},{4,5},{5,4},{6,7},{7,6},{8,9},{9,8},{10,11... | collective-permute-start | bytes 460808 | tf_op jit(solution)/shard_map/ppermute | solution.py:29
  121.4 21.6 %collective-permute-start.34 = (bf16[128,1280]{1,0:T(8,128)(2,1)S(1)}, bf16[128,1280]{1,0:T(8,128)(2,1)S(1)}, u32[]{:S(2)}, u32[]{:S(2)}) collective-permute-start(bf16[128,1280]{1,0:T(8,128)(2,1)S(1)} %collective-permute-done.30.refs_9_), channel_id=1, source_target_pairs={{0,1},{1,0},{2,3},{3,2},{4,5},{5,4},{6,7},{7,6},{8,9},{9,8},{10,11... | collective-permute-start | bytes 983048 | tf_op jit(solution)/shard_map/ppermute | solution.py:29
  140.9 26.7 %collective-permute-start.24 = (bf16[128,1024]{1,0:T(8,128)(2,1)S(1)}, bf16[128,1024]{1,0:T(8,128)(2,1)S(1)}, u32[]{:S(2)}, u32[]{:S(2)}) collective-permute-start(bf16[128,1024]{1,0:T(8,128)(2,1)S(1)} %fusion.8.refs_0_), channel_id=1, source_target_pairs={{0,2},{1,3},{2,0},{3,1},{4,6},{5,7},{6,4},{7,5},{8,10},{9,11},{10,... | collective-permute-start | bytes 786440 | tf_op jit(solution)/shard_map/ppermute | solution.py:29
  143.0 24.7 %collective-permute-start.25 = (bf16[128,1024]{1,0:T(8,128)(2,1)S(1)}, bf16[128,1024]{1,0:T(8,128)(2,1)S(1)}, u32[]{:S(2)}, u32[]{:S(2)}) collective-permute-start(bf16[128,1024]{1,0:T(8,128)(2,1)S(1)} %fusion.8.refs_0_), channel_id=1, source_target_pairs={{0,4},{1,5},{2,6},{3,7},{4,0},{5,1},{6,2},{7,3},{8,12},{9,13},{10,... | collective-permute-start | bytes 786440 | tf_op jit(solution)/shard_map/ppermute | solution.py:29
  143.1 24.6 %collective-permute-start.26 = (bf16[128,1024]{1,0:T(8,128)(2,1)S(1)}, bf16[128,1024]{1,0:T(8,128)(2,1)S(1)}, u32[]{:S(2)}, u32[]{:S(2)}) collective-permute-start(bf16[128,1024]{1,0:T(8,128)(2,1)S(1)} %fusion.8.refs_0_), channel_id=1, source_target_pairs={{0,6},{1,7},{2,4},{3,5},{4,2},{5,3},{6,0},{7,1},{8,14},{9,15},{10,... | collective-permute-start | bytes 786440 | tf_op jit(solution)/shard_map/ppermute | solution.py:29
  144.7 23.0 %collective-permute-start.28 = (bf16[128,960]{1,0:T(8,128)(2,1)S(1)}, bf16[128,960]{1,0:T(8,128)(2,1)S(1)}, u32[]{:S(2)}, u32[]{:S(2)}) collective-permute-start(bf16[128,960]{1,0:T(8,128)(2,1)S(1)} %copy.65.refs_4_.refs_1_), channel_id=1, source_target_pairs={{0,4},{1,5},{2,6},{3,7},{4,0},{5,1},{6,2},{7,3},{8,12},{9,13},{10,... | collective-permute-start | bytes 737288 | tf_op jit(solution)/shard_map/ppermute | solution.py:29
  201.1 44.5 %collective-permute-start.69 = (bf16[512,1280]{1,0:T(8,128)(2,1)}, bf16[512,1280]{1,0:T(8,128)(2,1)S(1)}, u32[]{:S(2)}, u32[]{:S(2)}) collective-permute-start(bf16[512,1280]{1,0:T(8,128)(2,1)} %get-tuple-element.130), channel_id=1, source_target_pairs={{0,1},{1,0},{2,3},{3,2},{4,5},{5,4},{6,7},{7,6},{8,9},{9,8},{10,11... | collective-permute-start | bytes 3932168 | tf_op jit(solution)/shard_map/ppermute | solution.py:29
  211.8 42.1 %collective-permute-start.73 = (bf16[320,960]{1,0:T(8,128)(2,1)}, bf16[320,960]{1,0:T(8,128)(2,1)S(1)}, u32[]{:S(2)}, u32[]{:S(2)}) collective-permute-start(bf16[320,960]{1,0:T(8,128)(2,1)} %get-tuple-element.135), channel_id=1, source_target_pairs={{0,1},{1,0},{2,3},{3,2},{4,5},{5,4},{6,7},{7,6},{8,9},{9,8},{10,11... | collective-permute-start | bytes 1843208 | tf_op jit(solution)/shard_map/ppermute | solution.py:29
  233.1 23.4 %collective-permute-start.77 = (bf16[128,960]{1,0:T(8,128)(2,1)}, bf16[128,960]{1,0:T(8,128)(2,1)}, u32[]{:S(2)}, u32[]{:S(2)}) collective-permute-start(bf16[128,960]{1,0:T(8,128)(2,1)} %get-tuple-element.139), channel_id=1, source_target_pairs={{0,2},{1,3},{2,0},{3,1},{4,6},{5,7},{6,4},{7,5},{8,10},{9,11},{10,... | collective-permute-start | bytes 737288 | tf_op jit(solution)/shard_map/ppermute | solution.py:29
  236.1 21.1 %collective-permute-start.78 = (bf16[128,960]{1,0:T(8,128)(2,1)}, bf16[128,960]{1,0:T(8,128)(2,1)}, u32[]{:S(2)}, u32[]{:S(2)}) collective-permute-start(bf16[128,960]{1,0:T(8,128)(2,1)} %get-tuple-element.140), channel_id=1, source_target_pairs={{0,4},{1,5},{2,6},{3,7},{4,0},{5,1},{6,2},{7,3},{8,12},{9,13},{10,... | collective-permute-start | bytes 737288 | tf_op jit(solution)/shard_map/ppermute | solution.py:29
  245.2 39.5 %collective-permute-start.56 = (bf16[128,1600]{1,0:T(8,128)(2,1)}, bf16[128,1600]{1,0:T(8,128)(2,1)S(1)}, u32[]{:S(2)}, u32[]{:S(2)}) collective-permute-start(bf16[128,1600]{1,0:T(8,128)(2,1)} %shard_map.239.refs_0_), channel_id=1, source_target_pairs={{0,1},{1,0},{2,3},{3,2},{4,5},{5,4},{6,7},{7,6},{8,9},{9,8},{10,11... | collective-permute-start | bytes 1228808 | tf_op jit(solution)/shard_map/ppermute | solution.py:29
  253.9 45.9 %collective-permute-start.70 = (bf16[128,1280]{1,0:T(8,128)(2,1)}, bf16[128,1280]{1,0:T(8,128)(2,1)S(1)}, u32[]{:S(2)}, u32[]{:S(2)}) collective-permute-start(bf16[128,1280]{1,0:T(8,128)(2,1)} %get-tuple-element.131), channel_id=1, source_target_pairs={{0,8},{1,9},{2,10},{3,11},{4,12},{5,13},{6,14},{7,15},{8,0},{9,1},... | collective-permute-start | bytes 983048 | tf_op jit(solution)/shard_map/ppermute | solution.py:29
  256.4 43.4 %collective-permute-start.71 = (bf16[128,1280]{1,0:T(8,128)(2,1)}, bf16[128,1280]{1,0:T(8,128)(2,1)S(1)}, u32[]{:S(2)}, u32[]{:S(2)}) collective-permute-start(bf16[128,1280]{1,0:T(8,128)(2,1)} %get-tuple-element.132), channel_id=1, source_target_pairs={{0,16},{1,17},{2,18},{3,19},{4,20},{5,21},{6,22},{7,23},{8,24},{9,... | collective-permute-start | bytes 983048 | tf_op jit(solution)/shard_map/ppermute | solution.py:29
  257.1 42.7 %collective-permute-start.72 = (bf16[128,1280]{1,0:T(8,128)(2,1)}, bf16[128,1280]{1,0:T(8,128)(2,1)S(1)}, u32[]{:S(2)}, u32[]{:S(2)}) collective-permute-start(bf16[128,1280]{1,0:T(8,128)(2,1)} %get-tuple-element.133), channel_id=1, source_target_pairs={{0,24},{1,25},{2,26},{3,27},{4,28},{5,29},{6,30},{7,31},{8,16},{9,... | collective-permute-start | bytes 983048 | tf_op jit(solution)/shard_map/ppermute | solution.py:29
  261.3 20.9 %collective-permute-start.74 = (bf16[80,960]{1,0:T(8,128)(2,1)}, bf16[80,960]{1,0:T(8,128)(2,1)S(1)}, u32[]{:S(2)}, u32[]{:S(2)}) collective-permute-start(bf16[80,960]{1,0:T(8,128)(2,1)} %get-tuple-element.136), channel_id=1, source_target_pairs={{0,8},{1,9},{2,10},{3,11},{4,12},{5,13},{6,14},{7,15},{8,0},{9,1},... | collective-permute-start | bytes 460808 | tf_op jit(solution)/shard_map/ppermute | solution.py:29
  311.4 18.5 %collective-permute-start.83 = (bf16[32,1280]{1,0:T(8,128)(2,1)}, bf16[32,1280]{1,0:T(8,128)(2,1)S(1)}, u32[]{:S(2)}, u32[]{:S(2)}) collective-permute-start(bf16[32,1280]{1,0:T(8,128)(2,1)} %get-tuple-element.206), channel_id=1, source_target_pairs={{0,6},{1,7},{2,4},{3,5},{4,2},{5,3},{6,0},{7,1},{8,14},{9,15},{10,... | collective-permute-start | bytes 245768 | tf_op jit(solution)/shard_map/ppermute | solution.py:29
  323.1 22.7 %collective-permute-start.63 = (bf16[128,1600]{1,0:T(8,128)(2,1)}, bf16[128,1600]{1,0:T(8,128)(2,1)}, u32[]{:S(2)}, u32[]{:S(2)}) collective-permute-start(bf16[128,1600]{1,0:T(8,128)(2,1)} %get-tuple-element.120), channel_id=1, source_target_pairs={{0,2},{1,3},{2,0},{3,1},{4,6},{5,7},{6,4},{7,5},{8,10},{9,11},{10,... | collective-permute-start | bytes 1228808 | tf_op jit(solution)/shard_map/ppermute | solution.py:29
  326.9 30.3 %collective-permute-start.64 = (bf16[128,1600]{1,0:T(8,128)(2,1)}, bf16[128,1600]{1,0:T(8,128)(2,1)}, u32[]{:S(2)}, u32[]{:S(2)}) collective-permute-start(bf16[128,1600]{1,0:T(8,128)(2,1)} %get-tuple-element.121), channel_id=1, source_target_pairs={{0,4},{1,5},{2,6},{3,7},{4,0},{5,1},{6,2},{7,3},{8,12},{9,13},{10,... | collective-permute-start | bytes 1228808 | tf_op jit(solution)/shard_map/ppermute | solution.py:29
  328.4 28.8 %collective-permute-start.65 = (bf16[128,1600]{1,0:T(8,128)(2,1)}, bf16[128,1600]{1,0:T(8,128)(2,1)}, u32[]{:S(2)}, u32[]{:S(2)}) collective-permute-start(bf16[128,1600]{1,0:T(8,128)(2,1)} %get-tuple-element.122), channel_id=1, source_target_pairs={{0,6},{1,7},{2,4},{3,5},{4,2},{5,3},{6,0},{7,1},{8,14},{9,15},{10,... | collective-permute-start | bytes 1228808 | tf_op jit(solution)/shard_map/ppermute | solution.py:29
  333.8 27.5 %collective-permute-start.59 = (f32[2,960]{1,0:T(2,128)S(1)}, f32[2,960]{1,0:T(2,128)}, u32[]{:S(2)}, u32[]{:S(2)}) collective-permute-start(f32[2,960]{1,0:T(2,128)S(1)} %fusion.28), channel_id=1, source_target_pairs={{0,2},{1,3},{2,0},{3,1},{4,6},{5,7},{6,4},{7,5},{8,10},{9,11},{10,... | collective-permute-start | bytes 23048 | tf_op jit(solution)/shard_map/ppermute | solution.py:29
  339.0 30.2 %collective-permute-start.51 = (bf16[128,960]{1,0:T(8,128)(2,1)}, bf16[128,960]{1,0:T(8,128)(2,1)S(1)}, u32[]{:S(2)}, u32[]{:S(2)}) collective-permute-start(bf16[128,960]{1,0:T(8,128)(2,1)} %get-tuple-element.110), channel_id=1, source_target_pairs={{0,6},{1,7},{2,4},{3,5},{4,2},{5,3},{6,0},{7,1},{8,14},{9,15},{10,... | collective-permute-start | bytes 737288 | tf_op jit(solution)/shard_map/ppermute | solution.py:29
  345.9 23.4 %collective-permute-start.50 = (bf16[128,960]{1,0:T(8,128)(2,1)}, bf16[128,960]{1,0:T(8,128)(2,1)S(1)}, u32[]{:S(2)}, u32[]{:S(2)}) collective-permute-start(bf16[128,960]{1,0:T(8,128)(2,1)} %get-tuple-element.109), channel_id=1, source_target_pairs={{0,4},{1,5},{2,6},{3,7},{4,0},{5,1},{6,2},{7,3},{8,12},{9,13},{10,... | collective-permute-start | bytes 737288 | tf_op jit(solution)/shard_map/ppermute | solution.py:29
  (125 other events, 1459.8 us)

commit v4 on v3

--- a/solution.py
+++ b/solution.py
@@ -145,6 +145,22 @@
             out[...] = total[i * rows : (i + 1) * rows].astype(out.dtype)
 
     outs = [((rows, width), jnp.float32 if i == 0 else LINK) for i in range(count)]
+    return kernel_call(body, outs, [own] + list(received))
+
+
+def sum_columns(own, received, rows, widths):
+    count = len(received)
+
+    def body(*refs):
+        start = 0
+        for out, width in zip(refs[1 + count :], widths):
+            total = refs[0][:rows, start : start + width]
+            for ref in refs[1 : 1 + count]:
+                total = total + ref[:rows, start : start + width].astype(jnp.float32)
+            out[...] = total
+            start += width
+
+    outs = [((rows, width), jnp.float32) for width in widths]
     return kernel_call(body, outs, [own] + list(received))
 
 
@@ -656,7 +672,7 @@
     out_outer, cotangent_late, _ = tie(out_outer, cotangent, projected_parts)
     weight_out = spread(out_outer, out_plan.team)
     query_low, key_value = turn(projected_parts, tables, q_width, k_width)
-    pieces = [passed_along(key_value, distance) for distance in range(window_span, 0, -1)]
+    pieces = [passed_along(key_value, d) for d in range(window_span, 0, -1)]
     cotangent_blocks = spread(cotangent_late, masks)
     window_blocks = pieces + [key_value]
     attended_low, log_total = attend(query_low, window_blocks, positions, prefix)
@@ -670,9 +686,10 @@
     hidden_low, grad_low, back_blocks = feed_forward(
         normed_blocks, cotangent_blocks, weight_pair, weight_down
     )
+    back_arrived = [swap(block, mask) for block, mask in zip(back_blocks[1:], masks[1:])]
     back_total = back_blocks[0]
-    for block, mask in zip(back_blocks[1:], masks[1:]):
-        back_total = back_total + swap(block, mask).astype(jnp.float32)
+    for block in back_arrived:
+        back_total = back_total + block.astype(jnp.float32)
     back_high = lax.reduce_precision(back_total, 8, 7)
     grad_normed_two = back_product(back_high.astype(jnp.bfloat16), select_ff) + back_product(
         (back_total - back_high).astype(jnp.bfloat16), select_ff
@@ -681,9 +698,7 @@
     pair_rows = placed_two.shape[1] // len(in_plan.last)
     pair_grads = split_products(normed_blocks, grad_low, pair_rows)
     pair_arrived = [swap(g, m) for g, m in zip(pair_grads[1:], in_plan.last[1:])]
-    down_grads = down_products(
-        hidden_low, cotangent_blocks, unit_starts, down_rows, select_unit
-    )
+    down_grads = down_products(hidden_low, cotangent_blocks, unit_starts, down_rows, select_unit)
     down_arrived = [swap(down_grads[1], 1)]
     outer_group = 1 << len(in_plan.outer[-1])
     pair_own, *pair_blocks = reduce_split(pair_grads[0], pair_arrived, outer_group)
@@ -708,16 +723,17 @@
         pair_parts.append(passed_along(grad_windows[window_span - distance], -distance))
     hidden_late, _ = tie(hidden_low, grad_query)
     out_blocks = block_products(hidden_late, weight_down, TEAM)
+    out_swapped = [swap(block, mask) for block, mask in zip(out_blocks[1:], masks[1:])]
     out_total = out_blocks[0]
-    for block, mask in zip(out_blocks[1:], masks[1:]):
-        out_total = out_total + swap(block, mask).astype(jnp.float32)
+    for block in out_swapped:
+        out_total = out_total + block.astype(jnp.float32)
     block_out = (mid_rows + out_total).astype(jnp.bfloat16)
     grad_projected = turn_back(grad_query, pair_parts, tables)
-    in_grads, normed_grads = pair_back(
-        both_cores(grad_projected), placed_one, select_in, weight_in
-    )
+    grad_projected_pair = both_cores(grad_projected)
+    in_grads, normed_grads = pair_back(grad_projected_pair, placed_one, select_in, weight_in)
     in_arrived = [swap(g, m) for g, m in zip(in_grads[1:], in_plan.team[1:])]
-    pair_sent, down_sent, out_arrived, _ = tie(pair_sent, down_sent, out_arrived, in_grads[0])
+    pair_sent, down_sent, _ = tie(pair_sent, down_sent, in_grads[0])
+    out_arrived, _ = tie(out_arrived, in_grads[0])
     pair_sum = in_plan.outer_sum(pair_own, pair_sent)
     down_sum = in_plan.outer_sum(down_own, down_sent)
     grad_down = lax.ppermute(down_sum.astype(LINK), AXIS, trade_route).astype(jnp.float32).reshape(-1)
@@ -744,22 +760,30 @@
     grad_gate = owned(natural[0])
     grad_up = owned(natural[1])
 
-    def weight_share(plan, own, arrived_blocks):
+    def team_share(plan, own, arrived_blocks):
         own, *blocks = reduce_split(own, arrived_blocks, 1 << len(plan.outer[-1]))
-        return plan.outer_sum(own, plan.outer_send(blocks))[: plan.rows]
-
-    out_share = weight_share(out_plan, out_grads[0], out_arrived)
+        return own, blocks
+
+    out_own, out_split = team_share(out_plan, out_grads[0], out_arrived)
+    out_sent = out_plan.outer_send(out_split)
+    in_own, in_split = team_share(in_plan, in_grads[0], in_arrived)
+    in_sent = in_plan.outer_send(in_split)
+    out_share = out_plan.outer_sum(out_own, out_sent)[: out_plan.rows]
     grad_out = out_plan.own_share(out_share, place)
-    in_share = weight_share(in_plan, in_grads[0], in_arrived)
-    grad_query_weight = in_plan.own_share(in_share[:, :q_width], place)
-    grad_key_weight = in_plan.own_share(in_share[:, q_width : q_width + k_width], place)
-    grad_value_weight = in_plan.own_share(in_share[:, q_width + k_width :], place)
+    if len(in_plan.outer) == 1:
+        in_shares = sum_columns(in_own, in_sent, in_plan.rows, (q_width, k_width, k_width))
+    else:
+        in_share = in_plan.outer_sum(in_own, in_sent)[: in_plan.rows]
+        in_shares = jnp.split(in_share, [q_width, q_width + k_width], axis=1)
+    grad_query_weight, grad_key_weight, grad_value_weight = (
+        in_plan.own_share(share, place) for share in in_shares
+    )
     grad_normed_one = pair_total(normed_grads)
     grad_in_norm, grad_gain_one = norm_backward(input_rows, scale_one, norm1_gain, grad_normed_one)
     grad_in = (grad_mid + grad_in_norm).astype(jnp.bfloat16)
     gains = jnp.stack([grad_gain_one, grad_gain_two])
     for bit in range(device_count.bit_length() - 1):
-        gains = gains + swap(gains, 1 << bit)
+        gains = reduce_split(gains, [swap(gains, 1 << bit)], 1)[0]
     return (
         block_out,
         grad_in,

time: 391 us -> 397 us (1.015)
  starting transfers between devices: 126 us -> 117 us
  Pallas kernels: 83.1 us -> 89.2 us
  local copies, waits for them, and re-layouts: 31.7 us -> 35.7 us
    ppermute x77, starting transfers between devices: 105 us -> 95.6 us  [swap(): return lax.ppermute(block, AXIS, [(i, i ^ mask) for i in range(size)])]
    pallas_call x19 -> x24, Pallas kernels: 76.9 us -> 82.9 us  [kernel_call(): pl.pallas_call(body, out_shape=[jax.ShapeDtypeStruct(shape, dtype) for sh...]
    unnamed x144 -> x160, local copies, waits for them, and re-layouts: 10.4 us -> 13 us
  transfers between devices with their start and end apart: 87 -> 87, of which waited for: 22 -> 24; matrix products, arithmetic and copies ran while one was open for 9% -> 10% of each run, Pallas kernels for 17% -> 19%
where the time goes in v4:
time: 397 us; the launch traced here: 391 us
  waiting for transfers between devices  126 us (32%)
  starting transfers between devices  117 us (29%)
  Pallas kernels  89.2 us (22%)
  local copies, waits for them, and re-layouts  35.7 us (9%)
  other arithmetic  16.5 us (4%)
  matrix products  4.1 us (1%)
    ppermute x77, waiting for transfers between devices, swap(): return lax.ppermute(block, AXIS, [(i, i ^ mask) for i in range(size)])  121 us
    ppermute x77, starting transfers between devices, swap(): return lax.ppermute(block, AXIS, [(i, i ^ mask) for i in range(size)])  95.6 us
    pallas_call x24, Pallas kernels, kernel_call(): pl.pallas_call(body, out_shape=[jax.ShapeDtypeStruct(shape, dtype) for sh...  82.9 us
    ppermute x8, starting transfers between devices, passed_along(): return lax.ppermute(block, AXIS, route)  17.6 us
    unnamed x160, local copies, waits for them, and re-layouts  13 us
  transfers between devices with their start and end apart: 87, of which 24 were waited for; matrix products, arithmetic and copies ran while one was open for 10% of the time, Pallas kernels for 19%

profile of v4, /device:TPU:0, one launch (start us, length us, event | category | flops | bytes accessed | tf_op | source)
XLA Modules:
  0.0 390.8 jit_solution(8327292632688238247)
XLA Ops:
  3.4 5.1 %collective-permute-start.3 = (bf16[32,1600]{1,0:T(8,128)(2,1)S(1)}, bf16[32,1600]{1,0:T(8,128)(2,1)S(1)}, u32[]{:S(2)}, u32[]{:S(2)}) collective-permute-start(bf16[32,1600]{1,0:T(8,128)(2,1)S(1)} %pad.12), channel_id=1, source_target_pairs={{0,24},{1,25},{2,26},{3,27},{4,28},{5,29},{6,30},{7,31},{8,16},{9,... | collective-permute-start | bytes 307208 | tf_op jit(solution)/shard_map/ppermute | solution.py:29
  24.4 5.9 %collective-permute-done.4.refs_4_.refs_5_ = bf16[128,1600]{1,0:T(8,128)(2,1)S(1)} collective-permute-done((bf16[128,1600]{1,0:T(8,128)(2,1)S(1)}, bf16[128,1600]{1,0:T(8,128)(2,1)S(1)}, u32[]{:S(2)}, u32[]{:S(2)}) %collective-permute-start.4) | collective-permute-done | bytes 409632 | tf_op jit(solution)/shard_map/ppermute | solution.py:29
  31.8 8.8 %collective-permute-done.5.refs_5_.refs_6_ = bf16[128,1600]{1,0:T(8,128)(2,1)S(1)} collective-permute-done((bf16[128,1600]{1,0:T(8,128)(2,1)S(1)}, bf16[128,1600]{1,0:T(8,128)(2,1)S(1)}, u32[]{:S(2)}, u32[]{:S(2)}) %collective-permute-start.5) | collective-permute-done | bytes 409632 | tf_op jit(solution)/shard_map/ppermute | solution.py:29
  42.8 4.5 %shard_map.230 = (f32[128,1600]{1,0:T(8,128)}, f32[128,1600]{1,0:T(8,128)}, bf16[256,512]{1,0:T(8,128)(2,1)}) custom-call(bf16[128,960]{1,0:T(8,128)(2,1)} %copy-done.16, bf16[128,960]{1,0:T(8,128)(2,1)} %copy-done.39, bf16[960,512]{1,0:T(8,128)(2,1)} %fusion.6.refs_2_.refs_3_, bf16[128,1600]{1,0:T(8,128)(2,1)} %copy-done, bf16[128,1600]{1,0:T(8,128)(2,1)} %copy-done.4, ...), custom_call_target="tpu_custom_call" | custom-call | tf_op jit(solution)/shard_map/pallas_call | solution.py:110
  50.8 4.5 %collective-permute-start.19 = (bf16[32,960]{1,0:T(8,128)(2,1)S(1)}, bf16[32,960]{1,0:T(8,128)(2,1)S(1)}, u32[]{:S(2)}, u32[]{:S(2)}) collective-permute-start(bf16[32,960]{1,0:T(8,128)(2,1)S(1)} %pad.14), channel_id=1, source_target_pairs={{0,24},{1,25},{2,26},{3,27},{4,28},{5,29},{6,30},{7,31},{8,16},{9,... | collective-permute-start | bytes 184328 | tf_op jit(solution)/shard_map/ppermute | solution.py:29
  62.3 5.1 %collective-permute-start.8 = (bf16[128,640]{1,0:T(8,128)(2,1)}, bf16[128,640]{1,0:T(8,128)(2,1)S(1)}, u32[]{:S(2)}, u32[]{:S(2)}) collective-permute-start(bf16[128,640]{1,0:T(8,128)(2,1)} %get-tuple-element.90.refs_4_), channel_id=1, source_target_pairs={{0,4},{1,5},{2,6},{3,7},{4,8},{5,9},{6,10},{7,11},{8,12},{9,13},{1... | collective-permute-start | bytes 491528 | tf_op jit(solution)/shard_map/ppermute | solution.py:35
  80.6 5.7 %shard_map.232 = (bf16[128,960]{1,0:T(8,128)(2,1)}, f32[5,384,1]{2,1,0:T(8,128)}) custom-call(bf16[128,960]{1,0:T(8,128)(2,1)} %get-tuple-element.89.query_ref, s32[128,1]{1,0:T(8,128)} %copy.61.position_ref, bf16[128,640]{1,0:T(8,128)(2,1)} %copy-done.23, bf16[128,640]{1,0:T(8,128)(2,1)} %copy-done.24, bf16[128,640]{1,0:T(8,128)(2,1)} %copy-done.25, ...), custom_call_target="tpu_custom_call" | custom-call | tf_op jit(solution)/shard_map/pallas_call | solution.py:110
  86.5 4.8 %collective-permute-done.21.refs_5_.refs_6_ = bf16[128,960]{1,0:T(8,128)(2,1)S(1)} collective-permute-done((bf16[128,960]{1,0:T(8,128)(2,1)S(1)}, bf16[128,960]{1,0:T(8,128)(2,1)S(1)}, u32[]{:S(2)}, u32[]{:S(2)}) %collective-permute-start.21) | collective-permute-done | bytes 245792 | tf_op jit(solution)/shard_map/ppermute | solution.py:29
  93.7 3.8 shard_map.233
  103.1 4.6 %collective-permute-done.37.refs_1_ = bf16[80,960]{1,0:T(8,128)(2,1)S(1)} collective-permute-done((bf16[80,960]{1,0:T(8,128)(2,1)}, bf16[80,960]{1,0:T(8,128)(2,1)S(1)}, u32[]{:S(2)}, u32[]{:S(2)}) %collective-permute-start.37) | collective-permute-done | bytes 153632 | tf_op jit(solution)/shard_map/ppermute | solution.py:29
  109.5 5.4 %collective-permute-done.38.refs_2_ = bf16[80,960]{1,0:T(8,128)(2,1)} collective-permute-done((bf16[80,960]{1,0:T(8,128)(2,1)}, bf16[80,960]{1,0:T(8,128)(2,1)}, u32[]{:S(2)}, u32[]{:S(2)}) %collective-permute-start.38) | collective-permute-done | bytes 153632 | tf_op jit(solution)/shard_map/ppermute | solution.py:29
  121.5 18.0 %collective-permute-done.31.refs_10_ = bf16[128,1280]{1,0:T(8,128)(2,1)S(1)} collective-permute-done((bf16[128,1280]{1,0:T(8,128)(2,1)S(1)}, bf16[128,1280]{1,0:T(8,128)(2,1)S(1)}, u32[]{:S(2)}, u32[]{:S(2)}) %collective-permute-start.31) | collective-permute-done | bytes 327712 | tf_op jit(solution)/shard_map/ppermute | solution.py:29
  145.5 3.8 collective-permute-done.27.refs_5_.refs_2_
  152.7 15.1 %collective-permute-done.28.refs_6_.refs_3_ = bf16[128,960]{1,0:T(8,128)(2,1)S(1)} collective-permute-done((bf16[128,960]{1,0:T(8,128)(2,1)S(1)}, bf16[128,960]{1,0:T(8,128)(2,1)S(1)}, u32[]{:S(2)}, u32[]{:S(2)}) %collective-permute-start.28) | collective-permute-done | bytes 245792 | tf_op jit(solution)/shard_map/ppermute | solution.py:29
  169.5 10.6 %shard_map.235 = (bf16[512,640]{1,0:T(8,128)(2,1)}, bf16[512,1280]{1,0:T(8,128)(2,1)}, f32[128,1024]{1,0:T(8,128)}, bf16[128,1024]{1,0:T(8,128)(2,1)}, bf16[128,...) custom-call(bf16[128,1024]{1,0:T(8,128)(2,1)} %copy-done.12, bf16[128,1024]{1,0:T(8,128)(2,1)} %copy-done.13, ...), custom_call_target="tpu_custom_call" | custom-call | tf_op jit(solution)/shard_map/pallas_call | solution.py:110
  183.8 6.7 %collective-permute-done.46 = bf16[128,1024]{1,0:T(8,128)(2,1)S(1)} collective-permute-done((bf16[128,1024]{1,0:T(8,128)(2,1)}, bf16[128,1024]{1,0:T(8,128)(2,1)S(1)}, u32[]{:S(2)}, u32[]{:S(2)}) %collective-permute-start.46) | collective-permute-done | bytes 262176 | tf_op jit(solution)/shard_map/ppermute | solution.py:29
  196.5 4.6 %shard_map.250 = (f32[512,1280]{1,0:T(8,128)}, bf16[512,1280]{1,0:T(8,128)(2,1)}) custom-call(bf16[128,1024]{1,0:T(8,128)(2,1)} %copy-done.12, bf16[128,1024]{1,0:T(8,128)(2,1)} %copy-done.13, bf16[128,1024]{1,0:T(8,128)(2,1)} %copy-done.14, bf16[128,1024]{1,0:T(8,128)(2,1)} %copy-done.15, bf16[512,1280]{1,0:T(8,128)(2,1)} %get-tuple-element.144.refs_4_), custom_call_target="tpu_custom_call" | custom-call | tf_op jit(solution)/shard_map/pallas_call | solution.py:110
  202.3 5.7 %shard_map.236 = (f32[128,960]{1,0:T(8,128)}, bf16[128,960]{1,0:T(8,128)(2,1)}, bf16[128,960]{1,0:T(8,128)(2,1)}, bf16[128,960]{1,0:T(8,128)(2,1)}, f32[128,960]{1,0:T(8,128)}, /*index=5*/f32[128,960]{1,0:T(8,128)}) custom-call(bf16[128,960]{1,0:T(8,128)(2,1)} %copy-done.20, bf16[128,960]{1,0:T(8,128)(2,1)} %copy-done.41, ...), custom_call_target="tpu_custom_call" | custom-call | tf_op jit(solution)/shard_map/pallas_call | solution.py:110
  208.0 3.7 shard_map.252
  214.0 8.3 %shard_map.237 = (f32[128,960]{1,0:T(8,128)}, bf16[128,640]{1,0:T(8,128)(2,1)}, bf16[128,640]{1,0:T(8,128)(2,1)}, bf16[128,640]{1,0:T(8,128)(2,1)}, bf16[128,640]{1,0:T(8,128)(2,1)}, /*index=5*/f32[128,640]{1,0:T(8,128)}) custom-call(bf16[128,960]{1,0:T(8,128)(2,1)} %get-tuple-element.89.query_ref, s32[128,1]{1,0:T(8,128)} %copy.61.position_ref, ...), custom_call_target="tpu_custom_call" | custom-call | tf_op jit(solution)/shard_map/pallas_call | solution.py:110
  227.5 5.5 %collective-permute-done.53.refs_2_ = bf16[128,640]{1,0:T(8,128)(2,1)S(1)} collective-permute-done((bf16[128,640]{1,0:T(8,128)(2,1)}, bf16[128,640]{1,0:T(8,128)(2,1)S(1)}, u32[]{:S(2)}, u32[]{:S(2)}) %collective-permute-start.53) | collective-permute-done | bytes 163872 | tf_op jit(solution)/shard_map/ppermute | solution.py:35
  236.0 6.5 %collective-permute-start.70 = (bf16[128,960]{1,0:T(8,128)(2,1)}, bf16[128,960]{1,0:T(8,128)(2,1)}, u32[]{:S(2)}, u32[]{:S(2)}) collective-permute-start(bf16[128,960]{1,0:T(8,128)(2,1)} %get-tuple-element.135), channel_id=1, source_target_pairs={{0,4},{1,5},{2,6},{3,7},{4,0},{5,1},{6,2},{7,3},{8,12},{9,13},{10,... | collective-permute-start | bytes 737288 | tf_op jit(solution)/shard_map/ppermute | solution.py:29
  245.7 4.9 %collective-permute-start.71 = (bf16[128,960]{1,0:T(8,128)(2,1)}, bf16[128,960]{1,0:T(8,128)(2,1)}, u32[]{:S(2)}, u32[]{:S(2)}) collective-permute-start(bf16[128,960]{1,0:T(8,128)(2,1)} %get-tuple-element.136), channel_id=1, source_target_pairs={{0,6},{1,7},{2,4},{3,5},{4,2},{5,3},{6,0},{7,1},{8,14},{9,15},{10,... | collective-permute-start | bytes 737288 | tf_op jit(solution)/shard_map/ppermute | solution.py:29
  250.6 3.4 shard_map.251
  262.4 19.9 %collective-permute-done.80.refs_1_ = bf16[80,960]{1,0:T(8,128)(2,1)S(1)} collective-permute-done((bf16[80,960]{1,0:T(8,128)(2,1)}, bf16[80,960]{1,0:T(8,128)(2,1)S(1)}, u32[]{:S(2)}, u32[]{:S(2)}) %collective-permute-start.80) | collective-permute-done | bytes 153632 | tf_op jit(solution)/shard_map/ppermute | solution.py:29
  286.5 6.5 %shard_map.240 = (f32[128,1600]{1,0:T(8,128)}, bf16[128,1600]{1,0:T(8,128)(2,1)}, bf16[128,1600]{1,0:T(8,128)(2,1)}, bf16[128,1600]{1,0:T(8,128)(2,1)}, f32[128,960]{1,0:T(8,128)}, /*index=5*/f32[128,960]{1,0:T(8,128)}) custom-call(bf16[128,1600]{1,0:T(8,128)(2,1)} %shard_map.239.refs_0_, bf16[128,1600]{1,0:T(8,128)(2,1)} %copy-done.28, ...), custom_call_target="tpu_custom_call" | custom-call | tf_op jit(solution)/shard_map/pallas_call | solution.py:110
  295.0 4.8 %collective-permute-done.81.refs_2_ = bf16[80,960]{1,0:T(8,128)(2,1)S(1)} collective-permute-done((bf16[80,960]{1,0:T(8,128)(2,1)}, bf16[80,960]{1,0:T(8,128)(2,1)S(1)}, u32[]{:S(2)}, u32[]{:S(2)}) %collective-permute-start.81) | collective-permute-done | bytes 153632 | tf_op jit(solution)/shard_map/ppermute | solution.py:29
  299.9 3.6 collective-permute-start.73
  314.5 3.5 shard_map.238
  337.9 8.0 %collective-permute-done.59.refs_1_ = f32[2,960]{1,0:T(2,128)S(1)} collective-permute-done((f32[2,960]{1,0:T(2,128)}, f32[2,960]{1,0:T(2,128)S(1)}, u32[]{:S(2)}, u32[]{:S(2)}) %collective-permute-start.59) | collective-permute-done | bytes 7712 | tf_op jit(solution)/shard_map/ppermute | solution.py:29
  347.8 3.4 collective-permute-start.50
  351.2 5.0 %collective-permute-done.64.refs_2_ = bf16[128,1600]{1,0:T(8,128)(2,1)S(1)} collective-permute-done((bf16[128,1600]{1,0:T(8,128)(2,1)}, bf16[128,1600]{1,0:T(8,128)(2,1)S(1)}, u32[]{:S(2)}, u32[]{:S(2)}) %collective-permute-start.64) | collective-permute-done | bytes 409632 | tf_op jit(solution)/shard_map/ppermute | solution.py:29
  (401 shorter events, 179.3 us)
Async XLA Ops:
  14.2 34.6 %collective-permute-start.15 = (bf16[32,1280]{1,0:T(8,128)(2,1)}, bf16[32,1280]{1,0:T(8,128)(2,1)}, u32[]{:S(2)}, u32[]{:S(2)}) collective-permute-start(bf16[32,1280]{1,0:T(8,128)(2,1)} %get-tuple-element.222), channel_id=1, source_target_pairs={{0,6},{1,7},{2,4},{3,5},{4,2},{5,3},{6,0},{7,1},{8,14},{9,15},{10,... | collective-permute-start | bytes 245768 | tf_op jit(solution)/shard_map/ppermute | solution.py:29
  19.1 21.5 %collective-permute-start.5 = (bf16[128,1600]{1,0:T(8,128)(2,1)S(1)}, bf16[128,1600]{1,0:T(8,128)(2,1)S(1)}, u32[]{:S(2)}, u32[]{:S(2)}) collective-permute-start(bf16[128,1600]{1,0:T(8,128)(2,1)S(1)} %pad_maximum_fusion.refs_3_.refs_4_), channel_id=1, source_target_pairs={{0,4},{1,5},{2,6},{3,7},{4,0},{5,1},{6,2},{7,3},{8,12},{9,13},{10,... | collective-permute-start | bytes 1228808 | tf_op jit(solution)/shard_map/ppermute | solution.py:29
  20.7 21.4 %collective-permute-start.6 = (bf16[128,1600]{1,0:T(8,128)(2,1)S(1)}, bf16[128,1600]{1,0:T(8,128)(2,1)S(1)}, u32[]{:S(2)}, u32[]{:S(2)}) collective-permute-start(bf16[128,1600]{1,0:T(8,128)(2,1)S(1)} %pad_maximum_fusion.refs_3_.refs_4_), channel_id=1, source_target_pairs={{0,6},{1,7},{2,4},{3,5},{4,2},{5,3},{6,0},{7,1},{8,14},{9,15},{10,... | collective-permute-start | bytes 1228808 | tf_op jit(solution)/shard_map/ppermute | solution.py:29
  22.8 26.0 %collective-permute-start.14 = (bf16[32,1280]{1,0:T(8,128)(2,1)S(1)}, bf16[32,1280]{1,0:T(8,128)(2,1)S(1)}, u32[]{:S(2)}, u32[]{:S(2)}) collective-permute-start(bf16[32,1280]{1,0:T(8,128)(2,1)S(1)} %get-tuple-element.220), channel_id=1, source_target_pairs={{0,4},{1,5},{2,6},{3,7},{4,0},{5,1},{6,2},{7,3},{8,12},{9,13},{10,... | collective-permute-start | bytes 245768 | tf_op jit(solution)/shard_map/ppermute | solution.py:29
  56.3 19.2 %collective-permute-start.17 = (bf16[32,960]{1,0:T(8,128)(2,1)S(1)}, bf16[32,960]{1,0:T(8,128)(2,1)S(1)}, u32[]{:S(2)}, u32[]{:S(2)}) collective-permute-start(bf16[32,960]{1,0:T(8,128)(2,1)S(1)} %pad.14), channel_id=1, source_target_pairs={{0,8},{1,9},{2,10},{3,11},{4,12},{5,13},{6,14},{7,15},{8,0},{9,1},... | collective-permute-start | bytes 184328 | tf_op jit(solution)/shard_map/ppermute | solution.py:29
  97.5 21.1 %collective-permute-start.23 = (f32[128,960]{1,0:T(8,128)}, f32[128,960]{1,0:T(8,128)S(1)}, u32[]{:S(2)}, u32[]{:S(2)}) collective-permute-start(f32[128,960]{1,0:T(8,128)} %get-tuple-element.95), channel_id=1, source_target_pairs={{0,1},{1,0},{2,3},{3,2},{4,5},{5,4},{6,7},{7,6},{8,9},{9,8},{10,11... | collective-permute-start | bytes 1474568 | tf_op jit(solution)/shard_map/ppermute | solution.py:29
  102.0 19.6 %collective-permute-start.30 = (bf16[128,1280]{1,0:T(8,128)(2,1)S(1)}, bf16[128,1280]{1,0:T(8,128)(2,1)S(1)}, u32[]{:S(2)}, u32[]{:S(2)}) collective-permute-start(bf16[128,1280]{1,0:T(8,128)(2,1)S(1)} %pad_maximum_fusion.2.refs_8_), channel_id=1, source_target_pairs={{0,8},{1,9},{2,10},{3,11},{4,12},{5,13},{6,14},{7,15},{8,0},{9,1},... | collective-permute-start | bytes 983048 | tf_op jit(solution)/shard_map/ppermute | solution.py:29
  107.6 31.9 %collective-permute-start.31 = (bf16[128,1280]{1,0:T(8,128)(2,1)S(1)}, bf16[128,1280]{1,0:T(8,128)(2,1)S(1)}, u32[]{:S(2)}, u32[]{:S(2)}) collective-permute-start(bf16[128,1280]{1,0:T(8,128)(2,1)S(1)} %pad_maximum_fusion.2.refs_8_), channel_id=1, source_target_pairs={{0,16},{1,17},{2,18},{3,19},{4,20},{5,21},{6,22},{7,23},{8,24},{9,... | collective-permute-start | bytes 983048 | tf_op jit(solution)/shard_map/ppermute | solution.py:29
  115.0 24.5 %collective-permute-start.32 = (bf16[128,1280]{1,0:T(8,128)(2,1)S(1)}, bf16[128,1280]{1,0:T(8,128)(2,1)S(1)}, u32[]{:S(2)}, u32[]{:S(2)}) collective-permute-start(bf16[128,1280]{1,0:T(8,128)(2,1)S(1)} %pad_maximum_fusion.2.refs_8_), channel_id=1, source_target_pairs={{0,24},{1,25},{2,26},{3,27},{4,28},{5,29},{6,30},{7,31},{8,16},{9,... | collective-permute-start | bytes 983048 | tf_op jit(solution)/shard_map/ppermute | solution.py:29
  120.3 20.7 %collective-permute-start.33 = (bf16[128,1280]{1,0:T(8,128)(2,1)S(1)}, bf16[128,1280]{1,0:T(8,128)(2,1)S(1)}, u32[]{:S(2)}, u32[]{:S(2)}) collective-permute-start(bf16[128,1280]{1,0:T(8,128)(2,1)S(1)} %pad_maximum_fusion.2.refs_8_), channel_id=1, source_target_pairs={{0,1},{1,0},{2,3},{3,2},{4,5},{5,4},{6,7},{7,6},{8,9},{9,8},{10,11... | collective-permute-start | bytes 983048 | tf_op jit(solution)/shard_map/ppermute | solution.py:29
  120.6 19.5 %collective-permute-start.43 = (bf16[80,960]{1,0:T(8,128)(2,1)}, bf16[80,960]{1,0:T(8,128)(2,1)}, u32[]{:S(2)}, u32[]{:S(2)}) collective-permute-start(bf16[80,960]{1,0:T(8,128)(2,1)} %copy-done.43), channel_id=1, source_target_pairs={{0,1},{1,0},{2,3},{3,2},{4,5},{5,4},{6,7},{7,6},{8,9},{9,8},{10,11... | collective-permute-start | bytes 460808 | tf_op jit(solution)/shard_map/ppermute | solution.py:29
  121.5 21.6 %collective-permute-start.34 = (bf16[128,1280]{1,0:T(8,128)(2,1)S(1)}, bf16[128,1280]{1,0:T(8,128)(2,1)S(1)}, u32[]{:S(2)}, u32[]{:S(2)}) collective-permute-start(bf16[128,1280]{1,0:T(8,128)(2,1)S(1)} %collective-permute-done.30.refs_9_), channel_id=1, source_target_pairs={{0,1},{1,0},{2,3},{3,2},{4,5},{5,4},{6,7},{7,6},{8,9},{9,8},{10,11... | collective-permute-start | bytes 983048 | tf_op jit(solution)/shard_map/ppermute | solution.py:29
  141.1 26.7 %collective-permute-start.24 = (bf16[128,1024]{1,0:T(8,128)(2,1)S(1)}, bf16[128,1024]{1,0:T(8,128)(2,1)S(1)}, u32[]{:S(2)}, u32[]{:S(2)}) collective-permute-start(bf16[128,1024]{1,0:T(8,128)(2,1)S(1)} %fusion.8.refs_0_), channel_id=1, source_target_pairs={{0,2},{1,3},{2,0},{3,1},{4,6},{5,7},{6,4},{7,5},{8,10},{9,11},{10,... | collective-permute-start | bytes 786440 | tf_op jit(solution)/shard_map/ppermute | solution.py:29
  143.1 24.7 %collective-permute-start.25 = (bf16[128,1024]{1,0:T(8,128)(2,1)S(1)}, bf16[128,1024]{1,0:T(8,128)(2,1)S(1)}, u32[]{:S(2)}, u32[]{:S(2)}) collective-permute-start(bf16[128,1024]{1,0:T(8,128)(2,1)S(1)} %fusion.8.refs_0_), channel_id=1, source_target_pairs={{0,4},{1,5},{2,6},{3,7},{4,0},{5,1},{6,2},{7,3},{8,12},{9,13},{10,... | collective-permute-start | bytes 786440 | tf_op jit(solution)/shard_map/ppermute | solution.py:29
  143.3 24.5 %collective-permute-start.26 = (bf16[128,1024]{1,0:T(8,128)(2,1)S(1)}, bf16[128,1024]{1,0:T(8,128)(2,1)S(1)}, u32[]{:S(2)}, u32[]{:S(2)}) collective-permute-start(bf16[128,1024]{1,0:T(8,128)(2,1)S(1)} %fusion.8.refs_0_), channel_id=1, source_target_pairs={{0,6},{1,7},{2,4},{3,5},{4,2},{5,3},{6,0},{7,1},{8,14},{9,15},{10,... | collective-permute-start | bytes 786440 | tf_op jit(solution)/shard_map/ppermute | solution.py:29
  144.8 23.0 %collective-permute-start.28 = (bf16[128,960]{1,0:T(8,128)(2,1)S(1)}, bf16[128,960]{1,0:T(8,128)(2,1)S(1)}, u32[]{:S(2)}, u32[]{:S(2)}) collective-permute-start(bf16[128,960]{1,0:T(8,128)(2,1)S(1)} %copy.65.refs_4_.refs_1_), channel_id=1, source_target_pairs={{0,4},{1,5},{2,6},{3,7},{4,0},{5,1},{6,2},{7,3},{8,12},{9,13},{10,... | collective-permute-start | bytes 737288 | tf_op jit(solution)/shard_map/ppermute | solution.py:29
  201.1 44.6 %collective-permute-start.75 = (bf16[512,1280]{1,0:T(8,128)(2,1)}, bf16[512,1280]{1,0:T(8,128)(2,1)S(1)}, u32[]{:S(2)}, u32[]{:S(2)}) collective-permute-start(bf16[512,1280]{1,0:T(8,128)(2,1)} %get-tuple-element.146), channel_id=1, source_target_pairs={{0,1},{1,0},{2,3},{3,2},{4,5},{5,4},{6,7},{7,6},{8,9},{9,8},{10,11... | collective-permute-start | bytes 3932168 | tf_op jit(solution)/shard_map/ppermute | solution.py:29
  211.7 42.2 %collective-permute-start.79 = (bf16[320,960]{1,0:T(8,128)(2,1)}, bf16[320,960]{1,0:T(8,128)(2,1)S(1)}, u32[]{:S(2)}, u32[]{:S(2)}) collective-permute-start(bf16[320,960]{1,0:T(8,128)(2,1)} %get-tuple-element.152), channel_id=1, source_target_pairs={{0,1},{1,0},{2,3},{3,2},{4,5},{5,4},{6,7},{7,6},{8,9},{9,8},{10,11... | collective-permute-start | bytes 1843208 | tf_op jit(solution)/shard_map/ppermute | solution.py:29
  233.0 23.5 %collective-permute-start.69 = (bf16[128,960]{1,0:T(8,128)(2,1)}, bf16[128,960]{1,0:T(8,128)(2,1)}, u32[]{:S(2)}, u32[]{:S(2)}) collective-permute-start(bf16[128,960]{1,0:T(8,128)(2,1)} %get-tuple-element.134), channel_id=1, source_target_pairs={{0,2},{1,3},{2,0},{3,1},{4,6},{5,7},{6,4},{7,5},{8,10},{9,11},{10,... | collective-permute-start | bytes 737288 | tf_op jit(solution)/shard_map/ppermute | solution.py:29
  236.0 21.2 %collective-permute-start.70 = (bf16[128,960]{1,0:T(8,128)(2,1)}, bf16[128,960]{1,0:T(8,128)(2,1)}, u32[]{:S(2)}, u32[]{:S(2)}) collective-permute-start(bf16[128,960]{1,0:T(8,128)(2,1)} %get-tuple-element.135), channel_id=1, source_target_pairs={{0,4},{1,5},{2,6},{3,7},{4,0},{5,1},{6,2},{7,3},{8,12},{9,13},{10,... | collective-permute-start | bytes 737288 | tf_op jit(solution)/shard_map/ppermute | solution.py:29
  245.2 39.6 %collective-permute-start.56 = (bf16[128,1600]{1,0:T(8,128)(2,1)}, bf16[128,1600]{1,0:T(8,128)(2,1)S(1)}, u32[]{:S(2)}, u32[]{:S(2)}) collective-permute-start(bf16[128,1600]{1,0:T(8,128)(2,1)} %shard_map.239.refs_0_), channel_id=1, source_target_pairs={{0,1},{1,0},{2,3},{3,2},{4,5},{5,4},{6,7},{7,6},{8,9},{9,8},{10,11... | collective-permute-start | bytes 1228808 | tf_op jit(solution)/shard_map/ppermute | solution.py:29
  253.9 49.6 %collective-permute-start.76 = (bf16[128,1280]{1,0:T(8,128)(2,1)}, bf16[128,1280]{1,0:T(8,128)(2,1)S(1)}, u32[]{:S(2)}, u32[]{:S(2)}) collective-permute-start(bf16[128,1280]{1,0:T(8,128)(2,1)} %get-tuple-element.148), channel_id=1, source_target_pairs={{0,8},{1,9},{2,10},{3,11},{4,12},{5,13},{6,14},{7,15},{8,0},{9,1},... | collective-permute-start | bytes 983048 | tf_op jit(solution)/shard_map/ppermute | solution.py:29
  256.5 47.0 %collective-permute-start.77 = (bf16[128,1280]{1,0:T(8,128)(2,1)}, bf16[128,1280]{1,0:T(8,128)(2,1)S(1)}, u32[]{:S(2)}, u32[]{:S(2)}) collective-permute-start(bf16[128,1280]{1,0:T(8,128)(2,1)} %get-tuple-element.149), channel_id=1, source_target_pairs={{0,16},{1,17},{2,18},{3,19},{4,20},{5,21},{6,22},{7,23},{8,24},{9,... | collective-permute-start | bytes 983048 | tf_op jit(solution)/shard_map/ppermute | solution.py:29
  257.2 46.3 %collective-permute-start.78 = (bf16[128,1280]{1,0:T(8,128)(2,1)}, bf16[128,1280]{1,0:T(8,128)(2,1)S(1)}, u32[]{:S(2)}, u32[]{:S(2)}) collective-permute-start(bf16[128,1280]{1,0:T(8,128)(2,1)} %get-tuple-element.150), channel_id=1, source_target_pairs={{0,24},{1,25},{2,26},{3,27},{4,28},{5,29},{6,30},{7,31},{8,16},{9,... | collective-permute-start | bytes 983048 | tf_op jit(solution)/shard_map/ppermute | solution.py:29
  261.4 20.9 %collective-permute-start.80 = (bf16[80,960]{1,0:T(8,128)(2,1)}, bf16[80,960]{1,0:T(8,128)(2,1)S(1)}, u32[]{:S(2)}, u32[]{:S(2)}) collective-permute-start(bf16[80,960]{1,0:T(8,128)(2,1)} %get-tuple-element.153), channel_id=1, source_target_pairs={{0,8},{1,9},{2,10},{3,11},{4,12},{5,13},{6,14},{7,15},{8,0},{9,1},... | collective-permute-start | bytes 460808 | tf_op jit(solution)/shard_map/ppermute | solution.py:29
  318.5 32.6 %collective-permute-start.63 = (bf16[128,1600]{1,0:T(8,128)(2,1)}, bf16[128,1600]{1,0:T(8,128)(2,1)}, u32[]{:S(2)}, u32[]{:S(2)}) collective-permute-start(bf16[128,1600]{1,0:T(8,128)(2,1)} %get-tuple-element.123), channel_id=1, source_target_pairs={{0,2},{1,3},{2,0},{3,1},{4,6},{5,7},{6,4},{7,5},{8,10},{9,11},{10,... | collective-permute-start | bytes 1228808 | tf_op jit(solution)/shard_map/ppermute | solution.py:29
  325.9 30.3 %collective-permute-start.64 = (bf16[128,1600]{1,0:T(8,128)(2,1)}, bf16[128,1600]{1,0:T(8,128)(2,1)S(1)}, u32[]{:S(2)}, u32[]{:S(2)}) collective-permute-start(bf16[128,1600]{1,0:T(8,128)(2,1)} %get-tuple-element.124), channel_id=1, source_target_pairs={{0,4},{1,5},{2,6},{3,7},{4,0},{5,1},{6,2},{7,3},{8,12},{9,13},{10,... | collective-permute-start | bytes 1228808 | tf_op jit(solution)/shard_map/ppermute | solution.py:29
  327.5 35.3 %collective-permute-start.65 = (bf16[128,1600]{1,0:T(8,128)(2,1)}, bf16[128,1600]{1,0:T(8,128)(2,1)}, u32[]{:S(2)}, u32[]{:S(2)}) collective-permute-start(bf16[128,1600]{1,0:T(8,128)(2,1)} %get-tuple-element.125), channel_id=1, source_target_pairs={{0,6},{1,7},{2,4},{3,5},{4,2},{5,3},{6,0},{7,1},{8,14},{9,15},{10,... | collective-permute-start | bytes 1228808 | tf_op jit(solution)/shard_map/ppermute | solution.py:29
  329.0 18.8 %collective-permute-start.86 = (bf16[80,960]{1,0:T(8,128)(2,1)}, bf16[80,960]{1,0:T(8,128)(2,1)}, u32[]{:S(2)}, u32[]{:S(2)}) collective-permute-start(bf16[80,960]{1,0:T(8,128)(2,1)} %convert_element_type.117), channel_id=1, source_target_pairs={{0,0},{1,1},{2,8},{3,9},{4,16},{5,17},{6,24},{7,25},{8,2},{9,3},{1... | collective-permute-start | bytes 460808 | tf_op jit(solution)/shard_map/ppermute | solution.py:739
  345.9 28.0 %collective-permute-start.51 = (bf16[128,960]{1,0:T(8,128)(2,1)}, bf16[128,960]{1,0:T(8,128)(2,1)S(1)}, u32[]{:S(2)}, u32[]{:S(2)}) collective-permute-start(bf16[128,960]{1,0:T(8,128)(2,1)} %get-tuple-element.113), channel_id=1, source_target_pairs={{0,6},{1,7},{2,4},{3,5},{4,2},{5,3},{6,0},{7,1},{8,14},{9,15},{10,... | collective-permute-start | bytes 737288 | tf_op jit(solution)/shard_map/ppermute | solution.py:29
  347.8 28.9 %collective-permute-start.50 = (bf16[128,960]{1,0:T(8,128)(2,1)}, bf16[128,960]{1,0:T(8,128)(2,1)}, u32[]{:S(2)}, u32[]{:S(2)}) collective-permute-start(bf16[128,960]{1,0:T(8,128)(2,1)} %get-tuple-element.112), channel_id=1, source_target_pairs={{0,4},{1,5},{2,6},{3,7},{4,0},{5,1},{6,2},{7,3},{8,12},{9,13},{10,... | collective-permute-start | bytes 737288 | tf_op jit(solution)/shard_map/ppermute | solution.py:29
  351.2 25.6 %collective-permute-start.49 = (bf16[128,960]{1,0:T(8,128)(2,1)}, bf16[128,960]{1,0:T(8,128)(2,1)}, u32[]{:S(2)}, u32[]{:S(2)}) collective-permute-start(bf16[128,960]{1,0:T(8,128)(2,1)} %get-tuple-element.111), channel_id=1, source_target_pairs={{0,2},{1,3},{2,0},{3,1},{4,6},{5,7},{6,4},{7,5},{8,10},{9,11},{10,... | collective-permute-start | bytes 737288 | tf_op jit(solution)/shard_map/ppermute | solution.py:29
  (133 other events, 1514.8 us)

commit v5 on v4

--- a/solution.py
+++ b/solution.py
@@ -106,9 +106,10 @@
     )
 
 
-def kernel_call(body, outs, operands):
+def kernel_call(body, outs, operands, scratch=()):
     return pl.pallas_call(
         body,
+        scratch_shapes=list(scratch),
         out_shape=[jax.ShapeDtypeStruct(shape, dtype) for shape, dtype in outs],
         compiler_params=pltpu.CompilerParams(vmem_limit_bytes=60 * 1024 * 1024),
     )(*operands)
@@ -234,7 +235,6 @@
     rows = tokens[0].shape[0]
     count = len(tokens)
     width = pieces[0].shape[1]
-    depth = pieces[0].shape[0]
 
     def body(*refs):
         select_ref = refs[count]
@@ -243,9 +243,7 @@
         tokens_all = jnp.concatenate([refs[i][...] for i in range(count)], axis=0)
         placed = product(tokens_all, select_ref[...], 1, 0).astype(jnp.bfloat16)
         outs[count][...] = placed
-        total = product(placed[:, :depth], weights[0][...], 1, 0)
-        for j in range(1, len(pieces)):
-            total += product(placed[:, j * depth : (j + 1) * depth], weights[j][...], 1, 0)
+        total = product(placed, jnp.concatenate([w[...] for w in weights], axis=0), 1, 0)
         for i in range(count):
             outs[i][...] = total[i * rows : (i + 1) * rows]
 
@@ -267,16 +265,14 @@
         weights = refs[count + 2 : count + 2 + len(pieces)]
         outs = refs[count + 2 + len(pieces) :]
         grads_all = jnp.concatenate([refs[i][...] for i in range(count)], axis=0)
-        total = None
+        grad_rows = product(placed_ref[...], grads_all, 0, 0)
         for j in range(len(pieces)):
-            span = slice(j * depth, (j + 1) * depth)
-            outs[j][...] = product(placed_ref[:, span], grads_all, 0, 0).astype(outs[j].dtype)
-            back = product(grads_all, weights[j][...], 1, 1)
-            high = back.astype(jnp.bfloat16)
-            rest = (back - high.astype(jnp.float32)).astype(jnp.bfloat16)
-            chosen = select_ref[:, span]
-            part = product(high, chosen, 1, 1) + product(rest, chosen, 1, 1)
-            total = part if total is None else total + part
+            outs[j][...] = grad_rows[j * depth : (j + 1) * depth].astype(outs[j].dtype)
+        back = product(grads_all, jnp.concatenate([w[...] for w in weights], axis=0), 1, 1)
+        high = back.astype(jnp.bfloat16)
+        rest = (back - high.astype(jnp.float32)).astype(jnp.bfloat16)
+        both = product(jnp.concatenate([high, rest], axis=0), select_ref[...], 1, 1)
+        total = both[: count * rows] + both[count * rows :]
         for i in range(count):
             outs[len(pieces) + i][...] = total[i * rows : (i + 1) * rows]
 
@@ -290,7 +286,7 @@
     count = len(normed_blocks)
     rows, features = normed_blocks[0].shape
     total_rows = count * rows
-    depth, both = pair_pieces[0].shape
+    both = pair_pieces[0].shape[1]
     width = both // 2
     pair_count = len(pair_pieces)
 
@@ -300,9 +296,8 @@
         hidden_out, low_out, *back_outs = refs[2 * count + pair_count + 1 :]
         placed = jnp.concatenate([refs[i][...] for i in range(count)], axis=0)
         grads = jnp.concatenate([refs[count + i][...] for i in range(count)], axis=0)
-        total = product(placed[:, :depth], weights[0][...], 1, 0)
-        for j in range(1, pair_count):
-            total += product(placed[:, j * depth : (j + 1) * depth], weights[j][...], 1, 0)
+        whole = jnp.concatenate([w[...] for w in weights], axis=0)
+        total = product(placed, whole, 1, 0)
         gate_pre = total[:, :width]
         up_pre = total[:, width:]
         sigmoid_gate = 1.0 / (1.0 + jnp.exp(-gate_pre))
@@ -314,11 +309,9 @@
         ).astype(jnp.bfloat16)
         low_out[:, width:] = (grad_hidden * silu_gate).astype(jnp.bfloat16)
         low = low_out[...]
-        for j in range(pair_count):
-            back = product(low, weights[j][...], 1, 1)
-            for i in range(count):
-                part = back[i * rows : (i + 1) * rows]
-                back_outs[i][:, j * depth : (j + 1) * depth] = part.astype(back_outs[i].dtype)
+        back = product(low, whole, 1, 1)
+        for i in range(count):
+            back_outs[i][...] = back[i * rows : (i + 1) * rows].astype(back_outs[i].dtype)
 
     outs = [((total_rows, width), jnp.bfloat16), ((total_rows, both), jnp.bfloat16)]
     outs += [((rows, features), jnp.float32 if i == 0 else LINK) for i in range(count)]
@@ -443,45 +436,58 @@
 
     def body(query_ref, position_ref, log_ref, attended_ref, grad_ref, *refs):
         window_refs = refs[:count]
-        query_out, *window_outs = refs[count:]
-        window = jnp.concatenate([ref[...] for ref in window_refs], axis=0)
+        query_out, *window_outs = refs[count:-7]
+        queries, outputs, grads, keys, values, query_grads, pair_grads = refs[-7:]
         allowed = allowed_pairs(position_ref, row_count, key_count, prefix)
         fill = jnp.where(allowed, 0.0, NEG_FILL)
         fill = jnp.concatenate([fill] * group_size, axis=0)
-        query_columns = []
-        key_columns = []
-        value_columns = []
         for g in range(KV_HEADS):
             span = slice(g * HEAD_DIM, (g + 1) * HEAD_DIM)
-            keys = window[:, span]
-            values = window[:, k_width + g * HEAD_DIM : k_width + (g + 1) * HEAD_DIM]
-            queries = group_rows(query_ref, g, group_size)
-            grads = group_rows(grad_ref, g, group_size)
-            outputs = group_rows(attended_ref, g, group_size)
-            scores = product(queries, keys, 1, 1)
+            value_span = slice(k_width + g * HEAD_DIM, k_width + (g + 1) * HEAD_DIM)
+            queries[g] = group_rows(query_ref, g, group_size)
+            outputs[g] = group_rows(attended_ref, g, group_size)
+            grads[g] = group_rows(grad_ref, g, group_size)
+            keys[g] = jnp.concatenate([ref[:, span] for ref in window_refs], axis=0)
+            values[g] = jnp.concatenate([ref[:, value_span] for ref in window_refs], axis=0)
+
+        def one_group(g, carry):
+            scores = product(queries[g], keys[g], 1, 1)
             scores = jnp.where(fill < 0.0, NEG_FILL, scores * HEAD_DIM ** (-0.5))
             prob_full = jnp.exp(scores - log_ref[g])
-            grad_prob = product(grads, values, 1, 1)
+            grad_prob = product(grads[g], values[g], 1, 1)
             delta_sum = jnp.sum(
-                grads.astype(jnp.float32) * outputs.astype(jnp.float32), axis=1, keepdims=True
+                grads[g].astype(jnp.float32) * outputs[g].astype(jnp.float32),
+                axis=1,
+                keepdims=True,
             )
             grad_score = (prob_full * (grad_prob - delta_sum) * HEAD_DIM ** (-0.5)).astype(
                 jnp.bfloat16
             )
-            query_columns += side_by_side(product(grad_score, keys, 1, 0), row_count)
-            key_columns.append(product(grad_score, queries, 0, 0))
-            value_columns.append(product(prob_full.astype(jnp.bfloat16), grads, 0, 0))
-        query_out[...] = jnp.concatenate(query_columns, axis=1)
-        total = jnp.concatenate(key_columns + value_columns, axis=1)
+            query_grads[g] = product(grad_score, keys[g], 1, 0)
+            pair_grads[0, g] = product(grad_score, queries[g], 0, 0)
+            pair_grads[1, g] = product(prob_full.astype(jnp.bfloat16), grads[g], 0, 0)
+            return carry
+
+        lax.fori_loop(0, KV_HEADS, one_group, 0)
+        columns = []
+        for g in range(KV_HEADS):
+            columns += side_by_side(query_grads[g], row_count)
+        query_out[...] = jnp.concatenate(columns, axis=1)
         for i, out in enumerate(window_outs):
-            out[...] = total[i * row_count : (i + 1) * row_count].astype(out.dtype)
+            span = slice(i * row_count, (i + 1) * row_count)
+            parts = [pair_grads[p, g, span, :] for p in range(2) for g in range(KV_HEADS)]
+            out[...] = jnp.concatenate(parts, axis=1).astype(out.dtype)
 
     outs = [((row_count, q_width), jnp.float32)]
     outs += [
         ((row_count, 2 * k_width), jnp.float32 if i == count - 1 else LINK) for i in range(count)
     ]
     operands = [query_block, position_block[:, None], log_total, attended_block, grad_block]
-    results = kernel_call(body, outs, operands + list(window_blocks))
+    heads = (KV_HEADS, group_size * row_count, HEAD_DIM)
+    window_heads = (KV_HEADS, key_count, HEAD_DIM)
+    scratch = [pltpu.VMEM(heads, jnp.bfloat16)] * 3 + [pltpu.VMEM(window_heads, jnp.bfloat16)] * 2
+    scratch += [pltpu.VMEM(heads, jnp.float32), pltpu.VMEM((2,) + window_heads, jnp.float32)]
+    results = kernel_call(body, outs, operands + list(window_blocks), scratch)
     return results[0], results[1:]
 
 
@@ -783,7 +789,10 @@
     grad_in = (grad_mid + grad_in_norm).astype(jnp.bfloat16)
     gains = jnp.stack([grad_gain_one, grad_gain_two])
     for bit in range(device_count.bit_length() - 1):
-        gains = reduce_split(gains, [swap(gains, 1 << bit)], 1)[0]
+        if bit < 1:
+            gains = reduce_split(gains, [swap(gains, 1 << bit)], 1)[0]
+        else:
+            gains = gains + swap(gains, 1 << bit)
     return (
         block_out,
         grad_in,

time: 397 us -> 385 us (0.970); the launches traced: 391 us -> 383 us
  Pallas kernels: 89.2 us -> 78.2 us
  waiting for transfers between devices: 126 us -> 131 us
    pallas_call x24 -> x20, Pallas kernels: 82.9 us -> 72 us  [kernel_call(): pl.pallas_call(body, scratch_shapes=list(scratch), out_shape=[jax.ShapeDt...]
    ppermute x77, waiting for transfers between devices: 121 us -> 126 us  [swap(): return lax.ppermute(block, AXIS, [(i, i ^ mask) for i in range(size)])]
    unnamed x160 -> x148, local copies, waits for them, and re-layouts: 13 us -> 11.8 us
  transfers between devices with their start and end apart: 87 -> 87, of which waited for: 24 -> 24; matrix products, arithmetic and copies ran while one was open for 10% -> 10% of each run, Pallas kernels for 19% -> 18%
where the time goes in v5:
time: 385 us; the launch traced here: 383 us
  waiting for transfers between devices  131 us (34%)
  starting transfers between devices  117 us (30%)
  Pallas kernels  78.2 us (20%)
  local copies, waits for them, and re-layouts  33.7 us (9%)
  other arithmetic  17.3 us (4%)
  matrix products  4.32 us (1%)
    ppermute x77, waiting for transfers between devices, swap(): return lax.ppermute(block, AXIS, [(i, i ^ mask) for i in range(size)])  126 us
    ppermute x77, starting transfers between devices, swap(): return lax.ppermute(block, AXIS, [(i, i ^ mask) for i in range(size)])  95 us
    pallas_call x20, Pallas kernels, kernel_call(): pl.pallas_call(body, scratch_shapes=list(scratch), out_shape=[jax.ShapeDt...  72 us
    ppermute x8, starting transfers between devices, passed_along(): return lax.ppermute(block, AXIS, route)  17.5 us
    unnamed x148, local copies, waits for them, and re-layouts  11.8 us
  transfers between devices with their start and end apart: 87, of which 24 were waited for; matrix products, arithmetic and copies ran while one was open for 10% of the time, Pallas kernels for 18%

profile of v5, /device:TPU:0, one launch (start us, length us, event | category | flops | bytes accessed | tf_op | source)
XLA Modules:
  0.0 382.9 jit_solution(4150415535425577935)
XLA Ops:
  3.4 5.1 %collective-permute-start.3 = (bf16[32,1600]{1,0:T(8,128)(2,1)S(1)}, bf16[32,1600]{1,0:T(8,128)(2,1)S(1)}, u32[]{:S(2)}, u32[]{:S(2)}) collective-permute-start(bf16[32,1600]{1,0:T(8,128)(2,1)S(1)} %pad.12), channel_id=1, source_target_pairs={{0,24},{1,25},{2,26},{3,27},{4,28},{5,29},{6,30},{7,31},{8,16},{9,... | collective-permute-start | bytes 307208 | tf_op jit(solution)/shard_map/ppermute | solution.py:29
  24.4 5.9 %collective-permute-done.4.refs_4_.refs_5_ = bf16[128,1600]{1,0:T(8,128)(2,1)S(1)} collective-permute-done((bf16[128,1600]{1,0:T(8,128)(2,1)S(1)}, bf16[128,1600]{1,0:T(8,128)(2,1)S(1)}, u32[]{:S(2)}, u32[]{:S(2)}) %collective-permute-start.4) | collective-permute-done | bytes 409632 | tf_op jit(solution)/shard_map/ppermute | solution.py:29
  31.8 8.8 %collective-permute-done.5.refs_5_.refs_6_ = bf16[128,1600]{1,0:T(8,128)(2,1)S(1)} collective-permute-done((bf16[128,1600]{1,0:T(8,128)(2,1)S(1)}, bf16[128,1600]{1,0:T(8,128)(2,1)S(1)}, u32[]{:S(2)}, u32[]{:S(2)}) %collective-permute-start.5) | collective-permute-done | bytes 409632 | tf_op jit(solution)/shard_map/ppermute | solution.py:29
  42.8 4.1 %shard_map.230 = (f32[128,1600]{1,0:T(8,128)}, f32[128,1600]{1,0:T(8,128)}, bf16[256,512]{1,0:T(8,128)(2,1)}) custom-call(bf16[128,960]{1,0:T(8,128)(2,1)} %copy-done.16, bf16[128,960]{1,0:T(8,128)(2,1)} %copy-done.39, bf16[960,512]{1,0:T(8,128)(2,1)} %fusion.6.refs_2_.refs_3_, bf16[128,1600]{1,0:T(8,128)(2,1)} %copy-done, bf16[128,1600]{1,0:T(8,128)(2,1)} %copy-done.4, ...), custom_call_target="tpu_custom_call" | custom-call | tf_op jit(solution)/shard_map/pallas_call | solution.py:110
  50.3 4.5 %collective-permute-start.19 = (bf16[32,960]{1,0:T(8,128)(2,1)S(1)}, bf16[32,960]{1,0:T(8,128)(2,1)S(1)}, u32[]{:S(2)}, u32[]{:S(2)}) collective-permute-start(bf16[32,960]{1,0:T(8,128)(2,1)S(1)} %pad.14), channel_id=1, source_target_pairs={{0,24},{1,25},{2,26},{3,27},{4,28},{5,29},{6,30},{7,31},{8,16},{9,... | collective-permute-start | bytes 184328 | tf_op jit(solution)/shard_map/ppermute | solution.py:29
  61.9 5.1 %collective-permute-start.8 = (bf16[128,640]{1,0:T(8,128)(2,1)}, bf16[128,640]{1,0:T(8,128)(2,1)S(1)}, u32[]{:S(2)}, u32[]{:S(2)}) collective-permute-start(bf16[128,640]{1,0:T(8,128)(2,1)} %get-tuple-element.90.refs_4_), channel_id=1, source_target_pairs={{0,4},{1,5},{2,6},{3,7},{4,8},{5,9},{6,10},{7,11},{8,12},{9,13},{1... | collective-permute-start | bytes 491528 | tf_op jit(solution)/shard_map/ppermute | solution.py:35
  79.9 5.7 %shard_map.232 = (bf16[128,960]{1,0:T(8,128)(2,1)}, f32[5,384,1]{2,1,0:T(8,128)}) custom-call(bf16[128,960]{1,0:T(8,128)(2,1)} %get-tuple-element.89.query_ref, s32[128,1]{1,0:T(8,128)} %copy.61.position_ref, bf16[128,640]{1,0:T(8,128)(2,1)} %copy-done.23, bf16[128,640]{1,0:T(8,128)(2,1)} %copy-done.24, bf16[128,640]{1,0:T(8,128)(2,1)} %copy-done.25, ...), custom_call_target="tpu_custom_call" | custom-call | tf_op jit(solution)/shard_map/pallas_call | solution.py:110
  85.8 5.1 %collective-permute-done.21.refs_5_.refs_6_ = bf16[128,960]{1,0:T(8,128)(2,1)S(1)} collective-permute-done((bf16[128,960]{1,0:T(8,128)(2,1)S(1)}, bf16[128,960]{1,0:T(8,128)(2,1)S(1)}, u32[]{:S(2)}, u32[]{:S(2)}) %collective-permute-start.21) | collective-permute-done | bytes 245792 | tf_op jit(solution)/shard_map/ppermute | solution.py:29
  93.0 3.5 shard_map.233
  102.4 4.6 %collective-permute-done.37.refs_1_ = bf16[80,960]{1,0:T(8,128)(2,1)S(1)} collective-permute-done((bf16[80,960]{1,0:T(8,128)(2,1)}, bf16[80,960]{1,0:T(8,128)(2,1)S(1)}, u32[]{:S(2)}, u32[]{:S(2)}) %collective-permute-start.37) | collective-permute-done | bytes 153632 | tf_op jit(solution)/shard_map/ppermute | solution.py:29
  108.8 5.4 %collective-permute-done.38.refs_2_ = bf16[80,960]{1,0:T(8,128)(2,1)} collective-permute-done((bf16[80,960]{1,0:T(8,128)(2,1)}, bf16[80,960]{1,0:T(8,128)(2,1)}, u32[]{:S(2)}, u32[]{:S(2)}) %collective-permute-start.38) | collective-permute-done | bytes 153632 | tf_op jit(solution)/shard_map/ppermute | solution.py:29
  120.8 18.0 %collective-permute-done.31.refs_10_ = bf16[128,1280]{1,0:T(8,128)(2,1)S(1)} collective-permute-done((bf16[128,1280]{1,0:T(8,128)(2,1)S(1)}, bf16[128,1280]{1,0:T(8,128)(2,1)S(1)}, u32[]{:S(2)}, u32[]{:S(2)}) %collective-permute-start.31) | collective-permute-done | bytes 327712 | tf_op jit(solution)/shard_map/ppermute | solution.py:29
  144.7 3.9 %collective-permute-done.27.refs_5_.refs_2_ = bf16[128,960]{1,0:T(8,128)(2,1)S(1)} collective-permute-done((bf16[128,960]{1,0:T(8,128)(2,1)S(1)}, bf16[128,960]{1,0:T(8,128)(2,1)S(1)}, u32[]{:S(2)}, u32[]{:S(2)}) %collective-permute-start.27) | collective-permute-done | bytes 245792 | tf_op jit(solution)/shard_map/ppermute | solution.py:29
  151.9 15.1 %collective-permute-done.28.refs_6_.refs_3_ = bf16[128,960]{1,0:T(8,128)(2,1)S(1)} collective-permute-done((bf16[128,960]{1,0:T(8,128)(2,1)S(1)}, bf16[128,960]{1,0:T(8,128)(2,1)S(1)}, u32[]{:S(2)}, u32[]{:S(2)}) %collective-permute-start.28) | collective-permute-done | bytes 245792 | tf_op jit(solution)/shard_map/ppermute | solution.py:29
  168.8 7.7 %shard_map.235 = (bf16[512,640]{1,0:T(8,128)(2,1)}, bf16[512,1280]{1,0:T(8,128)(2,1)}, f32[128,1024]{1,0:T(8,128)}, bf16[128,1024]{1,0:T(8,128)(2,1)}, bf16[128,...) custom-call(bf16[128,1024]{1,0:T(8,128)(2,1)} %copy-done.12, bf16[128,1024]{1,0:T(8,128)(2,1)} %copy-done.13, ...), custom_call_target="tpu_custom_call" | custom-call | tf_op jit(solution)/shard_map/pallas_call | solution.py:110
  180.2 6.6 %collective-permute-done.46 = bf16[128,1024]{1,0:T(8,128)(2,1)S(1)} collective-permute-done((bf16[128,1024]{1,0:T(8,128)(2,1)}, bf16[128,1024]{1,0:T(8,128)(2,1)S(1)}, u32[]{:S(2)}, u32[]{:S(2)}) %collective-permute-start.46) | collective-permute-done | bytes 262176 | tf_op jit(solution)/shard_map/ppermute | solution.py:29
  193.6 4.6 %shard_map.246 = (f32[512,1280]{1,0:T(8,128)}, bf16[512,1280]{1,0:T(8,128)(2,1)}) custom-call(bf16[128,1024]{1,0:T(8,128)(2,1)} %copy-done.12, bf16[128,1024]{1,0:T(8,128)(2,1)} %copy-done.13, bf16[128,1024]{1,0:T(8,128)(2,1)} %copy-done.14, bf16[128,1024]{1,0:T(8,128)(2,1)} %copy-done.15, bf16[512,1280]{1,0:T(8,128)(2,1)} %get-tuple-element.144.refs_4_), custom_call_target="tpu_custom_call" | custom-call | tf_op jit(solution)/shard_map/pallas_call | solution.py:110
  199.5 4.1 %shard_map.236 = (f32[128,960]{1,0:T(8,128)}, bf16[128,960]{1,0:T(8,128)(2,1)}, bf16[128,960]{1,0:T(8,128)(2,1)}, bf16[128,960]{1,0:T(8,128)(2,1)}, f32[128,960]{1,0:T(8,128)}, /*index=5*/f32[128,960]{1,0:T(8,128)}) custom-call(bf16[128,960]{1,0:T(8,128)(2,1)} %copy-done.20, bf16[128,960]{1,0:T(8,128)(2,1)} %copy-done.41, ...), custom_call_target="tpu_custom_call" | custom-call | tf_op jit(solution)/shard_map/pallas_call | solution.py:110
  203.6 3.6 shard_map.248
  209.5 9.5 %shard_map.237 = (f32[128,960]{1,0:T(8,128)}, bf16[128,640]{1,0:T(8,128)(2,1)}, bf16[128,640]{1,0:T(8,128)(2,1)}, bf16[128,640]{1,0:T(8,128)(2,1)}, bf16[128,640]{1,0:T(8,128)(2,1)}, /*index=5*/f32[128,640]{1,0:T(8,128)}) custom-call(bf16[128,960]{1,0:T(8,128)(2,1)} %get-tuple-element.89.query_ref, s32[128,1]{1,0:T(8,128)} %copy.61.position_ref, ...), custom_call_target="tpu_custom_call" | custom-call | tf_op jit(solution)/shard_map/pallas_call | solution.py:110
  224.5 5.3 %collective-permute-done.53.refs_2_ = bf16[128,640]{1,0:T(8,128)(2,1)S(1)} collective-permute-done((bf16[128,640]{1,0:T(8,128)(2,1)}, bf16[128,640]{1,0:T(8,128)(2,1)S(1)}, u32[]{:S(2)}, u32[]{:S(2)}) %collective-permute-start.53) | collective-permute-done | bytes 163872 | tf_op jit(solution)/shard_map/ppermute | solution.py:35
  232.8 6.4 %collective-permute-start.70 = (bf16[128,960]{1,0:T(8,128)(2,1)}, bf16[128,960]{1,0:T(8,128)(2,1)}, u32[]{:S(2)}, u32[]{:S(2)}) collective-permute-start(bf16[128,960]{1,0:T(8,128)(2,1)} %get-tuple-element.135), channel_id=1, source_target_pairs={{0,4},{1,5},{2,6},{3,7},{4,0},{5,1},{6,2},{7,3},{8,12},{9,13},{10,... | collective-permute-start | bytes 737288 | tf_op jit(solution)/shard_map/ppermute | solution.py:29
  242.4 4.9 %collective-permute-start.71 = (bf16[128,960]{1,0:T(8,128)(2,1)}, bf16[128,960]{1,0:T(8,128)(2,1)}, u32[]{:S(2)}, u32[]{:S(2)}) collective-permute-start(bf16[128,960]{1,0:T(8,128)(2,1)} %get-tuple-element.136), channel_id=1, source_target_pairs={{0,6},{1,7},{2,4},{3,5},{4,2},{5,3},{6,0},{7,1},{8,14},{9,15},{10,... | collective-permute-start | bytes 737288 | tf_op jit(solution)/shard_map/ppermute | solution.py:29
  247.3 3.4 shard_map.247
  259.1 19.9 %collective-permute-done.80.refs_1_ = bf16[80,960]{1,0:T(8,128)(2,1)S(1)} collective-permute-done((bf16[80,960]{1,0:T(8,128)(2,1)}, bf16[80,960]{1,0:T(8,128)(2,1)S(1)}, u32[]{:S(2)}, u32[]{:S(2)}) %collective-permute-start.80) | collective-permute-done | bytes 153632 | tf_op jit(solution)/shard_map/ppermute | solution.py:29
  283.2 4.7 %shard_map.240 = (f32[128,1600]{1,0:T(8,128)}, bf16[128,1600]{1,0:T(8,128)(2,1)}, bf16[128,1600]{1,0:T(8,128)(2,1)}, bf16[128,1600]{1,0:T(8,128)(2,1)}, f32[128,960]{1,0:T(8,128)}, /*index=5*/f32[128,960]{1,0:T(8,128)}) custom-call(bf16[128,1600]{1,0:T(8,128)(2,1)} %shard_map.239.refs_0_, bf16[128,1600]{1,0:T(8,128)(2,1)} %copy-done.28, ...), custom_call_target="tpu_custom_call" | custom-call | tf_op jit(solution)/shard_map/pallas_call | solution.py:110
  290.0 6.6 %collective-permute-done.81.refs_2_ = bf16[80,960]{1,0:T(8,128)(2,1)S(1)} collective-permute-done((bf16[80,960]{1,0:T(8,128)(2,1)}, bf16[80,960]{1,0:T(8,128)(2,1)S(1)}, u32[]{:S(2)}, u32[]{:S(2)}) %collective-permute-start.81) | collective-permute-done | bytes 153632 | tf_op jit(solution)/shard_map/ppermute | solution.py:29
  296.6 3.6 collective-permute-start.73
  311.3 3.5 shard_map.238
  334.0 8.6 %collective-permute-done.59 = f32[2,960]{1,0:T(2,128)S(1)} collective-permute-done((f32[2,960]{1,0:T(2,128)}, f32[2,960]{1,0:T(2,128)S(1)}, u32[]{:S(2)}, u32[]{:S(2)}) %collective-permute-start.59) | collective-permute-done | bytes 7712 | tf_op jit(solution)/shard_map/ppermute | solution.py:29
  343.4 3.9 %collective-permute-start.50 = (bf16[128,960]{1,0:T(8,128)(2,1)}, bf16[128,960]{1,0:T(8,128)(2,1)}, u32[]{:S(2)}, u32[]{:S(2)}) collective-permute-start(bf16[128,960]{1,0:T(8,128)(2,1)} %get-tuple-element.112), channel_id=1, source_target_pairs={{0,4},{1,5},{2,6},{3,7},{4,0},{5,1},{6,2},{7,3},{8,12},{9,13},{10,... | collective-permute-start | bytes 737288 | tf_op jit(solution)/shard_map/ppermute | solution.py:29
  347.3 5.6 %collective-permute-done.64.refs_2_ = bf16[128,1600]{1,0:T(8,128)(2,1)S(1)} collective-permute-done((bf16[128,1600]{1,0:T(8,128)(2,1)}, bf16[128,1600]{1,0:T(8,128)(2,1)S(1)}, u32[]{:S(2)}, u32[]{:S(2)}) %collective-permute-start.64) | collective-permute-done | bytes 409632 | tf_op jit(solution)/shard_map/ppermute | solution.py:29
  (389 shorter events, 173.7 us)
Async XLA Ops:
  14.2 34.2 %collective-permute-start.15 = (bf16[32,1280]{1,0:T(8,128)(2,1)}, bf16[32,1280]{1,0:T(8,128)(2,1)}, u32[]{:S(2)}, u32[]{:S(2)}) collective-permute-start(bf16[32,1280]{1,0:T(8,128)(2,1)} %get-tuple-element.222), channel_id=1, source_target_pairs={{0,6},{1,7},{2,4},{3,5},{4,2},{5,3},{6,0},{7,1},{8,14},{9,15},{10,... | collective-permute-start | bytes 245768 | tf_op jit(solution)/shard_map/ppermute | solution.py:29
  19.1 21.5 %collective-permute-start.5 = (bf16[128,1600]{1,0:T(8,128)(2,1)S(1)}, bf16[128,1600]{1,0:T(8,128)(2,1)S(1)}, u32[]{:S(2)}, u32[]{:S(2)}) collective-permute-start(bf16[128,1600]{1,0:T(8,128)(2,1)S(1)} %pad_maximum_fusion.refs_3_.refs_4_), channel_id=1, source_target_pairs={{0,4},{1,5},{2,6},{3,7},{4,0},{5,1},{6,2},{7,3},{8,12},{9,13},{10,... | collective-permute-start | bytes 1228808 | tf_op jit(solution)/shard_map/ppermute | solution.py:29
  20.7 21.4 %collective-permute-start.6 = (bf16[128,1600]{1,0:T(8,128)(2,1)S(1)}, bf16[128,1600]{1,0:T(8,128)(2,1)S(1)}, u32[]{:S(2)}, u32[]{:S(2)}) collective-permute-start(bf16[128,1600]{1,0:T(8,128)(2,1)S(1)} %pad_maximum_fusion.refs_3_.refs_4_), channel_id=1, source_target_pairs={{0,6},{1,7},{2,4},{3,5},{4,2},{5,3},{6,0},{7,1},{8,14},{9,15},{10,... | collective-permute-start | bytes 1228808 | tf_op jit(solution)/shard_map/ppermute | solution.py:29
  22.8 25.6 %collective-permute-start.14 = (bf16[32,1280]{1,0:T(8,128)(2,1)S(1)}, bf16[32,1280]{1,0:T(8,128)(2,1)S(1)}, u32[]{:S(2)}, u32[]{:S(2)}) collective-permute-start(bf16[32,1280]{1,0:T(8,128)(2,1)S(1)} %get-tuple-element.220), channel_id=1, source_target_pairs={{0,4},{1,5},{2,6},{3,7},{4,0},{5,1},{6,2},{7,3},{8,12},{9,13},{10,... | collective-permute-start | bytes 245768 | tf_op jit(solution)/shard_map/ppermute | solution.py:29
  55.9 18.9 %collective-permute-start.17 = (bf16[32,960]{1,0:T(8,128)(2,1)S(1)}, bf16[32,960]{1,0:T(8,128)(2,1)S(1)}, u32[]{:S(2)}, u32[]{:S(2)}) collective-permute-start(bf16[32,960]{1,0:T(8,128)(2,1)S(1)} %pad.14), channel_id=1, source_target_pairs={{0,8},{1,9},{2,10},{3,11},{4,12},{5,13},{6,14},{7,15},{8,0},{9,1},... | collective-permute-start | bytes 184328 | tf_op jit(solution)/shard_map/ppermute | solution.py:29
  96.5 21.4 %collective-permute-start.23 = (f32[128,960]{1,0:T(8,128)}, f32[128,960]{1,0:T(8,128)S(1)}, u32[]{:S(2)}, u32[]{:S(2)}) collective-permute-start(f32[128,960]{1,0:T(8,128)} %get-tuple-element.95), channel_id=1, source_target_pairs={{0,1},{1,0},{2,3},{3,2},{4,5},{5,4},{6,7},{7,6},{8,9},{9,8},{10,11... | collective-permute-start | bytes 1474568 | tf_op jit(solution)/shard_map/ppermute | solution.py:29
  101.3 19.6 %collective-permute-start.30 = (bf16[128,1280]{1,0:T(8,128)(2,1)S(1)}, bf16[128,1280]{1,0:T(8,128)(2,1)S(1)}, u32[]{:S(2)}, u32[]{:S(2)}) collective-permute-start(bf16[128,1280]{1,0:T(8,128)(2,1)S(1)} %pad_maximum_fusion.2.refs_8_), channel_id=1, source_target_pairs={{0,8},{1,9},{2,10},{3,11},{4,12},{5,13},{6,14},{7,15},{8,0},{9,1},... | collective-permute-start | bytes 983048 | tf_op jit(solution)/shard_map/ppermute | solution.py:29
  106.9 31.9 %collective-permute-start.31 = (bf16[128,1280]{1,0:T(8,128)(2,1)S(1)}, bf16[128,1280]{1,0:T(8,128)(2,1)S(1)}, u32[]{:S(2)}, u32[]{:S(2)}) collective-permute-start(bf16[128,1280]{1,0:T(8,128)(2,1)S(1)} %pad_maximum_fusion.2.refs_8_), channel_id=1, source_target_pairs={{0,16},{1,17},{2,18},{3,19},{4,20},{5,21},{6,22},{7,23},{8,24},{9,... | collective-permute-start | bytes 983048 | tf_op jit(solution)/shard_map/ppermute | solution.py:29
  114.3 24.5 %collective-permute-start.32 = (bf16[128,1280]{1,0:T(8,128)(2,1)S(1)}, bf16[128,1280]{1,0:T(8,128)(2,1)S(1)}, u32[]{:S(2)}, u32[]{:S(2)}) collective-permute-start(bf16[128,1280]{1,0:T(8,128)(2,1)S(1)} %pad_maximum_fusion.2.refs_8_), channel_id=1, source_target_pairs={{0,24},{1,25},{2,26},{3,27},{4,28},{5,29},{6,30},{7,31},{8,16},{9,... | collective-permute-start | bytes 983048 | tf_op jit(solution)/shard_map/ppermute | solution.py:29
  119.7 20.7 %collective-permute-start.33 = (bf16[128,1280]{1,0:T(8,128)(2,1)S(1)}, bf16[128,1280]{1,0:T(8,128)(2,1)S(1)}, u32[]{:S(2)}, u32[]{:S(2)}) collective-permute-start(bf16[128,1280]{1,0:T(8,128)(2,1)S(1)} %pad_maximum_fusion.2.refs_8_), channel_id=1, source_target_pairs={{0,1},{1,0},{2,3},{3,2},{4,5},{5,4},{6,7},{7,6},{8,9},{9,8},{10,11... | collective-permute-start | bytes 983048 | tf_op jit(solution)/shard_map/ppermute | solution.py:29
  119.9 19.5 %collective-permute-start.43 = (bf16[80,960]{1,0:T(8,128)(2,1)}, bf16[80,960]{1,0:T(8,128)(2,1)}, u32[]{:S(2)}, u32[]{:S(2)}) collective-permute-start(bf16[80,960]{1,0:T(8,128)(2,1)} %copy-done.43), channel_id=1, source_target_pairs={{0,1},{1,0},{2,3},{3,2},{4,5},{5,4},{6,7},{7,6},{8,9},{9,8},{10,11... | collective-permute-start | bytes 460808 | tf_op jit(solution)/shard_map/ppermute | solution.py:29
  120.8 21.6 %collective-permute-start.34 = (bf16[128,1280]{1,0:T(8,128)(2,1)S(1)}, bf16[128,1280]{1,0:T(8,128)(2,1)S(1)}, u32[]{:S(2)}, u32[]{:S(2)}) collective-permute-start(bf16[128,1280]{1,0:T(8,128)(2,1)S(1)} %collective-permute-done.30.refs_9_), channel_id=1, source_target_pairs={{0,1},{1,0},{2,3},{3,2},{4,5},{5,4},{6,7},{7,6},{8,9},{9,8},{10,11... | collective-permute-start | bytes 983048 | tf_op jit(solution)/shard_map/ppermute | solution.py:29
  140.4 26.7 %collective-permute-start.24 = (bf16[128,1024]{1,0:T(8,128)(2,1)S(1)}, bf16[128,1024]{1,0:T(8,128)(2,1)S(1)}, u32[]{:S(2)}, u32[]{:S(2)}) collective-permute-start(bf16[128,1024]{1,0:T(8,128)(2,1)S(1)} %fusion.8.refs_0_), channel_id=1, source_target_pairs={{0,2},{1,3},{2,0},{3,1},{4,6},{5,7},{6,4},{7,5},{8,10},{9,11},{10,... | collective-permute-start | bytes 786440 | tf_op jit(solution)/shard_map/ppermute | solution.py:29
  142.4 24.7 %collective-permute-start.25 = (bf16[128,1024]{1,0:T(8,128)(2,1)S(1)}, bf16[128,1024]{1,0:T(8,128)(2,1)S(1)}, u32[]{:S(2)}, u32[]{:S(2)}) collective-permute-start(bf16[128,1024]{1,0:T(8,128)(2,1)S(1)} %fusion.8.refs_0_), channel_id=1, source_target_pairs={{0,4},{1,5},{2,6},{3,7},{4,0},{5,1},{6,2},{7,3},{8,12},{9,13},{10,... | collective-permute-start | bytes 786440 | tf_op jit(solution)/shard_map/ppermute | solution.py:29
  142.5 24.6 %collective-permute-start.26 = (bf16[128,1024]{1,0:T(8,128)(2,1)S(1)}, bf16[128,1024]{1,0:T(8,128)(2,1)S(1)}, u32[]{:S(2)}, u32[]{:S(2)}) collective-permute-start(bf16[128,1024]{1,0:T(8,128)(2,1)S(1)} %fusion.8.refs_0_), channel_id=1, source_target_pairs={{0,6},{1,7},{2,4},{3,5},{4,2},{5,3},{6,0},{7,1},{8,14},{9,15},{10,... | collective-permute-start | bytes 786440 | tf_op jit(solution)/shard_map/ppermute | solution.py:29
  144.1 23.0 %collective-permute-start.28 = (bf16[128,960]{1,0:T(8,128)(2,1)S(1)}, bf16[128,960]{1,0:T(8,128)(2,1)S(1)}, u32[]{:S(2)}, u32[]{:S(2)}) collective-permute-start(bf16[128,960]{1,0:T(8,128)(2,1)S(1)} %copy.65.refs_4_.refs_1_), channel_id=1, source_target_pairs={{0,4},{1,5},{2,6},{3,7},{4,0},{5,1},{6,2},{7,3},{8,12},{9,13},{10,... | collective-permute-start | bytes 737288 | tf_op jit(solution)/shard_map/ppermute | solution.py:29
  148.6 18.5 %collective-permute-start.29 = (bf16[128,960]{1,0:T(8,128)(2,1)S(1)}, bf16[128,960]{1,0:T(8,128)(2,1)S(1)}, u32[]{:S(2)}, u32[]{:S(2)}) collective-permute-start(bf16[128,960]{1,0:T(8,128)(2,1)S(1)} %copy.65.refs_4_.refs_1_), channel_id=1, source_target_pairs={{0,6},{1,7},{2,4},{3,5},{4,2},{5,3},{6,0},{7,1},{8,14},{9,15},{10,... | collective-permute-start | bytes 737288 | tf_op jit(solution)/shard_map/ppermute | solution.py:29
  198.3 44.1 %collective-permute-start.75 = (bf16[512,1280]{1,0:T(8,128)(2,1)}, bf16[512,1280]{1,0:T(8,128)(2,1)S(1)}, u32[]{:S(2)}, u32[]{:S(2)}) collective-permute-start(bf16[512,1280]{1,0:T(8,128)(2,1)} %get-tuple-element.146), channel_id=1, source_target_pairs={{0,1},{1,0},{2,3},{3,2},{4,5},{5,4},{6,7},{7,6},{8,9},{9,8},{10,11... | collective-permute-start | bytes 3932168 | tf_op jit(solution)/shard_map/ppermute | solution.py:29
  207.2 43.5 %collective-permute-start.79 = (bf16[320,960]{1,0:T(8,128)(2,1)}, bf16[320,960]{1,0:T(8,128)(2,1)S(1)}, u32[]{:S(2)}, u32[]{:S(2)}) collective-permute-start(bf16[320,960]{1,0:T(8,128)(2,1)} %get-tuple-element.152), channel_id=1, source_target_pairs={{0,1},{1,0},{2,3},{3,2},{4,5},{5,4},{6,7},{7,6},{8,9},{9,8},{10,11... | collective-permute-start | bytes 1843208 | tf_op jit(solution)/shard_map/ppermute | solution.py:29
  229.8 23.5 %collective-permute-start.69 = (bf16[128,960]{1,0:T(8,128)(2,1)}, bf16[128,960]{1,0:T(8,128)(2,1)}, u32[]{:S(2)}, u32[]{:S(2)}) collective-permute-start(bf16[128,960]{1,0:T(8,128)(2,1)} %get-tuple-element.134), channel_id=1, source_target_pairs={{0,2},{1,3},{2,0},{3,1},{4,6},{5,7},{6,4},{7,5},{8,10},{9,11},{10,... | collective-permute-start | bytes 737288 | tf_op jit(solution)/shard_map/ppermute | solution.py:29
  232.8 21.2 %collective-permute-start.70 = (bf16[128,960]{1,0:T(8,128)(2,1)}, bf16[128,960]{1,0:T(8,128)(2,1)}, u32[]{:S(2)}, u32[]{:S(2)}) collective-permute-start(bf16[128,960]{1,0:T(8,128)(2,1)} %get-tuple-element.135), channel_id=1, source_target_pairs={{0,4},{1,5},{2,6},{3,7},{4,0},{5,1},{6,2},{7,3},{8,12},{9,13},{10,... | collective-permute-start | bytes 737288 | tf_op jit(solution)/shard_map/ppermute | solution.py:29
  241.9 39.6 %collective-permute-start.56 = (bf16[128,1600]{1,0:T(8,128)(2,1)}, bf16[128,1600]{1,0:T(8,128)(2,1)S(1)}, u32[]{:S(2)}, u32[]{:S(2)}) collective-permute-start(bf16[128,1600]{1,0:T(8,128)(2,1)} %shard_map.239.refs_0_), channel_id=1, source_target_pairs={{0,1},{1,0},{2,3},{3,2},{4,5},{5,4},{6,7},{7,6},{8,9},{9,8},{10,11... | collective-permute-start | bytes 1228808 | tf_op jit(solution)/shard_map/ppermute | solution.py:29
  250.6 49.6 %collective-permute-start.76 = (bf16[128,1280]{1,0:T(8,128)(2,1)}, bf16[128,1280]{1,0:T(8,128)(2,1)S(1)}, u32[]{:S(2)}, u32[]{:S(2)}) collective-permute-start(bf16[128,1280]{1,0:T(8,128)(2,1)} %get-tuple-element.148), channel_id=1, source_target_pairs={{0,8},{1,9},{2,10},{3,11},{4,12},{5,13},{6,14},{7,15},{8,0},{9,1},... | collective-permute-start | bytes 983048 | tf_op jit(solution)/shard_map/ppermute | solution.py:29
  253.2 47.0 %collective-permute-start.77 = (bf16[128,1280]{1,0:T(8,128)(2,1)}, bf16[128,1280]{1,0:T(8,128)(2,1)S(1)}, u32[]{:S(2)}, u32[]{:S(2)}) collective-permute-start(bf16[128,1280]{1,0:T(8,128)(2,1)} %get-tuple-element.149), channel_id=1, source_target_pairs={{0,16},{1,17},{2,18},{3,19},{4,20},{5,21},{6,22},{7,23},{8,24},{9,... | collective-permute-start | bytes 983048 | tf_op jit(solution)/shard_map/ppermute | solution.py:29
  254.0 46.3 %collective-permute-start.78 = (bf16[128,1280]{1,0:T(8,128)(2,1)}, bf16[128,1280]{1,0:T(8,128)(2,1)S(1)}, u32[]{:S(2)}, u32[]{:S(2)}) collective-permute-start(bf16[128,1280]{1,0:T(8,128)(2,1)} %get-tuple-element.150), channel_id=1, source_target_pairs={{0,24},{1,25},{2,26},{3,27},{4,28},{5,29},{6,30},{7,31},{8,16},{9,... | collective-permute-start | bytes 983048 | tf_op jit(solution)/shard_map/ppermute | solution.py:29
  258.1 20.9 %collective-permute-start.80 = (bf16[80,960]{1,0:T(8,128)(2,1)}, bf16[80,960]{1,0:T(8,128)(2,1)S(1)}, u32[]{:S(2)}, u32[]{:S(2)}) collective-permute-start(bf16[80,960]{1,0:T(8,128)(2,1)} %get-tuple-element.153), channel_id=1, source_target_pairs={{0,8},{1,9},{2,10},{3,11},{4,12},{5,13},{6,14},{7,15},{8,0},{9,1},... | collective-permute-start | bytes 460808 | tf_op jit(solution)/shard_map/ppermute | solution.py:29
  315.3 32.0 %collective-permute-start.63 = (bf16[128,1600]{1,0:T(8,128)(2,1)}, bf16[128,1600]{1,0:T(8,128)(2,1)}, u32[]{:S(2)}, u32[]{:S(2)}) collective-permute-start(bf16[128,1600]{1,0:T(8,128)(2,1)} %get-tuple-element.123), channel_id=1, source_target_pairs={{0,2},{1,3},{2,0},{3,1},{4,6},{5,7},{6,4},{7,5},{8,10},{9,11},{10,... | collective-permute-start | bytes 1228808 | tf_op jit(solution)/shard_map/ppermute | solution.py:29
  322.6 30.3 %collective-permute-start.64 = (bf16[128,1600]{1,0:T(8,128)(2,1)}, bf16[128,1600]{1,0:T(8,128)(2,1)S(1)}, u32[]{:S(2)}, u32[]{:S(2)}) collective-permute-start(bf16[128,1600]{1,0:T(8,128)(2,1)} %get-tuple-element.124), channel_id=1, source_target_pairs={{0,4},{1,5},{2,6},{3,7},{4,0},{5,1},{6,2},{7,3},{8,12},{9,13},{10,... | collective-permute-start | bytes 1228808 | tf_op jit(solution)/shard_map/ppermute | solution.py:29
  324.2 35.3 %collective-permute-start.65 = (bf16[128,1600]{1,0:T(8,128)(2,1)}, bf16[128,1600]{1,0:T(8,128)(2,1)}, u32[]{:S(2)}, u32[]{:S(2)}) collective-permute-start(bf16[128,1600]{1,0:T(8,128)(2,1)} %get-tuple-element.125), channel_id=1, source_target_pairs={{0,6},{1,7},{2,4},{3,5},{4,2},{5,3},{6,0},{7,1},{8,14},{9,15},{10,... | collective-permute-start | bytes 1228808 | tf_op jit(solution)/shard_map/ppermute | solution.py:29
  342.6 25.3 %collective-permute-start.51 = (bf16[128,960]{1,0:T(8,128)(2,1)}, bf16[128,960]{1,0:T(8,128)(2,1)S(1)}, u32[]{:S(2)}, u32[]{:S(2)}) collective-permute-start(bf16[128,960]{1,0:T(8,128)(2,1)} %get-tuple-element.113), channel_id=1, source_target_pairs={{0,6},{1,7},{2,4},{3,5},{4,2},{5,3},{6,0},{7,1},{8,14},{9,15},{10,... | collective-permute-start | bytes 737288 | tf_op jit(solution)/shard_map/ppermute | solution.py:29
  343.4 27.4 %collective-permute-start.50 = (bf16[128,960]{1,0:T(8,128)(2,1)}, bf16[128,960]{1,0:T(8,128)(2,1)}, u32[]{:S(2)}, u32[]{:S(2)}) collective-permute-start(bf16[128,960]{1,0:T(8,128)(2,1)} %get-tuple-element.112), channel_id=1, source_target_pairs={{0,4},{1,5},{2,6},{3,7},{4,0},{5,1},{6,2},{7,3},{8,12},{9,13},{10,... | collective-permute-start | bytes 737288 | tf_op jit(solution)/shard_map/ppermute | solution.py:29
  347.3 23.5 %collective-permute-start.49 = (bf16[128,960]{1,0:T(8,128)(2,1)}, bf16[128,960]{1,0:T(8,128)(2,1)}, u32[]{:S(2)}, u32[]{:S(2)}) collective-permute-start(bf16[128,960]{1,0:T(8,128)(2,1)} %get-tuple-element.111), channel_id=1, source_target_pairs={{0,2},{1,3},{2,0},{3,1},{4,6},{5,7},{6,4},{7,5},{8,10},{9,11},{10,... | collective-permute-start | bytes 737288 | tf_op jit(solution)/shard_map/ppermute | solution.py:29
  (127 other events, 1467.2 us)
